TPU v7x, 32 devices: a whole 2x2x4 slice. The times are simulated.
32 devices in a mesh: fsdp: 16 (over z, y, x), head: 2 (over core).
Axes of the slice: x: 2, y: 2, z: 4, core: 2. Of those that a mesh axis runs over, the one named last changes fastest.
Arguments:
- tokens: bfloat16 [8192, 2048], P('fsdp'), may hold values from -6 to 6
- norm_gains: float32 [1, 2, 2048], replicated, may hold values from 0.1 to 1.9
- w_mixer: bfloat16 [1, 2048, 8, 1536], P(None, 'fsdp', 'head'), may hold values from -0.125 to 0.125
- w_out: bfloat16 [1, 4096, 2048], P(None, 'head', 'fsdp'), may hold values from -0.1875 to 0.1875
- w_up: bfloat16 [1, 2048, 4096], P(None, 'fsdp', 'head'), may hold values from -0.125 to 0.125
- w_down: bfloat16 [1, 4096, 2048], P(None, 'head', 'fsdp'), may hold values from -0.125 to 0.125
- seg_ids: int32 [8192], P('fsdp'), may hold values from 0 to 5, never falling along the last dimension, each value on 1 to 2048 neighbouring positions
- cotangent: bfloat16 [8192, 2048], P('fsdp'), may hold values from -6 to 6
Outputs:
- output: bfloat16 [8192, 2048], P('fsdp')
- input_grad: bfloat16 [8192, 2048], P('fsdp')
- gain_grad: float32 [1, 2, 2048], replicated
- mixer_grad: float32 [1, 2048, 8, 1536], P(None, 'fsdp', 'head')
- out_grad: float32 [1, 4096, 2048], P(None, 'head', 'fsdp')
- up_grad: float32 [1, 2048, 4096], P(None, 'fsdp', 'head')
- down_grad: float32 [1, 4096, 2048], P(None, 'head', 'fsdp')
Inputs may be any that keep to these rules, and one draw needn't show every extreme that they name: `seg_ids`: sequence numbers never fall along the tokens; each sequence has 1 to 2048 tokens and one has exactly 2048.
All inputs are finite; a program needn't handle non-finite values.
Results may differ from a plain program's by a relative error of at most 0.02.
Values may be sent and summed in bfloat16 or wider, within the bound.
No kernel may reach another device: no remote copies, remote signals or barrier semaphores. Data moves between devices by JAX's collectives and lax.ppermute only.
A program may use at most 256 MiB of HBM per device.

v0:
```python
from functools import partial

import jax
import jax.numpy as jnp
from jax import lax
from jax.experimental import pallas as pl
from jax.experimental.pallas import tpu as pltpu
from jax.sharding import Mesh, PartitionSpec as P


HEADS = 8
KEY = 256
VALUE = 512
SEQ_MOST = 2048

eps_norm = 1e-05
eps_group = 1e-06
bf16 = jnp.bfloat16
f32 = jnp.float32


def team_size(devices, heads_here):
    team = 4
    while heads_here % team or devices % team:
        team //= 2
    return team


def dot(a, b, left=1, right=0):
    return lax.dot_general(a, b, (((left,), (right,)), ((), ())), preferred_element_type=f32)


def layer_norm(stream, gain):
    centered = stream - jnp.mean(stream, axis=-1, keepdims=True)
    scaled = lax.rsqrt(jnp.mean(centered * centered, axis=-1, keepdims=True) + eps_norm)
    normed = centered * scaled
    return (normed * gain, normed, scaled)


def norm_back(grad_out, normed, scaled, gain):
    grad_norm = grad_out * gain
    inner = jnp.mean(grad_norm, axis=-1, keepdims=True)
    along = jnp.mean(grad_norm * normed, axis=-1, keepdims=True)
    return (scaled * (grad_norm - inner - normed * along), jnp.sum(grad_out * normed, axis=0))


def swap(value, axis, d):
    count = lax.axis_size(axis)
    return lax.ppermute(value, axis, [(i, i ^ d) for i in range(count)])


def shift(value, steps):
    count = lax.axis_size("group")
    pairs = [(i, i + steps) for i in range(count) if 0 <= i + steps < count]
    return lax.ppermute(value, "group", pairs)


def total(value):
    for axis in ("head", "team", "group"):
        parts = [value] + [swap(value, axis, d) for d in range(1, lax.axis_size(axis))]
        while len(parts) > 1:
            parts = [parts[k] + parts[k + 1] for k in range(0, len(parts), 2)]
        value = parts[0]
    return value


def straight(pieces, axis):
    mine = lax.axis_index(axis)
    pieces = list(pieces)
    bit = 1
    while bit < len(pieces):
        odd = (mine & bit) != 0
        pieces = [jnp.where(odd, pieces[i ^ bit], pieces[i]) for i in range(len(pieces))]
        bit *= 2
    return pieces


def deal(pick):
    mine = lax.axis_index("team")
    got = [pick(mine)]
    for d in range(1, lax.axis_size("team")):
        got.append(swap(pick(mine ^ d), "team", d))
    return straight(got, "team")


def join(parts):
    rows = parts[0].shape[0]
    out = jnp.zeros((rows * len(parts),) + parts[0].shape[1:], parts[0].dtype)
    for i, part in enumerate(parts):
        out = lax.dynamic_update_slice_in_dim(out, part, i * rows, 0)
    return out


def share(own):
    parts = [own] + [swap(own, "team", d) for d in range(1, lax.axis_size("team"))]
    rows = join(parts)
    return [rows] + [swap(rows, "head", e) for e in range(1, lax.axis_size("head"))]


def after(values, first):
    return lax.optimization_barrier((values, first))[0]


def reduce_kernel(team, rows_ref, weight_ref, *refs):
    others, outs = refs[: len(refs) - team], refs[len(refs) - team :]
    total = dot(rows_ref[...], weight_ref[...], 1, 1)
    for other in others:
        total = total + other[...].astype(f32)
    piece = total.shape[0] // team
    for d, out in enumerate(outs):
        out[...] = total[d * piece : (d + 1) * piece].astype(out.dtype)


def reduce(rows, weight, column):
    team, cores = lax.axis_size("team"), len(rows)
    count, depth = rows[0].shape
    width = weight.shape[0]
    step = min(1024 if depth <= 512 else 512, width)
    part = weight[:, column * depth : (column + 1) * depth]
    first = [dot(rows[e], part, 1, 1).astype(bf16) for e in range(1, cores)]
    others = [swap(v, "head", e) for e, v in enumerate(first, 1)]
    piece = count // team
    out = pl.pallas_call(
        partial(reduce_kernel, team),
        grid=(width // step,),
        in_specs=[
            pl.BlockSpec((count, depth), lambda i: (0, 0)),
            pl.BlockSpec((step, depth), lambda i: (i, column)),
        ]
        + [pl.BlockSpec((count, step), lambda i: (0, i))] * (cores - 1),
        out_specs=[pl.BlockSpec((piece, step), lambda i: (0, i))] * team,
        out_shape=[jax.ShapeDtypeStruct((piece, width), bf16 if d else f32) for d in range(team)],
        compiler_params=pltpu.CompilerParams(dimension_semantics=("arbitrary",)),
        cost_estimate=pl.CostEstimate(
            flops=2 * count * depth * width,
            bytes_accessed=2 * width * (depth + 2 * count),
            transcendentals=0,
        ),
    )(rows[0], weight, *others)
    got = [swap(out[d], "team", d) for d in range(1, team)]
    value = out[0]
    for v in got:
        value = value + v.astype(f32)
    return value, out


def grads(left, right):
    value = dot(left[0], right[0], 0, 0)
    for a, b in zip(left[1:], right[1:]):
        value = value + dot(a, b, 0, 0)
    value = value.astype(bf16)
    return lax.psum_scatter(value, "group", scatter_dimension=0, tiled=True)


SUB = 128


def blocks_of(ref):
    size = min(SUB, ref.shape[0])
    return [slice(i, i + size) for i in range(0, ref.shape[0], size)]


def unit_kernel(hidden_ref, weight_ref, grad_ref, act_out, grad_out):
    for at in blocks_of(hidden_ref):
        value = dot(hidden_ref[at], weight_ref[...])
        cumulative = 0.5 + 0.5 * lax.erf(value * (0.5**0.5))
        density = jnp.exp(-0.5 * value * value) * 0.3989422804014327
        act_out[at] = (value * cumulative).astype(bf16)
        grad_out[at] = (grad_ref[at] * (cumulative + value * density)).astype(bf16)


def unit_step(hidden, weight, grad, units):
    rows, width = hidden.shape
    size = min(256, rows)
    own = lambda i: (i, 0)
    shape = jax.ShapeDtypeStruct((rows, units), bf16)
    return pl.pallas_call(
        unit_kernel,
        grid=(rows // size,),
        in_specs=[
            pl.BlockSpec((size, width), own),
            pl.BlockSpec((width, units), lambda i: (0, 0)),
            pl.BlockSpec((size, units), own),
        ],
        out_specs=[pl.BlockSpec((size, units), own)] * 2,
        out_shape=[shape] * 2,
        compiler_params=pltpu.CompilerParams(dimension_semantics=("arbitrary",)),
        cost_estimate=pl.CostEstimate(
            flops=2 * rows * width * units, bytes_accessed=2 * rows * width, transcendentals=0
        ),
    )(hidden, weight, grad)


def chosen(refs, at):
    team = at[1]
    value = refs[0][...]
    for e in range(1, len(refs)):
        value = jnp.where(at[0] >= e * team, refs[e][...], value)
    return value


def weights_of(rate, seg_col, seg_row):
    size = seg_col.shape[0]
    row = lax.broadcasted_iota(jnp.int32, (size, size), 0)
    col = lax.broadcasted_iota(jnp.int32, (size, size), 1)
    offset = row - col
    valid = (offset >= 0) & (seg_col == seg_row)
    decay = jnp.where(valid, jnp.exp(jnp.maximum(offset, 0).astype(f32) * rate), 0.0)
    place = lax.broadcasted_iota(jnp.int32, (size, 1), 0)
    ahead = jnp.exp((place + 1).astype(f32) * rate)
    behind = jnp.exp((size - 1 - place).astype(f32) * rate)
    return decay, ahead, behind


def forward_kernel(cores, team, order, firsts, lasts, before_group, floats, *refs):
    qkv_refs = refs[:cores]
    col_ref, row_ref, start_ref, normed_ref, scale_ref, states_ref, state = refs[cores:]
    step = pl.program_id(0)
    rank = step
    at = order[rank]
    rate = floats[0]

    @pl.when(step == 0)
    def _():
        state[...] = start_ref[...].astype(f32)

    qkv = chosen(qkv_refs, (at, team))
    query, key, value = qkv[:, :KEY], qkv[:, KEY : 2 * KEY], qkv[:, 2 * KEY :]
    seg = col_ref[...]
    grown = jnp.exp(jnp.full((1, 1), 1.0, f32) * floats[1])
    decay, ahead, behind = weights_of(rate, seg, row_ref[0])
    first, last = firsts[at], lasts[at]
    before = jnp.where(rank == 0, before_group[0], lasts[order[jnp.maximum(rank - 1, 0)]])
    ahead = jnp.where((seg == first) & (before == first), ahead, 0.0)
    behind = jnp.where(seg == last, behind, 0.0)
    carry = jnp.where((before == first) & (first == last), grown, 0.0)
    held = state[...].astype(bf16)
    states_ref[0] = held
    scores = dot(query, key, 1, 1)
    weights = (scores * decay).astype(bf16)
    mixed = dot(weights, value) + ahead * dot(query, held)
    scale = lax.rsqrt(jnp.mean(mixed * mixed, axis=-1, keepdims=True) + eps_group)
    normed_ref[...] = mixed * scale
    scale_ref[...] = scale
    state[...] = dot((key * behind).astype(bf16), value, 0, 0) + carry * state[...]


def backward_kernel(cores, team, order, firsts, lasts, before_group, floats, *refs):
    groups = [refs[i * cores : (i + 1) * cores] for i in range(4)]
    qkv_refs, mixed_refs, rest_refs, gate_refs = groups
    states_ref, col_ref, row_ref, start_ref, out_ref, state = refs[4 * cores :]
    step = pl.program_id(0)
    rank = pl.num_programs(0) - 1 - step
    at = order[rank]
    rate = floats[0]

    @pl.when(step == 0)
    def _():
        state[...] = start_ref[...].astype(f32)

    qkv = chosen(qkv_refs, (at, team))
    grad = chosen(mixed_refs, (at, team))
    query, key, value = qkv[:, :KEY], qkv[:, KEY : 2 * KEY], qkv[:, 2 * KEY :]
    seg = col_ref[...]
    grown = jnp.exp(jnp.full((1, 1), 1.0, f32) * floats[1])
    decay, ahead, behind = weights_of(rate, seg, row_ref[0])
    first, last = firsts[at], lasts[at]
    before = jnp.where(rank == 0, before_group[0], lasts[order[jnp.maximum(rank - 1, 0)]])
    ahead = jnp.where((seg == first) & (before == first), ahead, 0.0)
    behind = jnp.where(seg == last, behind, 0.0)
    carry = jnp.where((before == first) & (first == last), grown, 0.0)
    held = state[...].astype(bf16)
    weights = (dot(query, key, 1, 1) * decay).astype(bf16)
    grad_rest = chosen(rest_refs, (at, team))
    grad_weights = dot(grad, value, 1, 1) + dot(grad_rest, value, 1, 1)
    grad_scores = (grad_weights * decay).astype(bf16)
    grad_query = dot(grad_scores, key) + ahead * dot(grad, states_ref[0], 1, 1)
    grad_key = dot(grad_scores, query, 0, 0) + behind * dot(value, held, 1, 1)
    grad_value = dot(weights, grad, 0, 0) + behind * dot(key, held)
    out_ref[:, :KEY] = grad_query.astype(bf16)
    out_ref[:, KEY : 2 * KEY] = grad_key.astype(bf16)
    out_ref[:, 2 * KEY : 2 * KEY + VALUE] = grad_value.astype(bf16)
    out_ref[:, 2 * KEY + VALUE :] = chosen(gate_refs, (at, team))
    state[...] = dot((query * ahead).astype(bf16), grad, 0, 0) + carry * state[...]


def walk(kernel, cores, team, edges, split, whole, outs, reverse, flops, moved):
    chunks = cores * team

    def at(step, order):
        return order[chunks - 1 - step] if reverse else order[step]

    def block(e, width, size):
        return pl.BlockSpec(
            (size, width),
            lambda i, order, *_: (jnp.clip(at(i, order) - e * team, 0, team - 1), 0),
        )

    def spec(shape, each):
        zeros = (0,) * (len(shape) - 1)
        if each:
            return pl.BlockSpec(shape, lambda i, order, *_: (at(i, order),) + zeros)
        return pl.BlockSpec(shape, lambda i, order, *_: (0,) + zeros)

    arrays, specs = [], []
    for group in split:
        for e, array in enumerate(group):
            arrays.append(array)
            specs.append(block(e, array.shape[1], array.shape[0] // team))
    for array, shape, each in whole:
        arrays.append(array)
        specs.append(spec(shape, each))
    return pl.pallas_call(
        partial(kernel, cores, team),
        grid_spec=pltpu.PrefetchScalarGridSpec(
            num_scalar_prefetch=len(edges),
            grid=(chunks,),
            in_specs=specs,
            out_specs=[spec(shape, each) for _, shape, each in outs],
            scratch_shapes=[pltpu.VMEM((KEY, VALUE), f32)],
        ),
        out_shape=[shape for shape, _, _ in outs],
        compiler_params=pltpu.CompilerParams(dimension_semantics=("arbitrary",)),
        cost_estimate=pl.CostEstimate(flops=flops, bytes_accessed=moved, transcendentals=0),
    )(*edges, *arrays)


def gate_back_kernel(grad_ref, weight_ref, gate_ref, normed_ref, scale_ref, gate_out, mixed_out, rest_out):
    for at in blocks_of(grad_ref):
        grad_gated = dot(grad_ref[at], weight_ref[...])
        gate = gate_ref[at]
        normed = normed_ref[at]
        sigmoid = 1.0 / (1.0 + jnp.exp(-gate))
        gate_out[at] = (
            grad_gated * normed * (sigmoid + gate * sigmoid * (1.0 - sigmoid))
        ).astype(bf16)
        grad_normed = grad_gated * (gate * sigmoid)
        along = jnp.mean(grad_normed * normed, axis=-1, keepdims=True)
        grad_mixed = scale_ref[at] * (grad_normed - normed * along)
        rounded = grad_mixed.astype(bf16)
        mixed_out[at] = rounded
        rest_out[at] = (grad_mixed - rounded.astype(f32)).astype(bf16)


def gate_back(grad, weight, gate, normed, scale, e):
    rows, width = grad.shape
    size = min(256, rows)
    steps = rows // size
    own = lambda i: (i, 0)
    far = lambda i: (e * steps + i, 0)
    shape = jax.ShapeDtypeStruct((rows, VALUE), bf16)
    return pl.pallas_call(
        gate_back_kernel,
        grid=(steps,),
        in_specs=[
            pl.BlockSpec((size, width), own),
            pl.BlockSpec(weight.shape, lambda i: (0, 0)),
            pl.BlockSpec((size, VALUE), own),
            pl.BlockSpec((size, VALUE), far),
            pl.BlockSpec((size, 1), far),
        ],
        out_specs=[pl.BlockSpec((size, VALUE), own)] * 3,
        out_shape=[shape] * 3,
        compiler_params=pltpu.CompilerParams(dimension_semantics=("arbitrary",)),
        cost_estimate=pl.CostEstimate(
            flops=2 * rows * width * VALUE, bytes_accessed=2 * rows * width, transcendentals=0
        ),
    )(grad, weight, gate, normed, scale)


def shards(tokens, norm_gains, w_mixer, w_out, w_up, w_down, seg_ids, cotangent):
    team, _, cores = (lax.axis_size(a) for a in ("team", "group", "head"))
    _, j, c = (lax.axis_index(a) for a in ("group", "team", "head"))
    heads_here = w_mixer.shape[2]
    length, _ = tokens.shape
    size = length // cores
    chunks = team
    near = range(cores)
    units = w_up.shape[2] // team

    rows_here = w_mixer.shape[1]
    mixer_slabs = w_mixer[0].transpose(1, 0, 2)
    rest = jnp.concatenate(
        [
            w_out[0].reshape(team, VALUE, rows_here).transpose(0, 2, 1),
            w_up[0].reshape(rows_here, team, units).transpose(1, 0, 2),
            w_down[0].reshape(team, units, rows_here).transpose(0, 2, 1),
        ],
        axis=2,
    )
    mixer_rows = join(deal(lambda m: lax.dynamic_index_in_dim(mixer_slabs, m, 0, keepdims=False)))
    whole = partial(lax.all_gather, axis_name="group", axis=0, tiled=True)
    w_mixer_all = whole(mixer_rows)

    segs = [seg_ids] + [swap(seg_ids, "team", d) for d in range(1, team)]
    seg = jnp.stack(
        [
            lax.dynamic_slice_in_dim(segs[d], (c ^ e) * size, size, 0)
            for e in near
            for d in range(team)
        ]
    )
    chunks = cores * team
    rank = jnp.arange(chunks)
    order = (((rank % cores) ^ c) * team + ((rank // cores) ^ j)).astype(jnp.int32)
    place = jnp.stack([(j ^ d) * length + (c ^ e) * size for e in near for d in range(team)])
    group_length = team * length
    group_first = jnp.min(seg, keepdims=True)
    group_last = jnp.max(seg, keepdims=True)
    before_group = shift(group_last + 1, 1) - 1
    head = c * heads_here + j
    rate = jnp.log1p(-jnp.exp2(-5.0 - head.astype(f32)))
    floats = rate * jnp.array([1.0, size], f32)
    seg_col = seg.reshape(-1, 1)
    seg_row = seg[:, None, :]
    token = (place[:, None] + jnp.arange(size)).reshape(-1, 1)
    to_end = jnp.where(
        seg_col == group_last, jnp.exp((group_length - 1 - token).astype(f32) * rate), 0.0
    )
    from_start = jnp.where(
        seg_col == before_group, jnp.exp((token + 1).astype(f32) * rate), 0.0
    )
    through = jnp.where(
        (before_group == group_first) & (group_first == group_last),
        jnp.exp(group_length * rate),
        0.0,
    )
    edges = (order, seg[:, 0], seg[:, size - 1], before_group.reshape(1), floats)
    hops = -(-(SEQ_MOST - 1) // group_length)
    rows = team * size

    def here(value, e):
        return value[e * rows : (e + 1) * rows]

    def state_sum(left, factor, right):
        return sum(
            dot((left[e] * here(factor, e)).astype(bf16), right[e], 0, 0) for e in near
        )

    def passed(value, steps):
        state = shift(value.astype(bf16), steps)
        for _ in range(hops - 1):
            state = shift((value + through * state.astype(f32)).astype(bf16), steps)
        return state

    gain_one, gain_two = norm_gains[0, 0], norm_gains[0, 1]
    stream = lax.dynamic_slice_in_dim(tokens, c * size, size, 0).astype(f32)
    cot = lax.dynamic_slice_in_dim(cotangent, c * size, size, 0)
    hidden_own, normed1, scaled1 = layer_norm(stream, gain_one)
    hidden = share(after(hidden_own.astype(bf16), mixer_rows))
    rest = after(rest, mixer_rows)
    rest_rows = join(deal(lambda m: lax.dynamic_index_in_dim(rest, m, 0, keepdims=False)))
    w_o = whole(rest_rows[:, :VALUE])
    w_ud = whole(rest_rows[:, VALUE:])
    cot_all = share(after(cot, hidden[0]))

    qkv = [dot(h, w_mixer_all[:, : 2 * KEY + VALUE]).astype(bf16) for h in hidden]
    end_state = state_sum(
        [v[:, KEY : 2 * KEY] for v in qkv], to_end, [v[:, 2 * KEY :] for v in qkv]
    )
    chunk_flops = 2 * size * size * (KEY + VALUE) + 4 * size * KEY * VALUE
    state_in = passed(end_state, 1)
    normed, scale, states = walk(
        forward_kernel,
        cores,
        team,
        edges,
        [qkv],
        [
            (seg_col, (size, 1), True),
            (seg_row, (1, 1, size), True),
            (state_in, (KEY, VALUE), False),
        ],
        [
            (jax.ShapeDtypeStruct((chunks * size, VALUE), f32), (size, VALUE), True),
            (jax.ShapeDtypeStruct((chunks * size, 1), f32), (size, 1), True),
            (jax.ShapeDtypeStruct((chunks, KEY, VALUE), bf16), (1, KEY, VALUE), True),
        ],
        False,
        chunks * chunk_flops,
        chunks * size * 4096,
    )
    gate = [dot(h, w_mixer_all[:, 2 * KEY + VALUE :]) for h in hidden]
    gate = after(gate, state_in)
    gated = []
    for e in near:
        gated.append(
            (gate[e] * jax.nn.sigmoid(gate[e]) * here(normed, e)).astype(bf16)
        )
    stream = stream + reduce(gated, w_o, 0)[0]

    hidden2_own, normed2, scaled2 = layer_norm(stream, gain_two)
    hidden2 = share(hidden2_own.astype(bf16))
    grad_act = [dot(t, w_ud[:, units:]) for t in cot_all]
    pairs = []
    for e in near:
        pairs.append(unit_step(hidden2[e], w_ud, grad_act[e], units))
    act, grad_up = [p[0] for p in pairs], [p[1] for p in pairs]

    def both_cores(rows):
        rows = rows.astype(bf16)
        got = [rows] + [swap(rows, "head", e) for e in range(1, cores)]
        return join(straight(got, "head"))

    grad_hidden2, sent = reduce(grad_up, w_ud, 0)
    down_done = grads(after(cot_all, sent), act)
    up_done = grads(after(hidden2, sent), grad_up)
    norm_part, gain_grad_two = norm_back(grad_hidden2, normed2, scaled2, gain_two)
    grad = cot.astype(f32) + norm_part
    grad_all = share(grad.astype(bf16))
    out_done = grads(grad_all, gated)
    backs = []
    for e in near:
        backs.append(gate_back(grad_all[e], w_o, gate[e], normed, scale, e))
    grad_gate, grad_mixed, mixed_rest = ([v[i] for v in backs] for i in range(3))
    gate_done = grads(hidden, grad_gate)
    grad_before = state_sum([v[:, :KEY] for v in qkv], from_start, grad_mixed)
    grad_in = passed(grad_before, -1)
    stream = stream + reduce(after(act, grad_before), w_ud, 1)[0]
    (proj,) = walk(
        backward_kernel,
        cores,
        team,
        edges,
        [qkv, grad_mixed, mixed_rest, grad_gate],
        [
            (states, (1, KEY, VALUE), True),
            (seg_col, (size, 1), True),
            (seg_row, (1, 1, size), True),
            (grad_in, (KEY, VALUE), False),
        ],
        [
            (
                jax.ShapeDtypeStruct((chunks * size, 2 * KEY + 2 * VALUE), bf16),
                (size, 2 * KEY + 2 * VALUE),
                True,
            ),
        ],
        True,
        3 * chunks * chunk_flops,
        chunks * size * 12000,
    )
    grad_proj = [here(proj, e) for e in near]
    qkv_done = grads(hidden, [v[:, : 2 * KEY + VALUE] for v in grad_proj])
    grad_hidden = reduce(grad_proj, w_mixer_all, 0)[0]
    output = both_cores(stream)
    norm_part, gain_grad_one = norm_back(grad_hidden, normed1, scaled1, gain_one)
    input_grad = both_cores(grad + norm_part)
    gain_grad = total(jnp.stack([gain_grad_one, gain_grad_two]))

    def own_rows(done):
        return deal(lambda m: lax.dynamic_slice_in_dim(done, m * rows_here, rows_here, 0))

    own_units = own_rows(jnp.concatenate([up_done, down_done], axis=1))
    own_heads = own_rows(jnp.concatenate([out_done, gate_done], axis=1))
    own_qkv = own_rows(qkv_done)
    mixer_grad = jnp.concatenate(
        [
            jnp.stack(own_qkv, axis=1),
            jnp.stack([v[:, VALUE:] for v in own_heads], axis=1),
        ],
        axis=-1,
    ).astype(f32)
    up_grad = jnp.concatenate([v[:, :units] for v in own_units], axis=1).astype(f32)
    down_grad = jnp.concatenate([v[:, units:].T for v in own_units], axis=0).astype(f32)
    out_grad = jnp.concatenate([v[:, :VALUE].T for v in own_heads], axis=0).astype(f32)
    return (
        output,
        input_grad,
        gain_grad[None],
        mixer_grad[None],
        out_grad[None],
        up_grad[None],
        down_grad[None],
    )


def solution(mesh):
    devices, cores = mesh.devices.shape
    team = team_size(devices, HEADS // cores)
    fine = Mesh(mesh.devices.reshape(devices // team, team, cores), ("group", "team", "head"))
    fsdp = ("group", "team")

    return jax.shard_map(
        shards,
        mesh=fine,
        in_specs=(
            P(fsdp, None),
            P(),
            P(None, fsdp, "head", None),
            P(None, "head", fsdp),
            P(None, fsdp, "head"),
            P(None, "head", fsdp),
            P(fsdp),
            P(fsdp, None),
        ),
        out_specs=(
            P(fsdp, None),
            P(fsdp, None),
            P(),
            P(None, fsdp, "head", None),
            P(None, "head", fsdp),
            P(None, fsdp, "head"),
            P(None, "head", fsdp),
        ),
        check_vma=False,
    )
```

profile of v0, /device:TPU:0, one launch (start us, length us, event | category | flops | bytes accessed | tf_op | source)
XLA Modules:
  0.0 828.4 jit_solution(2465590654356940971)
XLA Ops:
  7.2 6.3 constant_dynamic-slice_fusion.10
  13.6 4.0 collective-permute-start
  18.4 9.2 %collective-permute-done = bf16[128,1536]{1,0:T(8,128)(2,1)S(1)} collective-permute-done((bf16[128,1536]{1,0:T(8,128)(2,1)S(1)}, bf16[128,1536]{1,0:T(8,128)(2,1)S(1)}, u32[]{:S(2)}, u32[]{:S(2)}) %collective-permute-start) | collective-permute-done | bytes 393248 | tf_op jit(solution)/shard_map/ppermute | solution.py:49
  27.6 7.5 collective-permute-done.1
  59.6 12.9 %collective-permute-done.3 = bf16[256,2048]{1,0:T(8,128)(2,1)} collective-permute-done((bf16[256,2048]{1,0:T(8,128)(2,1)S(1)}, bf16[256,2048]{1,0:T(8,128)(2,1)}, u32[]{:S(2)}, u32[]{:S(2)}) %collective-permute-start.3) | collective-permute-done | bytes 1048608 | tf_op jit(solution)/shard_map/ppermute | solution.py:49
  74.8 19.9 %collective-permute-done.4 = bf16[256,2048]{1,0:T(8,128)(2,1)} collective-permute-done((bf16[256,2048]{1,0:T(8,128)(2,1)S(1)}, bf16[256,2048]{1,0:T(8,128)(2,1)}, u32[]{:S(2)}, u32[]{:S(2)}) %collective-permute-start.4) | collective-permute-done | bytes 1048608 | tf_op jit(solution)/shard_map/ppermute | solution.py:49
  104.0 4.7 collective-permute-start.11
  115.2 8.5 %collective-permute-done.14 = bf16[128,1536]{1,0:T(8,128)(2,1)S(1)} collective-permute-done((bf16[128,1536]{1,0:T(8,128)(2,1)S(1)}, bf16[128,1536]{1,0:T(8,128)(2,1)S(1)}, u32[]{:S(2)}, u32[]{:S(2)}) %collective-permute-start.14) | collective-permute-done | bytes 393248 | tf_op jit(solution)/shard_map/ppermute | solution.py:49
  123.7 7.4 collective-permute-done.13
  134.2 19.2 %all-gather.4.cloned.1.call-done.weight_ref = bf16[2048,1536]{1,0:T(8,128)(2,1)} async-done(((bf16[512,1536]{1,0:T(8,128)(2,1)}), bf16[2048,1536]{1,0:T(8,128)(2,1)}) %all-gather.4.cloned.1.call-update) | async-done | bytes 6291472 | tf_op jit(solution)/shard_map/all_gather | solution.py:393
  153.4 8.1 fusion.23.refs_0_
  161.5 7.6 fusion.26.refs_1_
  172.4 5.8 fusion.31.gate_ref
  178.2 4.5 fusion.29.gate_ref
  184.9 10.6 %shard_map.144 = (f32[2048,512]{1,0:T(8,128)}, f32[2048,1]{1,0:T(8,128)}, bf16[8,256,512]{2,1,0:T(8,128)(2,1)}) custom-call(s32[8]{0:T(128)} %fusion.53.order, s32[8]{0:T(128)} %get-tuple-element.108.firsts, s32[8]{0:T(128)} %get-tuple-element.107.lasts, s32[1]{0:T(128)} %bitcast.24.before_group, f32[2]{0:T(128)} %broadcast_multiply_fusion.6.floats, ...), custom_call_target="tpu_custom_call" | custom-call | flops 1879048192 | bytes 8388608 | tf_op jit(solution)/shard_map/pallas_call | solution.py:313
  195.5 5.2 multiply_convert_fusion.1
  201.3 4.0 convolution_convert_fusion.3
  205.4 7.1 collective-permute-done.15.refs_0_
  214.5 6.5 shard_map.145
  225.8 10.9 %reduce-scatter.12.cloned.1.call-start = ((), (), s32[]{:S(2)}) async-start(), calls=%async_computation.11 | async-start | bytes 2621440 | tf_op jit(solution)/shard_map/reduce_scatter | solution.py:152
  239.6 7.8 collective-permute-done.16
  248.7 44.9 %collective-permute-done.17 = bf16[256,2048]{1,0:T(8,128)(2,1)} collective-permute-done((bf16[256,2048]{1,0:T(8,128)(2,1)}, bf16[256,2048]{1,0:T(8,128)(2,1)}, u32[]{:S(2)}, u32[]{:S(2)}) %collective-permute-start.17) | collective-permute-done | bytes 1048608 | tf_op jit(solution)/shard_map/ppermute | solution.py:49
  293.7 3.5 fusion.57
  300.5 14.2 %collective-permute-done.22 = bf16[256,2048]{1,0:T(8,128)(2,1)S(1)} collective-permute-done((bf16[256,2048]{1,0:T(8,128)(2,1)S(1)}, bf16[256,2048]{1,0:T(8,128)(2,1)S(1)}, u32[]{:S(2)}, u32[]{:S(2)}) %collective-permute-start.22) | collective-permute-done | bytes 1048608 | tf_op jit(solution)/shard_map/ppermute | solution.py:49
  317.6 2.9 dynamic_update_slice.92
  320.8 16.4 %collective-permute-done.19 = bf16[256,2048]{1,0:T(8,128)(2,1)S(1)} collective-permute-done((bf16[256,2048]{1,0:T(8,128)(2,1)S(1)}, bf16[256,2048]{1,0:T(8,128)(2,1)S(1)}, u32[]{:S(2)}, u32[]{:S(2)}) %collective-permute-start.19) | collective-permute-done | bytes 1048608 | tf_op jit(solution)/shard_map/ppermute | solution.py:49
  338.3 21.6 %collective-permute-done.20 = bf16[256,2048]{1,0:T(8,128)(2,1)S(1)} collective-permute-done((bf16[256,2048]{1,0:T(8,128)(2,1)S(1)}, bf16[256,2048]{1,0:T(8,128)(2,1)S(1)}, u32[]{:S(2)}, u32[]{:S(2)}) %collective-permute-start.20) | collective-permute-done | bytes 1048608 | tf_op jit(solution)/shard_map/ppermute | solution.py:49
  362.0 6.5 fusion.34.grad_ref
  369.5 7.3 shard_map.147
  376.9 6.4 convolution_convert_fusion.2
  383.4 3.6 fusion.36.grad_ref
  387.0 7.3 shard_map.146
  394.4 6.6 shard_map.148
  404.5 4.9 fusion.71
  409.4 5.9 add_convert_fusion.2
  415.8 11.4 %collective-permute-done.28 = bf16[256,2048]{1,0:T(8,128)(2,1)S(1)} collective-permute-done((bf16[256,2048]{1,0:T(8,128)(2,1)}, bf16[256,2048]{1,0:T(8,128)(2,1)S(1)}, u32[]{:S(2)}, u32[]{:S(2)}) %collective-permute-start.28) | collective-permute-done | bytes 1048608 | tf_op jit(solution)/shard_map/ppermute | solution.py:49
  427.2 21.3 %collective-permute-done.29 = bf16[256,2048]{1,0:T(8,128)(2,1)} collective-permute-done((bf16[256,2048]{1,0:T(8,128)(2,1)}, bf16[256,2048]{1,0:T(8,128)(2,1)}, u32[]{:S(2)}, u32[]{:S(2)}) %collective-permute-start.29) | collective-permute-done | bytes 1048608 | tf_op jit(solution)/shard_map/ppermute | solution.py:49
  450.3 3.3 multiply_reduce_fusion
  461.8 20.1 %collective-permute-done.31 = bf16[256,2048]{1,0:T(8,128)(2,1)S(1)} collective-permute-done((bf16[256,2048]{1,0:T(8,128)(2,1)S(1)}, bf16[256,2048]{1,0:T(8,128)(2,1)S(1)}, u32[]{:S(2)}, u32[]{:S(2)}) %collective-permute-start.31) | collective-permute-done | bytes 1048608 | tf_op jit(solution)/shard_map/ppermute | solution.py:49
  483.0 20.1 %collective-permute-done.32 = bf16[256,2048]{1,0:T(8,128)(2,1)S(1)} collective-permute-done((bf16[256,2048]{1,0:T(8,128)(2,1)S(1)}, bf16[256,2048]{1,0:T(8,128)(2,1)S(1)}, u32[]{:S(2)}, u32[]{:S(2)}) %collective-permute-start.32) | collective-permute-done | bytes 1048608 | tf_op jit(solution)/shard_map/ppermute | solution.py:49
  505.3 4.7 fusion.72
  510.0 3.7 add_convert_fusion.1
  513.8 4.9 fusion.69
  518.7 5.9 add_convert_fusion.4
  524.9 8.0 shard_map.149
  532.9 8.1 shard_map.150
  547.6 4.5 convolution_convert_fusion.1
  552.7 4.7 fusion.70
  557.4 5.9 add_convert_fusion.3
  563.6 4.8 collective-permute-done.40.refs_11_
  569.1 14.6 %shard_map.152 = bf16[2048,1536]{1,0:T(8,128)(2,1)} custom-call(s32[8]{0:T(128)} %fusion.53.order, s32[8]{0:T(128)} %get-tuple-element.108.firsts, s32[8]{0:T(128)} %get-tuple-element.107.lasts, s32[1]{0:T(128)} %bitcast.24.before_group, f32[2]{0:T(128)} %broadcast_multiply_fusion.6.floats, bf16[1024,1024]{1,0:T(8,128)(2,1)} %copy-done.45, ...), custom_call_target="tpu_custom_call" | custom-call | flops 5637144576 | bytes 24576000 | tf_op jit(solution)/shard_map/pallas_call | solution.py:313
  583.8 11.1 %convolution_convert_fusion = bf16[1024,2048]{1,0:T(8,128)(2,1)} fusion(bf16[2048,1536]{1,0:T(8,128)(2,1)} %all-gather.4.cloned.1.call-done.weight_ref, bf16[2048,1536]{1,0:T(8,128)(2,1)} %shard_map.152), kind=kOutput, calls=%fused_computation.5 | convolution fusion | flops 6444548096 | bytes 13631488 | tf_op jit(solution)/shard_map/dot_general | solution.py:30
  602.2 4.0 slice.192.rows_ref
  606.2 6.4 fusion.19
  612.6 8.4 %add_convert_fusion = bf16[2048,1024]{1,0:T(8,128)(2,1)} fusion(f32[2048,1024]{1,0:T(8,128)S(1)} %fusion.19, bf16[1024,2048]{1,0:T(8,128)(2,1)} %constant_dynamic-update-slice_fusion.13, bf16[2048,1536]{1,0:T(8,128)(2,1)S(1)} %copy-done.18), kind=kOutput, calls=%fused_computation | convolution fusion | flops 4299161600 | bytes 18874368 | tf_op jit(solution)/shard_map/dot_general | solution.py:30
  623.0 36.3 %reduce-scatter.10.cloned.1.call-done = bf16[512,512]{1,0:T(8,128)(2,1)} async-done(((bf16[2048,512]{1,0:T(8,128)(2,1)}), bf16[512,512]{1,0:T(8,128)(2,1)}) %reduce-scatter.10.cloned.1.call-update) | async-done | bytes 524304 | tf_op jit(solution)/shard_map/reduce_scatter | solution.py:152
  664.7 7.0 shard_map.151
  673.2 12.0 %shard_map.153 = (f32[256,2048]{1,0:T(8,128)}, bf16[256,2048]{1,0:T(8,128)(2,1)}, bf16[256,2048]{1,0:T(8,128)(2,1)}, bf16[256,2048]{1,0:T(8,128)(2,1)}) custom-call(bf16[1024,1536]{1,0:T(8,128)(2,1)} %slice.192.rows_ref, bf16[2048,1536]{1,0:T(8,128)(2,1)} %all-gather.4.cloned.1.call-done.weight_ref, bf16[1024,2048]{1,0:T(8,128)(2,1)} %collective-permute-done.41.refs_0_), custom_call_target="tpu_custom_call" | custom-call | flops 6442450944 | bytes 14680064 | tf_op jit(solution)/shard_map/pallas_call | solution.py:123
  697.3 36.8 %collective-permute-done.42 = bf16[256,2048]{1,0:T(8,128)(2,1)} collective-permute-done((bf16[256,2048]{1,0:T(8,128)(2,1)}, bf16[256,2048]{1,0:T(8,128)(2,1)}, u32[]{:S(2)}, u32[]{:S(2)}) %collective-permute-start.42) | collective-permute-done | bytes 1048608 | tf_op jit(solution)/shard_map/ppermute | solution.py:49
  743.8 34.0 %collective-permute-done.43 = bf16[256,2048]{1,0:T(8,128)(2,1)} collective-permute-done((bf16[256,2048]{1,0:T(8,128)(2,1)}, bf16[256,2048]{1,0:T(8,128)(2,1)}, u32[]{:S(2)}, u32[]{:S(2)}) %collective-permute-start.43) | collective-permute-done | bytes 1048608 | tf_op jit(solution)/shard_map/ppermute | solution.py:49
  777.9 3.8 fusion.17
  806.7 4.2 collective-permute-done.55
  810.9 4.8 collective-permute-done.54
  817.4 3.7 copy.33
  (324 shorter events, 158.7 us)
Async XLA Ops:
  7.2 146.2 %all-gather.4.cloned.1.call-start = ((), (), s32[]{:S(2)}) async-start(), calls=%async_computation.5 | async-start | bytes 7864320 | tf_op jit(solution)/shard_map/all_gather | solution.py:393
  13.6 14.0 %collective-permute-start = (bf16[128,1536]{1,0:T(8,128)(2,1)S(1)}, bf16[128,1536]{1,0:T(8,128)(2,1)S(1)}, u32[]{:S(2)}, u32[]{:S(2)}) collective-permute-start(bf16[128,1536]{1,0:T(8,128)(2,1)S(1)} %bitcast.180), channel_id=1, source_target_pairs={{0,6},{2,4},{4,2},{6,0},{1,7},{3,5},{5,3},{7,1},{8,14},{10,12},{12... | collective-permute-start | bytes 1179656 | tf_op jit(solution)/shard_map/ppermute | solution.py:49
  17.6 17.5 %collective-permute-start.1 = (bf16[128,1536]{1,0:T(8,128)(2,1)S(1)}, bf16[128,1536]{1,0:T(8,128)(2,1)S(1)}, u32[]{:S(2)}, u32[]{:S(2)}) collective-permute-start(bf16[128,1536]{1,0:T(8,128)(2,1)S(1)} %bitcast.181), channel_id=1, source_target_pairs={{0,4},{2,6},{4,0},{6,2},{1,5},{3,7},{5,1},{7,3},{8,12},{10,14},{12... | collective-permute-start | bytes 1179656 | tf_op jit(solution)/shard_map/ppermute | solution.py:49
  18.3 17.1 %collective-permute-start.2 = (bf16[128,1536]{1,0:T(8,128)(2,1)S(1)}, bf16[128,1536]{1,0:T(8,128)(2,1)S(1)}, u32[]{:S(2)}, u32[]{:S(2)}) collective-permute-start(bf16[128,1536]{1,0:T(8,128)(2,1)S(1)} %bitcast.182), channel_id=1, source_target_pairs={{0,2},{2,0},{4,6},{6,4},{1,3},{3,1},{5,7},{7,5},{8,10},{10,8},{12,... | collective-permute-start | bytes 1179656 | tf_op jit(solution)/shard_map/ppermute | solution.py:49
  37.3 163.9 %all-gather.6.cloned.1.call-start = ((), (), s32[]{:S(2)}) async-start(), calls=%async_computation.6 | async-start | bytes 2621440 | tf_op jit(solution)/shard_map/all_gather | solution.py:453
  37.4 14.8 %collective-permute-start.7 = (s32[512]{0:T(512)S(1)}, s32[512]{0:T(512)S(1)}, u32[]{:S(2)}, u32[]{:S(2)}) collective-permute-start(s32[512]{0:T(512)S(1)} %copy-done.35), channel_id=1, source_target_pairs={{0,2},{2,0},{4,6},{6,4},{1,3},{3,1},{5,7},{7,5},{8,10},{10,8},{12,... | collective-permute-start | bytes 6152 | tf_op jit(solution)/shard_map/ppermute | solution.py:49
  39.0 16.7 %collective-permute-start.8 = (s32[512]{0:T(512)S(1)}, s32[512]{0:T(512)S(1)}, u32[]{:S(2)}, u32[]{:S(2)}) collective-permute-start(s32[512]{0:T(512)S(1)} %copy-done.35), channel_id=1, source_target_pairs={{0,4},{2,6},{4,0},{6,2},{1,5},{3,7},{5,1},{7,3},{8,12},{10,14},{12... | collective-permute-start | bytes 6152 | tf_op jit(solution)/shard_map/ppermute | solution.py:49
  46.3 26.2 %collective-permute-start.3 = (bf16[256,2048]{1,0:T(8,128)(2,1)S(1)}, bf16[256,2048]{1,0:T(8,128)(2,1)}, u32[]{:S(2)}, u32[]{:S(2)}) collective-permute-start(bf16[256,2048]{1,0:T(8,128)(2,1)S(1)} %fusion.11), channel_id=1, source_target_pairs={{0,2},{2,0},{4,6},{6,4},{1,3},{3,1},{5,7},{7,5},{8,10},{10,8},{12,... | collective-permute-start | bytes 3145736 | tf_op jit(solution)/shard_map/ppermute | solution.py:49
  47.8 46.9 %collective-permute-start.4 = (bf16[256,2048]{1,0:T(8,128)(2,1)S(1)}, bf16[256,2048]{1,0:T(8,128)(2,1)}, u32[]{:S(2)}, u32[]{:S(2)}) collective-permute-start(bf16[256,2048]{1,0:T(8,128)(2,1)S(1)} %fusion.11), channel_id=1, source_target_pairs={{0,4},{2,6},{4,0},{6,2},{1,5},{3,7},{5,1},{7,3},{8,12},{10,14},{12... | collective-permute-start | bytes 3145736 | tf_op jit(solution)/shard_map/ppermute | solution.py:49
  49.4 47.6 %collective-permute-start.5 = (bf16[256,2048]{1,0:T(8,128)(2,1)S(1)}, bf16[256,2048]{1,0:T(8,128)(2,1)}, u32[]{:S(2)}, u32[]{:S(2)}) collective-permute-start(bf16[256,2048]{1,0:T(8,128)(2,1)S(1)} %fusion.11), channel_id=1, source_target_pairs={{0,6},{2,4},{4,2},{6,0},{1,7},{3,5},{5,3},{7,1},{8,14},{10,12},{12... | collective-permute-start | bytes 3145736 | tf_op jit(solution)/shard_map/ppermute | solution.py:49
  52.2 47.2 %collective-permute-start.9 = (s32[512]{0:T(512)S(1)}, s32[512]{0:T(512)S(1)}, u32[]{:S(2)}, u32[]{:S(2)}) collective-permute-start(s32[512]{0:T(512)S(1)} %copy-done.35), channel_id=1, source_target_pairs={{0,6},{2,4},{4,2},{6,0},{1,7},{3,5},{5,3},{7,1},{8,14},{10,12},{12... | collective-permute-start | bytes 6152 | tf_op jit(solution)/shard_map/ppermute | solution.py:49
  99.4 62.1 %collective-permute-start.6 = (bf16[1024,2048]{1,0:T(8,128)(2,1)}, bf16[1024,2048]{1,0:T(8,128)(2,1)}, u32[]{:S(2)}, u32[]{:S(2)}) collective-permute-start(bf16[1024,2048]{1,0:T(8,128)(2,1)} %constant_dynamic-update-slice_fusion.13), channel_id=1, source_target_pairs={{0,1},{1,0},{2,3},{3,2},{4,5},{5,4},{6,7},{7,6},{8,9},{9,8},{10,11... | collective-permute-start | bytes 12582920 | tf_op jit(solution)/shard_map/ppermute | solution.py:49
  104.0 6.9 collective-permute-start.11
  111.7 12.1 %collective-permute-start.14 = (bf16[128,1536]{1,0:T(8,128)(2,1)S(1)}, bf16[128,1536]{1,0:T(8,128)(2,1)S(1)}, u32[]{:S(2)}, u32[]{:S(2)}) collective-permute-start(bf16[128,1536]{1,0:T(8,128)(2,1)S(1)} %get-tuple-element.153), channel_id=1, source_target_pairs={{0,2},{2,0},{4,6},{6,4},{1,3},{3,1},{5,7},{7,5},{8,10},{10,8},{12,... | collective-permute-start | bytes 1179656 | tf_op jit(solution)/shard_map/ppermute | solution.py:49
  112.3 18.8 %collective-permute-start.13 = (bf16[128,1536]{1,0:T(8,128)(2,1)S(1)}, bf16[128,1536]{1,0:T(8,128)(2,1)S(1)}, u32[]{:S(2)}, u32[]{:S(2)}) collective-permute-start(bf16[128,1536]{1,0:T(8,128)(2,1)S(1)} %get-tuple-element.154), channel_id=1, source_target_pairs={{0,4},{2,6},{4,0},{6,2},{1,5},{3,7},{5,1},{7,3},{8,12},{10,14},{12... | collective-permute-start | bytes 1179656 | tf_op jit(solution)/shard_map/ppermute | solution.py:49
  113.7 17.4 %collective-permute-start.12 = (bf16[128,1536]{1,0:T(8,128)(2,1)S(1)}, bf16[128,1536]{1,0:T(8,128)(2,1)S(1)}, u32[]{:S(2)}, u32[]{:S(2)}) collective-permute-start(bf16[128,1536]{1,0:T(8,128)(2,1)S(1)} %get-tuple-element.155), channel_id=1, source_target_pairs={{0,6},{2,4},{4,2},{6,0},{1,7},{3,5},{5,3},{7,1},{8,14},{10,12},{12... | collective-permute-start | bytes 1179656 | tf_op jit(solution)/shard_map/ppermute | solution.py:49
  134.0 228.1 %all-gather.8.cloned.1.call-start = ((), (), s32[]{:S(2)}) async-start(), calls=%async_computation.7 | async-start | bytes 5242880 | tf_op jit(solution)/shard_map/all_gather | solution.py:454
  170.8 13.4 %collective-permute-start.10 = (bf16[256,512]{1,0:T(8,128)(2,1)S(1)}, bf16[256,512]{1,0:T(8,128)(2,1)S(1)}, u32[]{:S(2)}, u32[]{:S(2)}) collective-permute-start(bf16[256,512]{1,0:T(8,128)(2,1)S(1)} %fusion.38), channel_id=1, source_target_pairs={{0,8},{8,16},{16,24},{1,9},{9,17},{17,25},{2,10},{10,18},{18,26},{... | collective-permute-start | bytes 786440 | tf_op jit(solution)/shard_map/ppermute | solution.py:55
  205.3 7.2 collective-permute-start.15
  221.0 26.4 %collective-permute-start.16 = (bf16[256,2048]{1,0:T(8,128)(2,1)}, bf16[256,2048]{1,0:T(8,128)(2,1)}, u32[]{:S(2)}, u32[]{:S(2)}) collective-permute-start(bf16[256,2048]{1,0:T(8,128)(2,1)} %get-tuple-element.53), channel_id=1, source_target_pairs={{0,2},{2,0},{4,6},{6,4},{1,3},{3,1},{5,7},{7,5},{8,10},{10,8},{12,... | collective-permute-start | bytes 3145736 | tf_op jit(solution)/shard_map/ppermute | solution.py:49
  222.4 71.3 %collective-permute-start.17 = (bf16[256,2048]{1,0:T(8,128)(2,1)}, bf16[256,2048]{1,0:T(8,128)(2,1)}, u32[]{:S(2)}, u32[]{:S(2)}) collective-permute-start(bf16[256,2048]{1,0:T(8,128)(2,1)} %get-tuple-element.54), channel_id=1, source_target_pairs={{0,4},{2,6},{4,0},{6,2},{1,5},{3,7},{5,1},{7,3},{8,12},{10,14},{12... | collective-permute-start | bytes 3145736 | tf_op jit(solution)/shard_map/ppermute | solution.py:49
  224.1 69.6 %collective-permute-start.18 = (bf16[256,2048]{1,0:T(8,128)(2,1)}, bf16[256,2048]{1,0:T(8,128)(2,1)}, u32[]{:S(2)}, u32[]{:S(2)}) collective-permute-start(bf16[256,2048]{1,0:T(8,128)(2,1)} %get-tuple-element.55), channel_id=1, source_target_pairs={{0,6},{2,4},{4,2},{6,0},{1,7},{3,5},{5,3},{7,1},{8,14},{10,12},{12... | collective-permute-start | bytes 3145736 | tf_op jit(solution)/shard_map/ppermute | solution.py:49
  225.8 369.8 %reduce-scatter.12.cloned.1.call-start = ((), (), s32[]{:S(2)}) async-start(), calls=%async_computation.11 | async-start | bytes 2621440 | tf_op jit(solution)/shard_map/reduce_scatter | solution.py:152
  236.7 80.7 %collective-permute-start.24 = (bf16[256,2048]{1,0:T(8,128)(2,1)S(1)}, bf16[256,2048]{1,0:T(8,128)(2,1)S(1)}, u32[]{:S(2)}, u32[]{:S(2)}) collective-permute-start(bf16[256,2048]{1,0:T(8,128)(2,1)S(1)} %constant_dynamic-slice_fusion.9), channel_id=1, source_target_pairs={{0,6},{2,4},{4,2},{6,0},{1,7},{3,5},{5,3},{7,1},{8,14},{10,12},{12... | collective-permute-start | bytes 3145736 | tf_op jit(solution)/shard_map/ppermute | solution.py:49
  239.2 78.1 %collective-permute-start.23 = (bf16[256,2048]{1,0:T(8,128)(2,1)S(1)}, bf16[256,2048]{1,0:T(8,128)(2,1)S(1)}, u32[]{:S(2)}, u32[]{:S(2)}) collective-permute-start(bf16[256,2048]{1,0:T(8,128)(2,1)S(1)} %constant_dynamic-slice_fusion.9), channel_id=1, source_target_pairs={{0,4},{2,6},{4,0},{6,2},{1,5},{3,7},{5,1},{7,3},{8,12},{10,14},{12... | collective-permute-start | bytes 3145736 | tf_op jit(solution)/shard_map/ppermute | solution.py:49
  247.4 67.4 %collective-permute-start.22 = (bf16[256,2048]{1,0:T(8,128)(2,1)S(1)}, bf16[256,2048]{1,0:T(8,128)(2,1)S(1)}, u32[]{:S(2)}, u32[]{:S(2)}) collective-permute-start(bf16[256,2048]{1,0:T(8,128)(2,1)S(1)} %constant_dynamic-slice_fusion.9), channel_id=1, source_target_pairs={{0,2},{2,0},{4,6},{6,4},{1,3},{3,1},{5,7},{7,5},{8,10},{10,8},{12,... | collective-permute-start | bytes 3145736 | tf_op jit(solution)/shard_map/ppermute | solution.py:49
  297.9 39.3 %collective-permute-start.19 = (bf16[256,2048]{1,0:T(8,128)(2,1)S(1)}, bf16[256,2048]{1,0:T(8,128)(2,1)S(1)}, u32[]{:S(2)}, u32[]{:S(2)}) collective-permute-start(bf16[256,2048]{1,0:T(8,128)(2,1)S(1)} %multiply_convert_fusion), channel_id=1, source_target_pairs={{0,2},{2,0},{4,6},{6,4},{1,3},{3,1},{5,7},{7,5},{8,10},{10,8},{12,... | collective-permute-start | bytes 3145736 | tf_op jit(solution)/shard_map/ppermute | solution.py:49
  298.2 61.7 %collective-permute-start.20 = (bf16[256,2048]{1,0:T(8,128)(2,1)S(1)}, bf16[256,2048]{1,0:T(8,128)(2,1)S(1)}, u32[]{:S(2)}, u32[]{:S(2)}) collective-permute-start(bf16[256,2048]{1,0:T(8,128)(2,1)S(1)} %multiply_convert_fusion), channel_id=1, source_target_pairs={{0,4},{2,6},{4,0},{6,2},{1,5},{3,7},{5,1},{7,3},{8,12},{10,14},{12... | collective-permute-start | bytes 3145736 | tf_op jit(solution)/shard_map/ppermute | solution.py:49
  314.7 46.2 %collective-permute-start.21 = (bf16[256,2048]{1,0:T(8,128)(2,1)S(1)}, bf16[256,2048]{1,0:T(8,128)(2,1)S(1)}, u32[]{:S(2)}, u32[]{:S(2)}) collective-permute-start(bf16[256,2048]{1,0:T(8,128)(2,1)S(1)} %multiply_convert_fusion), channel_id=1, source_target_pairs={{0,6},{2,4},{4,2},{6,0},{1,7},{3,5},{5,3},{7,1},{8,14},{10,12},{12... | collective-permute-start | bytes 3145736 | tf_op jit(solution)/shard_map/ppermute | solution.py:49
  317.5 44.5 %collective-permute-start.26 = (bf16[1024,2048]{1,0:T(8,128)(2,1)S(1)}, bf16[1024,2048]{1,0:T(8,128)(2,1)}, u32[]{:S(2)}, u32[]{:S(2)}) collective-permute-start(bf16[1024,2048]{1,0:T(8,128)(2,1)S(1)} %constant_dynamic-update-slice_fusion.7), channel_id=1, source_target_pairs={{0,1},{1,0},{2,3},{3,2},{4,5},{5,4},{6,7},{7,6},{8,9},{9,8},{10,11... | collective-permute-start | bytes 12582920 | tf_op jit(solution)/shard_map/ppermute | solution.py:49
  362.0 7.5 collective-permute-start.25
  383.3 11.1 %collective-permute-start.27 = (bf16[1024,2048]{1,0:T(8,128)(2,1)}, bf16[1024,2048]{1,0:T(8,128)(2,1)}, u32[]{:S(2)}, u32[]{:S(2)}) collective-permute-start(bf16[1024,2048]{1,0:T(8,128)(2,1)} %convolution_convert_fusion.2), channel_id=1, source_target_pairs={{0,1},{1,0},{2,3},{3,2},{4,5},{5,4},{6,7},{7,6},{8,9},{9,8},{10,11... | collective-permute-start | bytes 12582920 | tf_op jit(solution)/shard_map/ppermute | solution.py:49
  401.0 26.2 %collective-permute-start.28 = (bf16[256,2048]{1,0:T(8,128)(2,1)}, bf16[256,2048]{1,0:T(8,128)(2,1)S(1)}, u32[]{:S(2)}, u32[]{:S(2)}) collective-permute-start(bf16[256,2048]{1,0:T(8,128)(2,1)} %get-tuple-element.62), channel_id=1, source_target_pairs={{0,2},{2,0},{4,6},{6,4},{1,3},{3,1},{5,7},{7,5},{8,10},{10,8},{12,... | collective-permute-start | bytes 3145736 | tf_op jit(solution)/shard_map/ppermute | solution.py:49
  401.3 47.2 %collective-permute-start.29 = (bf16[256,2048]{1,0:T(8,128)(2,1)}, bf16[256,2048]{1,0:T(8,128)(2,1)}, u32[]{:S(2)}, u32[]{:S(2)}) collective-permute-start(bf16[256,2048]{1,0:T(8,128)(2,1)} %get-tuple-element.63), channel_id=1, source_target_pairs={{0,4},{2,6},{4,0},{6,2},{1,5},{3,7},{5,1},{7,3},{8,12},{10,14},{12... | collective-permute-start | bytes 3145736 | tf_op jit(solution)/shard_map/ppermute | solution.py:49
  403.0 47.3 %collective-permute-start.30 = (bf16[256,2048]{1,0:T(8,128)(2,1)}, bf16[256,2048]{1,0:T(8,128)(2,1)}, u32[]{:S(2)}, u32[]{:S(2)}) collective-permute-start(bf16[256,2048]{1,0:T(8,128)(2,1)} %get-tuple-element.64), channel_id=1, source_target_pairs={{0,6},{2,4},{4,2},{6,0},{1,7},{3,5},{5,3},{7,1},{8,14},{10,12},{12... | collective-permute-start | bytes 3145736 | tf_op jit(solution)/shard_map/ppermute | solution.py:49
  415.3 181.3 %reduce-scatter.14.cloned.1.call-start = ((), (), s32[]{:S(2)}) async-start(), calls=%async_computation.12 | async-start | bytes 2621440 | tf_op jit(solution)/shard_map/reduce_scatter | solution.py:152
  455.9 26.0 %collective-permute-start.31 = (bf16[256,2048]{1,0:T(8,128)(2,1)S(1)}, bf16[256,2048]{1,0:T(8,128)(2,1)S(1)}, u32[]{:S(2)}, u32[]{:S(2)}) collective-permute-start(bf16[256,2048]{1,0:T(8,128)(2,1)S(1)} %get-tuple-element.110), channel_id=1, source_target_pairs={{0,2},{2,0},{4,6},{6,4},{1,3},{3,1},{5,7},{7,5},{8,10},{10,8},{12,... | collective-permute-start | bytes 3145736 | tf_op jit(solution)/shard_map/ppermute | solution.py:49
  456.5 46.6 %collective-permute-start.32 = (bf16[256,2048]{1,0:T(8,128)(2,1)S(1)}, bf16[256,2048]{1,0:T(8,128)(2,1)S(1)}, u32[]{:S(2)}, u32[]{:S(2)}) collective-permute-start(bf16[256,2048]{1,0:T(8,128)(2,1)S(1)} %get-tuple-element.110), channel_id=1, source_target_pairs={{0,4},{2,6},{4,0},{6,2},{1,5},{3,7},{5,1},{7,3},{8,12},{10,14},{12... | collective-permute-start | bytes 3145736 | tf_op jit(solution)/shard_map/ppermute | solution.py:49
  458.2 46.0 %collective-permute-start.33 = (bf16[256,2048]{1,0:T(8,128)(2,1)S(1)}, bf16[256,2048]{1,0:T(8,128)(2,1)S(1)}, u32[]{:S(2)}, u32[]{:S(2)}) collective-permute-start(bf16[256,2048]{1,0:T(8,128)(2,1)S(1)} %get-tuple-element.110), channel_id=1, source_target_pairs={{0,6},{2,4},{4,2},{6,0},{1,7},{3,5},{5,3},{7,1},{8,14},{10,12},{12... | collective-permute-start | bytes 3145736 | tf_op jit(solution)/shard_map/ppermute | solution.py:49
  505.3 8.5 %collective-permute-start.34 = (bf16[1024,2048]{1,0:T(8,128)(2,1)}, bf16[1024,2048]{1,0:T(8,128)(2,1)}, u32[]{:S(2)}, u32[]{:S(2)}) collective-permute-start(bf16[1024,2048]{1,0:T(8,128)(2,1)} %constant_dynamic-update-slice_fusion.4.grad_ref), channel_id=1, source_target_pairs={{0,1},{1,0},{2,3},{3,2},{4,5},{5,4},{6,7},{7,6},{8,9},{9,8},{10,11... | collective-permute-start | bytes 12582920 | tf_op jit(solution)/shard_map/ppermute | solution.py:49
  513.7 107.3 %reduce-scatter.8.cloned.1.call-start = ((), (), s32[]{:S(2)}) async-start(), calls=%async_computation.9 | async-start | bytes 2621440 | tf_op jit(solution)/shard_map/reduce_scatter | solution.py:152
  524.7 134.6 %reduce-scatter.10.cloned.1.call-start = ((), (), s32[]{:S(2)}) async-start(), calls=%async_computation.10 | async-start | bytes 2621440 | tf_op jit(solution)/shard_map/reduce_scatter | solution.py:152
  546.1 22.3 %collective-permute-start.40 = (bf16[256,512]{1,0:T(8,128)(2,1)}, bf16[256,512]{1,0:T(8,128)(2,1)S(1)}, u32[]{:S(2)}, u32[]{:S(2)}) collective-permute-start(bf16[256,512]{1,0:T(8,128)(2,1)} %convolution_add_fusion), channel_id=1, source_target_pairs={{8,0},{16,8},{24,16},{9,1},{17,9},{25,17},{10,2},{18,10},{26,18},{... | collective-permute-start | bytes 786440 | tf_op jit(solution)/shard_map/ppermute | solution.py:55
  552.1 111.1 %collective-permute-start.35 = (bf16[1024,2048]{1,0:T(8,128)(2,1)}, bf16[1024,2048]{1,0:T(8,128)(2,1)}, u32[]{:S(2)}, u32[]{:S(2)}) collective-permute-start(bf16[1024,2048]{1,0:T(8,128)(2,1)} %convolution_convert_fusion.1), channel_id=1, source_target_pairs={{0,1},{1,0},{2,3},{3,2},{4,5},{5,4},{6,7},{7,6},{8,9},{9,8},{10,11... | collective-permute-start | bytes 12582920 | tf_op jit(solution)/shard_map/ppermute | solution.py:49
  563.4 237.1 %reduce-scatter.6.cloned.1.call-start = ((), (), s32[]{:S(2)}) async-start(), calls=%async_computation.8 | async-start | bytes 5242880 | tf_op jit(solution)/shard_map/reduce_scatter | solution.py:152
  594.9 77.9 %collective-permute-start.41 = (bf16[1024,2048]{1,0:T(8,128)(2,1)}, bf16[1024,2048]{1,0:T(8,128)(2,1)}, u32[]{:S(2)}, u32[]{:S(2)}) collective-permute-start(bf16[1024,2048]{1,0:T(8,128)(2,1)} %convolution_convert_fusion), channel_id=1, source_target_pairs={{0,1},{1,0},{2,3},{3,2},{4,5},{5,4},{6,7},{7,6},{8,9},{9,8},{10,11... | collective-permute-start | bytes 12582920 | tf_op jit(solution)/shard_map/ppermute | solution.py:49
  598.7 72.9 %collective-permute-start.61 = (bf16[128,1024]{1,0:T(8,128)(2,1)}, bf16[128,1024]{1,0:T(8,128)(2,1)S(1)}, u32[]{:S(2)}, u32[]{:S(2)}) collective-permute-start(bf16[128,1024]{1,0:T(8,128)(2,1)} %get-tuple-element.160), channel_id=1, source_target_pairs={{0,2},{2,0},{4,6},{6,4},{1,3},{3,1},{5,7},{7,5},{8,10},{10,8},{12,... | collective-permute-start | bytes 786440 | tf_op jit(solution)/shard_map/ppermute | solution.py:49
  600.1 85.1 %collective-permute-start.60 = (bf16[128,1024]{1,0:T(8,128)(2,1)}, bf16[128,1024]{1,0:T(8,128)(2,1)}, u32[]{:S(2)}, u32[]{:S(2)}) collective-permute-start(bf16[128,1024]{1,0:T(8,128)(2,1)} %get-tuple-element.161), channel_id=1, source_target_pairs={{0,4},{2,6},{4,0},{6,2},{1,5},{3,7},{5,1},{7,3},{8,12},{10,14},{12... | collective-permute-start | bytes 786440 | tf_op jit(solution)/shard_map/ppermute | solution.py:49
  601.7 85.6 %collective-permute-start.59 = (bf16[128,1024]{1,0:T(8,128)(2,1)}, bf16[128,1024]{1,0:T(8,128)(2,1)}, u32[]{:S(2)}, u32[]{:S(2)}) collective-permute-start(bf16[128,1024]{1,0:T(8,128)(2,1)} %get-tuple-element.162), channel_id=1, source_target_pairs={{0,6},{2,4},{4,2},{6,0},{1,7},{3,5},{5,3},{7,1},{8,14},{10,12},{12... | collective-permute-start | bytes 786440 | tf_op jit(solution)/shard_map/ppermute | solution.py:49
  663.2 25.2 %collective-permute-start.58 = (bf16[128,1024]{1,0:T(8,128)(2,1)}, bf16[128,1024]{1,0:T(8,128)(2,1)}, u32[]{:S(2)}, u32[]{:S(2)}) collective-permute-start(bf16[128,1024]{1,0:T(8,128)(2,1)} %get-tuple-element.166), channel_id=1, source_target_pairs={{0,2},{2,0},{4,6},{6,4},{1,3},{3,1},{5,7},{7,5},{8,10},{10,8},{12,... | collective-permute-start | bytes 786440 | tf_op jit(solution)/shard_map/ppermute | solution.py:49
  671.6 17.2 %collective-permute-start.57 = (bf16[128,1024]{1,0:T(8,128)(2,1)}, bf16[128,1024]{1,0:T(8,128)(2,1)}, u32[]{:S(2)}, u32[]{:S(2)}) collective-permute-start(bf16[128,1024]{1,0:T(8,128)(2,1)} %get-tuple-element.167), channel_id=1, source_target_pairs={{0,4},{2,6},{4,0},{6,2},{1,5},{3,7},{5,1},{7,3},{8,12},{10,14},{12... | collective-permute-start | bytes 786440 | tf_op jit(solution)/shard_map/ppermute | solution.py:49
  672.8 16.0 %collective-permute-start.56 = (bf16[128,1024]{1,0:T(8,128)(2,1)}, bf16[128,1024]{1,0:T(8,128)(2,1)}, u32[]{:S(2)}, u32[]{:S(2)}) collective-permute-start(bf16[128,1024]{1,0:T(8,128)(2,1)} %get-tuple-element.168), channel_id=1, source_target_pairs={{0,6},{2,4},{4,2},{6,0},{1,7},{3,5},{5,3},{7,1},{8,14},{10,12},{12... | collective-permute-start | bytes 786440 | tf_op jit(solution)/shard_map/ppermute | solution.py:49
  685.2 96.6 %collective-permute-start.36 = (bf16[256,2048]{1,0:T(8,128)(2,1)}, bf16[256,2048]{1,0:T(8,128)(2,1)}, u32[]{:S(2)}, u32[]{:S(2)}) collective-permute-start(bf16[256,2048]{1,0:T(8,128)(2,1)} %get-tuple-element.71), channel_id=1, source_target_pairs={{0,2},{2,0},{4,6},{6,4},{1,3},{3,1},{5,7},{7,5},{8,10},{10,8},{12,... | collective-permute-start | bytes 3145736 | tf_op jit(solution)/shard_map/ppermute | solution.py:49
  687.3 94.5 %collective-permute-start.37 = (bf16[256,2048]{1,0:T(8,128)(2,1)}, bf16[256,2048]{1,0:T(8,128)(2,1)}, u32[]{:S(2)}, u32[]{:S(2)}) collective-permute-start(bf16[256,2048]{1,0:T(8,128)(2,1)} %get-tuple-element.72), channel_id=1, source_target_pairs={{0,4},{2,6},{4,0},{6,2},{1,5},{3,7},{5,1},{7,3},{8,12},{10,14},{12... | collective-permute-start | bytes 3145736 | tf_op jit(solution)/shard_map/ppermute | solution.py:49
  688.4 45.8 %collective-permute-start.42 = (bf16[256,2048]{1,0:T(8,128)(2,1)}, bf16[256,2048]{1,0:T(8,128)(2,1)}, u32[]{:S(2)}, u32[]{:S(2)}) collective-permute-start(bf16[256,2048]{1,0:T(8,128)(2,1)} %get-tuple-element.80), channel_id=1, source_target_pairs={{0,2},{2,0},{4,6},{6,4},{1,3},{3,1},{5,7},{7,5},{8,10},{10,8},{12,... | collective-permute-start | bytes 3145736 | tf_op jit(solution)/shard_map/ppermute | solution.py:49
  692.2 85.7 %collective-permute-start.43 = (bf16[256,2048]{1,0:T(8,128)(2,1)}, bf16[256,2048]{1,0:T(8,128)(2,1)}, u32[]{:S(2)}, u32[]{:S(2)}) collective-permute-start(bf16[256,2048]{1,0:T(8,128)(2,1)} %get-tuple-element.81), channel_id=1, source_target_pairs={{0,4},{2,6},{4,0},{6,2},{1,5},{3,7},{5,1},{7,3},{8,12},{10,14},{12... | collective-permute-start | bytes 3145736 | tf_op jit(solution)/shard_map/ppermute | solution.py:49
  692.8 85.0 %collective-permute-start.44 = (bf16[256,2048]{1,0:T(8,128)(2,1)}, bf16[256,2048]{1,0:T(8,128)(2,1)}, u32[]{:S(2)}, u32[]{:S(2)}) collective-permute-start(bf16[256,2048]{1,0:T(8,128)(2,1)} %get-tuple-element.82), channel_id=1, source_target_pairs={{0,6},{2,4},{4,2},{6,0},{1,7},{3,5},{5,3},{7,1},{8,14},{10,12},{12... | collective-permute-start | bytes 3145736 | tf_op jit(solution)/shard_map/ppermute | solution.py:49
  734.1 47.7 %collective-permute-start.38 = (bf16[256,2048]{1,0:T(8,128)(2,1)}, bf16[256,2048]{1,0:T(8,128)(2,1)}, u32[]{:S(2)}, u32[]{:S(2)}) collective-permute-start(bf16[256,2048]{1,0:T(8,128)(2,1)} %get-tuple-element.73), channel_id=1, source_target_pairs={{0,6},{2,4},{4,2},{6,0},{1,7},{3,5},{5,3},{7,1},{8,14},{10,12},{12... | collective-permute-start | bytes 3145736 | tf_op jit(solution)/shard_map/ppermute | solution.py:49
  784.6 14.0 %collective-permute-start.39 = (bf16[256,2048]{1,0:T(8,128)(2,1)S(1)}, bf16[256,2048]{1,0:T(8,128)(2,1)S(1)}, u32[]{:S(2)}, u32[]{:S(2)}) collective-permute-start(bf16[256,2048]{1,0:T(8,128)(2,1)S(1)} %add_convert_fusion.5), channel_id=1, source_target_pairs={{0,1},{1,0},{2,3},{3,2},{4,5},{5,4},{6,7},{7,6},{8,9},{9,8},{10,11... | collective-permute-start | bytes 3145736 | tf_op jit(solution)/shard_map/ppermute | solution.py:49
  791.4 5.6 collective-permute-start.52
  793.3 4.6 collective-permute-start.51
  801.7 9.2 %collective-permute-start.55 = (bf16[128,1024]{1,0:T(8,128)(2,1)S(1)}, bf16[128,1024]{1,0:T(8,128)(2,1)S(1)}, u32[]{:S(2)}, u32[]{:S(2)}) collective-permute-start(bf16[128,1024]{1,0:T(8,128)(2,1)S(1)} %get-tuple-element.163), channel_id=1, source_target_pairs={{0,2},{2,0},{4,6},{6,4},{1,3},{3,1},{5,7},{7,5},{8,10},{10,8},{12,... | collective-permute-start | bytes 786440 | tf_op jit(solution)/shard_map/ppermute | solution.py:49
  802.8 12.8 %collective-permute-start.54 = (bf16[128,1024]{1,0:T(8,128)(2,1)S(1)}, bf16[128,1024]{1,0:T(8,128)(2,1)S(1)}, u32[]{:S(2)}, u32[]{:S(2)}) collective-permute-start(bf16[128,1024]{1,0:T(8,128)(2,1)S(1)} %get-tuple-element.164), channel_id=1, source_target_pairs={{0,4},{2,6},{4,0},{6,2},{1,5},{3,7},{5,1},{7,3},{8,12},{10,14},{12... | collective-permute-start | bytes 786440 | tf_op jit(solution)/shard_map/ppermute | solution.py:49
  804.3 11.4 %collective-permute-start.53 = (bf16[128,1024]{1,0:T(8,128)(2,1)S(1)}, bf16[128,1024]{1,0:T(8,128)(2,1)S(1)}, u32[]{:S(2)}, u32[]{:S(2)}) collective-permute-start(bf16[128,1024]{1,0:T(8,128)(2,1)S(1)} %get-tuple-element.165), channel_id=1, source_target_pairs={{0,6},{2,4},{4,2},{6,0},{1,7},{3,5},{5,3},{7,1},{8,14},{10,12},{12... | collective-permute-start | bytes 786440 | tf_op jit(solution)/shard_map/ppermute | solution.py:49
  (53 other events, 423.6 us)
Sparse Core Ops, SparseCore 0:
  37.5 115.8 all-gather.3
  155.0 46.2 all-gather.5
  225.9 88.7 all-gather.7
  415.5 50.8 reduce-scatter.11
  513.8 52.9 reduce-scatter.13
  569.0 45.1 reduce-scatter.7
  616.4 42.8 reduce-scatter.9
  661.6 75.9 reduce-scatter.5
where the time goes:
time: 836 us; the launch traced here: 828 us
  waiting for transfers between devices  400 us (48%)
  matrix products  124 us (15%)
  Pallas kernels  87.9 us (11%)
  starting transfers between devices  84.3 us (10%)
  local copies, waits for them, and re-layouts  70.8 us (8%)
  other arithmetic  39.9 us (5%)
  between operations  21.6 us (3%)
    ppermute x59, waiting for transfers between devices, swap(): return lax.ppermute(value, axis, [(i, i ^ d) for i in range(count)])  337 us
    dot_general x24, matrix products, dot(): lax.dot_general(a, b, (((left,), (right,)), ((), ())), preferred_element_...  124 us
    ppermute x59, starting transfers between devices, swap(): return lax.ppermute(value, axis, [(i, i ^ d) for i in range(count)])  64.3 us
    reduce_scatter x5, waiting for transfers between devices, grads(): return lax.psum_scatter(value, 'group', scatter_dimension=0, tiled=True)  36.3 us
    pallas_call x4, Pallas kernels, reduce(): pl.pallas_call(partial(reduce_kernel, team), grid=(width // step,), in_sp...  32 us
    pallas_call x2, Pallas kernels, walk(): pl.pallas_call(partial(kernel, cores, team), grid_spec=pltpu.PrefetchScal...  25.2 us
    dynamic_update_slice x18, local copies, waits for them, and re-layouts, join(): out = lax.dynamic_update_slice_in_dim(out, part, i * rows, 0)  22.5 us
    all_gather x1, waiting for transfers between devices, shards(): w_mixer_all = whole(mixer_rows)  19.2 us
  transfers between devices with their start and end apart: 70, of which 32 were waited for; matrix products, arithmetic and copies ran while one was open for 25% of the time, Pallas kernels for 8%

commit v1 on v0

--- a/solution.py
+++ b/solution.py
@@ -50,13 +50,13 @@
 
 
 def shift(value, steps):
-    count = lax.axis_size("group")
+    count = lax.axis_size("g")
     pairs = [(i, i + steps) for i in range(count) if 0 <= i + steps < count]
-    return lax.ppermute(value, "group", pairs)
+    return lax.ppermute(value, "g", pairs)
 
 
 def total(value):
-    for axis in ("head", "team", "group"):
+    for axis in ("h", "t", "g"):
         parts = [value] + [swap(value, axis, d) for d in range(1, lax.axis_size(axis))]
         while len(parts) > 1:
             parts = [parts[k] + parts[k + 1] for k in range(0, len(parts), 2)]
@@ -76,11 +76,11 @@
 
 
 def deal(pick):
-    mine = lax.axis_index("team")
+    mine = lax.axis_index("t")
     got = [pick(mine)]
-    for d in range(1, lax.axis_size("team")):
-        got.append(swap(pick(mine ^ d), "team", d))
-    return straight(got, "team")
+    for d in range(1, lax.axis_size("t")):
+        got.append(swap(pick(mine ^ d), "t", d))
+    return straight(got, "t")
 
 
 def join(parts):
@@ -92,9 +92,9 @@
 
 
 def share(own):
-    parts = [own] + [swap(own, "team", d) for d in range(1, lax.axis_size("team"))]
+    parts = [own] + [swap(own, "t", d) for d in range(1, lax.axis_size("t"))]
     rows = join(parts)
-    return [rows] + [swap(rows, "head", e) for e in range(1, lax.axis_size("head"))]
+    return [rows] + [swap(rows, "h", e) for e in range(1, lax.axis_size("h"))]
 
 
 def after(values, first):
@@ -111,14 +111,14 @@
         out[...] = total[d * piece : (d + 1) * piece].astype(out.dtype)
 
 
-def reduce(rows, weight, column):
-    team, cores = lax.axis_size("team"), len(rows)
+def reduce(rows, weight, column, stack=None):
+    team, cores = lax.axis_size("t"), len(rows)
     count, depth = rows[0].shape
     width = weight.shape[0]
     step = min(1024 if depth <= 512 else 512, width)
     part = weight[:, column * depth : (column + 1) * depth]
     first = [dot(rows[e], part, 1, 1).astype(bf16) for e in range(1, cores)]
-    others = [swap(v, "head", e) for e, v in enumerate(first, 1)]
+    others = [swap(v, "h", e) for e, v in enumerate(first, 1)]
     piece = count // team
     out = pl.pallas_call(
         partial(reduce_kernel, team),
@@ -130,14 +130,13 @@
         + [pl.BlockSpec((count, step), lambda i: (0, i))] * (cores - 1),
         out_specs=[pl.BlockSpec((piece, step), lambda i: (0, i))] * team,
         out_shape=[jax.ShapeDtypeStruct((piece, width), bf16 if d else f32) for d in range(team)],
-        compiler_params=pltpu.CompilerParams(dimension_semantics=("arbitrary",)),
         cost_estimate=pl.CostEstimate(
             flops=2 * count * depth * width,
             bytes_accessed=2 * width * (depth + 2 * count),
             transcendentals=0,
         ),
-    )(rows[0], weight, *others)
-    got = [swap(out[d], "team", d) for d in range(1, team)]
+    )(rows[0] if stack is None else stack, weight, *others)
+    got = [swap(out[d], "t", d) for d in range(1, team)]
     value = out[0]
     for v in got:
         value = value + v.astype(f32)
@@ -149,7 +148,7 @@
     for a, b in zip(left[1:], right[1:]):
         value = value + dot(a, b, 0, 0)
     value = value.astype(bf16)
-    return lax.psum_scatter(value, "group", scatter_dimension=0, tiled=True)
+    return lax.psum_scatter(value, "g", scatter_dimension=0, tiled=True)
 
 
 SUB = 128
@@ -184,7 +183,6 @@
         ],
         out_specs=[pl.BlockSpec((size, units), own)] * 2,
         out_shape=[shape] * 2,
-        compiler_params=pltpu.CompilerParams(dimension_semantics=("arbitrary",)),
         cost_estimate=pl.CostEstimate(
             flops=2 * rows * width * units, bytes_accessed=2 * rows * width, transcendentals=0
         ),
@@ -320,7 +318,6 @@
             scratch_shapes=[pltpu.VMEM((KEY, VALUE), f32)],
         ),
         out_shape=[shape for shape, _, _ in outs],
-        compiler_params=pltpu.CompilerParams(dimension_semantics=("arbitrary",)),
         cost_estimate=pl.CostEstimate(flops=flops, bytes_accessed=moved, transcendentals=0),
     )(*edges, *arrays)
 
@@ -361,7 +358,6 @@
         ],
         out_specs=[pl.BlockSpec((size, VALUE), own)] * 3,
         out_shape=[shape] * 3,
-        compiler_params=pltpu.CompilerParams(dimension_semantics=("arbitrary",)),
         cost_estimate=pl.CostEstimate(
             flops=2 * rows * width * VALUE, bytes_accessed=2 * rows * width, transcendentals=0
         ),
@@ -369,8 +365,8 @@
 
 
 def shards(tokens, norm_gains, w_mixer, w_out, w_up, w_down, seg_ids, cotangent):
-    team, _, cores = (lax.axis_size(a) for a in ("team", "group", "head"))
-    _, j, c = (lax.axis_index(a) for a in ("group", "team", "head"))
+    team, _, cores = (lax.axis_size(a) for a in ("t", "g", "h"))
+    _, j, c = (lax.axis_index(a) for a in ("g", "t", "h"))
     heads_here = w_mixer.shape[2]
     length, _ = tokens.shape
     size = length // cores
@@ -389,10 +385,10 @@
         axis=2,
     )
     mixer_rows = join(deal(lambda m: lax.dynamic_index_in_dim(mixer_slabs, m, 0, keepdims=False)))
-    whole = partial(lax.all_gather, axis_name="group", axis=0, tiled=True)
+    whole = partial(lax.all_gather, axis_name="g", axis=0, tiled=True)
     w_mixer_all = whole(mixer_rows)
 
-    segs = [seg_ids] + [swap(seg_ids, "team", d) for d in range(1, team)]
+    segs = [seg_ids] + [swap(seg_ids, "t", d) for d in range(1, team)]
     seg = jnp.stack(
         [
             lax.dynamic_slice_in_dim(segs[d], (c ^ e) * size, size, 0)
@@ -499,8 +495,8 @@
 
     def both_cores(rows):
         rows = rows.astype(bf16)
-        got = [rows] + [swap(rows, "head", e) for e in range(1, cores)]
-        return join(straight(got, "head"))
+        got = [rows] + [swap(rows, "h", e) for e in range(1, cores)]
+        return join(straight(got, "h"))
 
     grad_hidden2, sent = reduce(grad_up, w_ud, 0)
     down_done = grads(after(cot_all, sent), act)
@@ -516,7 +512,7 @@
     gate_done = grads(hidden, grad_gate)
     grad_before = state_sum([v[:, :KEY] for v in qkv], from_start, grad_mixed)
     grad_in = passed(grad_before, -1)
-    stream = stream + reduce(after(act, grad_before), w_ud, 1)[0]
+    added = reduce(after(act, grad_before), w_ud, 1)[0]
     (proj,) = walk(
         backward_kernel,
         cores,
@@ -542,8 +538,8 @@
     )
     grad_proj = [here(proj, e) for e in near]
     qkv_done = grads(hidden, [v[:, : 2 * KEY + VALUE] for v in grad_proj])
-    grad_hidden = reduce(grad_proj, w_mixer_all, 0)[0]
-    output = both_cores(stream)
+    grad_hidden = reduce(grad_proj, w_mixer_all, 0, proj)[0]
+    output = both_cores(stream + added)
     norm_part, gain_grad_one = norm_back(grad_hidden, normed1, scaled1, gain_one)
     input_grad = both_cores(grad + norm_part)
     gain_grad = total(jnp.stack([gain_grad_one, gain_grad_two]))
@@ -578,8 +574,8 @@
 def solution(mesh):
     devices, cores = mesh.devices.shape
     team = team_size(devices, HEADS // cores)
-    fine = Mesh(mesh.devices.reshape(devices // team, team, cores), ("group", "team", "head"))
-    fsdp = ("group", "team")
+    fine = Mesh(mesh.devices.reshape(devices // team, team, cores), ("g", "t", "h"))
+    fsdp = ("g", "t")
 
     return jax.shard_map(
         shards,
@@ -587,10 +583,10 @@
         in_specs=(
             P(fsdp, None),
             P(),
-            P(None, fsdp, "head", None),
-            P(None, "head", fsdp),
-            P(None, fsdp, "head"),
-            P(None, "head", fsdp),
+            P(None, fsdp, "h", None),
+            P(None, "h", fsdp),
+            P(None, fsdp, "h"),
+            P(None, "h", fsdp),
             P(fsdp),
             P(fsdp, None),
         ),
@@ -598,10 +594,10 @@
             P(fsdp, None),
             P(fsdp, None),
             P(),
-            P(None, fsdp, "head", None),
-            P(None, "head", fsdp),
-            P(None, fsdp, "head"),
-            P(None, "head", fsdp),
+            P(None, fsdp, "h", None),
+            P(None, "h", fsdp),
+            P(None, fsdp, "h"),
+            P(None, "h", fsdp),
         ),
         check_vma=False,
     )

time: 836 us -> 836 us (level)
    unnamed x105 -> x103, local copies, waits for them, and re-layouts: 17 us -> 16.9 us
  transfers between devices with their start and end apart: 70 -> 70, of which waited for: 32 -> 32; matrix products, arithmetic and copies ran while one was open for 25% -> 24% of each run, Pallas kernels for 8% -> 8%
where the time goes in v1:
time: 836 us; the launch traced here: 828 us
  waiting for transfers between devices  402 us (48%)
  matrix products  126 us (15%)
  Pallas kernels  87.7 us (10%)
  starting transfers between devices  84.3 us (10%)
  local copies, waits for them, and re-layouts  66.7 us (8%)
  other arithmetic  39.8 us (5%)
  between operations  21.6 us (3%)
    ppermute x59, waiting for transfers between devices, swap(): return lax.ppermute(value, axis, [(i, i ^ d) for i in range(count)])  337 us
    dot_general x24, matrix products, dot(): lax.dot_general(a, b, (((left,), (right,)), ((), ())), preferred_element_...  126 us
    ppermute x59, starting transfers between devices, swap(): return lax.ppermute(value, axis, [(i, i ^ d) for i in range(count)])  64.4 us
    reduce_scatter x5, waiting for transfers between devices, grads(): return lax.psum_scatter(value, 'g', scatter_dimension=0, tiled=True)  38.6 us
    pallas_call x4, Pallas kernels, reduce(): pl.pallas_call(partial(reduce_kernel, team), grid=(width // step,), in_sp...  31.8 us
    pallas_call x2, Pallas kernels, walk(): pl.pallas_call(partial(kernel, cores, team), grid_spec=pltpu.PrefetchScal...  25.2 us
    dynamic_update_slice x18, local copies, waits for them, and re-layouts, join(): out = lax.dynamic_update_slice_in_dim(out, part, i * rows, 0)  22.5 us
    all_gather x1, waiting for transfers between devices, shards(): w_mixer_all = whole(mixer_rows)  19.1 us
  transfers between devices with their start and end apart: 70, of which 32 were waited for; matrix products, arithmetic and copies ran while one was open for 24% of the time, Pallas kernels for 8%

profile of v1, /device:TPU:0, one launch (start us, length us, event | category | flops | bytes accessed | tf_op | source)
XLA Modules:
  0.0 828.1 jit_solution(7042760687484763793)
XLA Ops:
  7.2 6.3 constant_dynamic-slice_fusion.10
  13.6 4.0 collective-permute-start
  18.4 9.2 %collective-permute-done = bf16[128,1536]{1,0:T(8,128)(2,1)S(1)} collective-permute-done((bf16[128,1536]{1,0:T(8,128)(2,1)S(1)}, bf16[128,1536]{1,0:T(8,128)(2,1)S(1)}, u32[]{:S(2)}, u32[]{:S(2)}) %collective-permute-start) | collective-permute-done | bytes 393248 | tf_op jit(solution)/shard_map/ppermute | solution.py:49
  27.6 7.5 collective-permute-done.1
  59.5 13.0 %collective-permute-done.3 = bf16[256,2048]{1,0:T(8,128)(2,1)} collective-permute-done((bf16[256,2048]{1,0:T(8,128)(2,1)S(1)}, bf16[256,2048]{1,0:T(8,128)(2,1)}, u32[]{:S(2)}, u32[]{:S(2)}) %collective-permute-start.3) | collective-permute-done | bytes 1048608 | tf_op jit(solution)/shard_map/ppermute | solution.py:49
  74.8 19.9 %collective-permute-done.4 = bf16[256,2048]{1,0:T(8,128)(2,1)} collective-permute-done((bf16[256,2048]{1,0:T(8,128)(2,1)S(1)}, bf16[256,2048]{1,0:T(8,128)(2,1)}, u32[]{:S(2)}, u32[]{:S(2)}) %collective-permute-start.4) | collective-permute-done | bytes 1048608 | tf_op jit(solution)/shard_map/ppermute | solution.py:49
  104.1 4.7 collective-permute-start.11
  115.3 8.5 %collective-permute-done.14 = bf16[128,1536]{1,0:T(8,128)(2,1)S(1)} collective-permute-done((bf16[128,1536]{1,0:T(8,128)(2,1)S(1)}, bf16[128,1536]{1,0:T(8,128)(2,1)S(1)}, u32[]{:S(2)}, u32[]{:S(2)}) %collective-permute-start.14) | collective-permute-done | bytes 393248 | tf_op jit(solution)/shard_map/ppermute | solution.py:49
  123.8 7.4 collective-permute-done.13
  134.3 19.1 %all-gather.4.cloned.1.call-done.weight_ref = bf16[2048,1536]{1,0:T(8,128)(2,1)} async-done(((bf16[512,1536]{1,0:T(8,128)(2,1)}), bf16[2048,1536]{1,0:T(8,128)(2,1)}) %all-gather.4.cloned.1.call-update) | async-done | bytes 6291472 | tf_op jit(solution)/shard_map/all_gather | solution.py:389
  153.4 8.1 fusion.23.refs_0_
  161.5 7.6 fusion.26.refs_1_
  172.4 5.8 fusion.31.gate_ref
  178.2 4.5 fusion.29.gate_ref
  184.9 10.5 %shard_map.144 = (f32[2048,512]{1,0:T(8,128)}, f32[2048,1]{1,0:T(8,128)}, bf16[8,256,512]{2,1,0:T(8,128)(2,1)}) custom-call(s32[8]{0:T(128)} %fusion.53.order, s32[8]{0:T(128)} %get-tuple-element.108.firsts, s32[8]{0:T(128)} %get-tuple-element.107.lasts, s32[1]{0:T(128)} %bitcast.24.before_group, f32[2]{0:T(128)} %broadcast_multiply_fusion.6.floats, ...), custom_call_target="tpu_custom_call" | custom-call | flops 1879048192 | bytes 8388608 | tf_op jit(solution)/shard_map/pallas_call | solution.py:311
  195.4 5.2 multiply_convert_fusion.1
  201.3 4.0 convolution_convert_fusion.3
  205.4 7.1 collective-permute-done.15.refs_0_
  214.5 6.3 shard_map.145
  225.7 10.9 %reduce-scatter.12.cloned.1.call-start = ((), (), s32[]{:S(2)}) async-start(), calls=%async_computation.11 | async-start | bytes 2621440 | tf_op jit(solution)/shard_map/reduce_scatter | solution.py:151
  239.4 7.8 collective-permute-done.16
  248.6 44.9 %collective-permute-done.17 = bf16[256,2048]{1,0:T(8,128)(2,1)} collective-permute-done((bf16[256,2048]{1,0:T(8,128)(2,1)}, bf16[256,2048]{1,0:T(8,128)(2,1)}, u32[]{:S(2)}, u32[]{:S(2)}) %collective-permute-start.17) | collective-permute-done | bytes 1048608 | tf_op jit(solution)/shard_map/ppermute | solution.py:49
  293.5 3.5 fusion.57
  300.4 14.2 %collective-permute-done.22 = bf16[256,2048]{1,0:T(8,128)(2,1)S(1)} collective-permute-done((bf16[256,2048]{1,0:T(8,128)(2,1)S(1)}, bf16[256,2048]{1,0:T(8,128)(2,1)S(1)}, u32[]{:S(2)}, u32[]{:S(2)}) %collective-permute-start.22) | collective-permute-done | bytes 1048608 | tf_op jit(solution)/shard_map/ppermute | solution.py:49
  317.5 2.9 dynamic_update_slice.92
  320.7 16.4 %collective-permute-done.19 = bf16[256,2048]{1,0:T(8,128)(2,1)S(1)} collective-permute-done((bf16[256,2048]{1,0:T(8,128)(2,1)S(1)}, bf16[256,2048]{1,0:T(8,128)(2,1)S(1)}, u32[]{:S(2)}, u32[]{:S(2)}) %collective-permute-start.19) | collective-permute-done | bytes 1048608 | tf_op jit(solution)/shard_map/ppermute | solution.py:49
  338.1 21.6 %collective-permute-done.20 = bf16[256,2048]{1,0:T(8,128)(2,1)S(1)} collective-permute-done((bf16[256,2048]{1,0:T(8,128)(2,1)S(1)}, bf16[256,2048]{1,0:T(8,128)(2,1)S(1)}, u32[]{:S(2)}, u32[]{:S(2)}) %collective-permute-start.20) | collective-permute-done | bytes 1048608 | tf_op jit(solution)/shard_map/ppermute | solution.py:49
  361.9 6.5 fusion.34.grad_ref
  369.4 7.3 shard_map.147
  376.7 6.4 convolution_convert_fusion.2
  383.3 3.6 fusion.36.grad_ref
  386.9 7.3 shard_map.146
  394.2 6.5 shard_map.148
  404.2 5.0 fusion.71
  409.2 5.9 add_convert_fusion.2
  415.6 11.4 %collective-permute-done.28 = bf16[256,2048]{1,0:T(8,128)(2,1)S(1)} collective-permute-done((bf16[256,2048]{1,0:T(8,128)(2,1)}, bf16[256,2048]{1,0:T(8,128)(2,1)S(1)}, u32[]{:S(2)}, u32[]{:S(2)}) %collective-permute-start.28) | collective-permute-done | bytes 1048608 | tf_op jit(solution)/shard_map/ppermute | solution.py:49
  427.0 21.3 %collective-permute-done.29 = bf16[256,2048]{1,0:T(8,128)(2,1)} collective-permute-done((bf16[256,2048]{1,0:T(8,128)(2,1)}, bf16[256,2048]{1,0:T(8,128)(2,1)}, u32[]{:S(2)}, u32[]{:S(2)}) %collective-permute-start.29) | collective-permute-done | bytes 1048608 | tf_op jit(solution)/shard_map/ppermute | solution.py:49
  450.1 3.3 multiply_reduce_fusion
  461.7 20.1 %collective-permute-done.31 = bf16[256,2048]{1,0:T(8,128)(2,1)S(1)} collective-permute-done((bf16[256,2048]{1,0:T(8,128)(2,1)S(1)}, bf16[256,2048]{1,0:T(8,128)(2,1)S(1)}, u32[]{:S(2)}, u32[]{:S(2)}) %collective-permute-start.31) | collective-permute-done | bytes 1048608 | tf_op jit(solution)/shard_map/ppermute | solution.py:49
  482.8 20.1 %collective-permute-done.32 = bf16[256,2048]{1,0:T(8,128)(2,1)S(1)} collective-permute-done((bf16[256,2048]{1,0:T(8,128)(2,1)S(1)}, bf16[256,2048]{1,0:T(8,128)(2,1)S(1)}, u32[]{:S(2)}, u32[]{:S(2)}) %collective-permute-start.32) | collective-permute-done | bytes 1048608 | tf_op jit(solution)/shard_map/ppermute | solution.py:49
  505.1 4.7 fusion.72
  509.8 3.7 add_convert_fusion.1
  513.6 4.9 fusion.69
  518.6 5.9 add_convert_fusion.4
  524.7 8.1 shard_map.149
  532.8 8.0 shard_map.150
  543.1 2.9 convolution_add_fusion
  547.4 4.5 convolution_convert_fusion.1
  552.6 4.7 fusion.70
  557.3 5.9 add_convert_fusion.3
  563.5 4.7 collective-permute-done.40.refs_11_
  568.9 14.6 %shard_map.152.rows_ref = bf16[2048,1536]{1,0:T(8,128)(2,1)} custom-call(s32[8]{0:T(128)} %fusion.53.order, s32[8]{0:T(128)} %get-tuple-element.108.firsts, s32[8]{0:T(128)} %get-tuple-element.107.lasts, s32[1]{0:T(128)} %bitcast.24.before_group, f32[2]{0:T(128)} %broadcast_multiply_fusion.6.floats, bf16[1024,1024]{1,0:T(8,128)(2,1)} %copy-done.44, ...), custom_call_target="tpu_custom_call" | custom-call | flops 5637144576 | bytes 24576000 | tf_op jit(solution)/shard_map/pallas_call | solution.py:311
  583.5 11.2 %convolution_convert_fusion = bf16[1024,2048]{1,0:T(8,128)(2,1)} fusion(bf16[2048,1536]{1,0:T(8,128)(2,1)} %all-gather.4.cloned.1.call-done.weight_ref, bf16[2048,1536]{1,0:T(8,128)(2,1)} %shard_map.152.rows_ref), kind=kOutput, calls=%fused_computation.5 | convolution fusion | flops 6444548096 | bytes 13631488 | tf_op jit(solution)/shard_map/dot_general | solution.py:30
  602.1 7.0 fusion.19
  609.1 9.5 %add_convert_fusion = bf16[2048,1024]{1,0:T(8,128)(2,1)} fusion(f32[2048,1024]{1,0:T(8,128)S(1)} %fusion.19, bf16[1024,2048]{1,0:T(8,128)(2,1)} %constant_dynamic-update-slice_fusion.13, bf16[2048,1536]{1,0:T(8,128)(2,1)} %shard_map.152.rows_ref), kind=kOutput, calls=%fused_computation | convolution fusion | flops 4299161600 | bytes 18874368 | tf_op jit(solution)/shard_map/dot_general | solution.py:30
  620.5 38.6 %reduce-scatter.10.cloned.1.call-done = bf16[512,512]{1,0:T(8,128)(2,1)} async-done(((bf16[2048,512]{1,0:T(8,128)(2,1)}), bf16[512,512]{1,0:T(8,128)(2,1)}) %reduce-scatter.10.cloned.1.call-update) | async-done | bytes 524304 | tf_op jit(solution)/shard_map/reduce_scatter | solution.py:151
  664.4 6.9 shard_map.151
  673.0 12.0 %shard_map.153 = (f32[256,2048]{1,0:T(8,128)}, bf16[256,2048]{1,0:T(8,128)(2,1)}, bf16[256,2048]{1,0:T(8,128)(2,1)}, bf16[256,2048]{1,0:T(8,128)(2,1)}) custom-call(bf16[2048,1536]{1,0:T(8,128)(2,1)} %shard_map.152.rows_ref, bf16[2048,1536]{1,0:T(8,128)(2,1)} %all-gather.4.cloned.1.call-done.weight_ref, bf16[1024,2048]{1,0:T(8,128)(2,1)} %collective-permute-done.41.refs_0_), custom_call_target="tpu_custom_call" | custom-call | flops 6442450944 | bytes 14680064 | tf_op jit(solution)/shard_map/pallas_call | solution.py:123
  697.1 36.8 %collective-permute-done.42 = bf16[256,2048]{1,0:T(8,128)(2,1)} collective-permute-done((bf16[256,2048]{1,0:T(8,128)(2,1)}, bf16[256,2048]{1,0:T(8,128)(2,1)}, u32[]{:S(2)}, u32[]{:S(2)}) %collective-permute-start.42) | collective-permute-done | bytes 1048608 | tf_op jit(solution)/shard_map/ppermute | solution.py:49
  743.6 34.0 %collective-permute-done.43 = bf16[256,2048]{1,0:T(8,128)(2,1)} collective-permute-done((bf16[256,2048]{1,0:T(8,128)(2,1)}, bf16[256,2048]{1,0:T(8,128)(2,1)}, u32[]{:S(2)}, u32[]{:S(2)}) %collective-permute-start.43) | collective-permute-done | bytes 1048608 | tf_op jit(solution)/shard_map/ppermute | solution.py:49
  777.6 3.8 fusion.17
  806.4 4.2 collective-permute-done.55
  810.7 4.8 collective-permute-done.54
  817.2 3.7 copy.33
  (321 shorter events, 155.6 us)
Async XLA Ops:
  7.2 146.2 %all-gather.4.cloned.1.call-start = ((), (), s32[]{:S(2)}) async-start(), calls=%async_computation.5 | async-start | bytes 7864320 | tf_op jit(solution)/shard_map/all_gather | solution.py:389
  13.6 14.0 %collective-permute-start = (bf16[128,1536]{1,0:T(8,128)(2,1)S(1)}, bf16[128,1536]{1,0:T(8,128)(2,1)S(1)}, u32[]{:S(2)}, u32[]{:S(2)}) collective-permute-start(bf16[128,1536]{1,0:T(8,128)(2,1)S(1)} %bitcast.180), channel_id=1, source_target_pairs={{0,6},{2,4},{4,2},{6,0},{1,7},{3,5},{5,3},{7,1},{8,14},{10,12},{12... | collective-permute-start | bytes 1179656 | tf_op jit(solution)/shard_map/ppermute | solution.py:49
  17.6 17.5 %collective-permute-start.1 = (bf16[128,1536]{1,0:T(8,128)(2,1)S(1)}, bf16[128,1536]{1,0:T(8,128)(2,1)S(1)}, u32[]{:S(2)}, u32[]{:S(2)}) collective-permute-start(bf16[128,1536]{1,0:T(8,128)(2,1)S(1)} %bitcast.181), channel_id=1, source_target_pairs={{0,4},{2,6},{4,0},{6,2},{1,5},{3,7},{5,1},{7,3},{8,12},{10,14},{12... | collective-permute-start | bytes 1179656 | tf_op jit(solution)/shard_map/ppermute | solution.py:49
  18.3 17.1 %collective-permute-start.2 = (bf16[128,1536]{1,0:T(8,128)(2,1)S(1)}, bf16[128,1536]{1,0:T(8,128)(2,1)S(1)}, u32[]{:S(2)}, u32[]{:S(2)}) collective-permute-start(bf16[128,1536]{1,0:T(8,128)(2,1)S(1)} %bitcast.182), channel_id=1, source_target_pairs={{0,2},{2,0},{4,6},{6,4},{1,3},{3,1},{5,7},{7,5},{8,10},{10,8},{12,... | collective-permute-start | bytes 1179656 | tf_op jit(solution)/shard_map/ppermute | solution.py:49
  37.3 163.9 %all-gather.6.cloned.1.call-start = ((), (), s32[]{:S(2)}) async-start(), calls=%async_computation.6 | async-start | bytes 2621440 | tf_op jit(solution)/shard_map/all_gather | solution.py:449
  37.4 14.7 %collective-permute-start.7 = (s32[512]{0:T(512)S(1)}, s32[512]{0:T(512)S(1)}, u32[]{:S(2)}, u32[]{:S(2)}) collective-permute-start(s32[512]{0:T(512)S(1)} %copy-done.34), channel_id=1, source_target_pairs={{0,2},{2,0},{4,6},{6,4},{1,3},{3,1},{5,7},{7,5},{8,10},{10,8},{12,... | collective-permute-start | bytes 6152 | tf_op jit(solution)/shard_map/ppermute | solution.py:49
  39.0 16.6 %collective-permute-start.8 = (s32[512]{0:T(512)S(1)}, s32[512]{0:T(512)S(1)}, u32[]{:S(2)}, u32[]{:S(2)}) collective-permute-start(s32[512]{0:T(512)S(1)} %copy-done.34), channel_id=1, source_target_pairs={{0,4},{2,6},{4,0},{6,2},{1,5},{3,7},{5,1},{7,3},{8,12},{10,14},{12... | collective-permute-start | bytes 6152 | tf_op jit(solution)/shard_map/ppermute | solution.py:49
  46.3 26.2 %collective-permute-start.3 = (bf16[256,2048]{1,0:T(8,128)(2,1)S(1)}, bf16[256,2048]{1,0:T(8,128)(2,1)}, u32[]{:S(2)}, u32[]{:S(2)}) collective-permute-start(bf16[256,2048]{1,0:T(8,128)(2,1)S(1)} %fusion.11), channel_id=1, source_target_pairs={{0,2},{2,0},{4,6},{6,4},{1,3},{3,1},{5,7},{7,5},{8,10},{10,8},{12,... | collective-permute-start | bytes 3145736 | tf_op jit(solution)/shard_map/ppermute | solution.py:49
  47.8 46.9 %collective-permute-start.4 = (bf16[256,2048]{1,0:T(8,128)(2,1)S(1)}, bf16[256,2048]{1,0:T(8,128)(2,1)}, u32[]{:S(2)}, u32[]{:S(2)}) collective-permute-start(bf16[256,2048]{1,0:T(8,128)(2,1)S(1)} %fusion.11), channel_id=1, source_target_pairs={{0,4},{2,6},{4,0},{6,2},{1,5},{3,7},{5,1},{7,3},{8,12},{10,14},{12... | collective-permute-start | bytes 3145736 | tf_op jit(solution)/shard_map/ppermute | solution.py:49
  49.4 47.6 %collective-permute-start.5 = (bf16[256,2048]{1,0:T(8,128)(2,1)S(1)}, bf16[256,2048]{1,0:T(8,128)(2,1)}, u32[]{:S(2)}, u32[]{:S(2)}) collective-permute-start(bf16[256,2048]{1,0:T(8,128)(2,1)S(1)} %fusion.11), channel_id=1, source_target_pairs={{0,6},{2,4},{4,2},{6,0},{1,7},{3,5},{5,3},{7,1},{8,14},{10,12},{12... | collective-permute-start | bytes 3145736 | tf_op jit(solution)/shard_map/ppermute | solution.py:49
  52.1 47.3 %collective-permute-start.9 = (s32[512]{0:T(512)S(1)}, s32[512]{0:T(512)S(1)}, u32[]{:S(2)}, u32[]{:S(2)}) collective-permute-start(s32[512]{0:T(512)S(1)} %copy-done.34), channel_id=1, source_target_pairs={{0,6},{2,4},{4,2},{6,0},{1,7},{3,5},{5,3},{7,1},{8,14},{10,12},{12... | collective-permute-start | bytes 6152 | tf_op jit(solution)/shard_map/ppermute | solution.py:49
  99.4 62.1 %collective-permute-start.6 = (bf16[1024,2048]{1,0:T(8,128)(2,1)}, bf16[1024,2048]{1,0:T(8,128)(2,1)}, u32[]{:S(2)}, u32[]{:S(2)}) collective-permute-start(bf16[1024,2048]{1,0:T(8,128)(2,1)} %constant_dynamic-update-slice_fusion.13), channel_id=1, source_target_pairs={{0,1},{1,0},{2,3},{3,2},{4,5},{5,4},{6,7},{7,6},{8,9},{9,8},{10,11... | collective-permute-start | bytes 12582920 | tf_op jit(solution)/shard_map/ppermute | solution.py:49
  104.1 6.9 collective-permute-start.11
  111.7 12.1 %collective-permute-start.14 = (bf16[128,1536]{1,0:T(8,128)(2,1)S(1)}, bf16[128,1536]{1,0:T(8,128)(2,1)S(1)}, u32[]{:S(2)}, u32[]{:S(2)}) collective-permute-start(bf16[128,1536]{1,0:T(8,128)(2,1)S(1)} %get-tuple-element.153), channel_id=1, source_target_pairs={{0,2},{2,0},{4,6},{6,4},{1,3},{3,1},{5,7},{7,5},{8,10},{10,8},{12,... | collective-permute-start | bytes 1179656 | tf_op jit(solution)/shard_map/ppermute | solution.py:49
  112.4 18.8 %collective-permute-start.13 = (bf16[128,1536]{1,0:T(8,128)(2,1)S(1)}, bf16[128,1536]{1,0:T(8,128)(2,1)S(1)}, u32[]{:S(2)}, u32[]{:S(2)}) collective-permute-start(bf16[128,1536]{1,0:T(8,128)(2,1)S(1)} %get-tuple-element.154), channel_id=1, source_target_pairs={{0,4},{2,6},{4,0},{6,2},{1,5},{3,7},{5,1},{7,3},{8,12},{10,14},{12... | collective-permute-start | bytes 1179656 | tf_op jit(solution)/shard_map/ppermute | solution.py:49
  113.8 17.4 %collective-permute-start.12 = (bf16[128,1536]{1,0:T(8,128)(2,1)S(1)}, bf16[128,1536]{1,0:T(8,128)(2,1)S(1)}, u32[]{:S(2)}, u32[]{:S(2)}) collective-permute-start(bf16[128,1536]{1,0:T(8,128)(2,1)S(1)} %get-tuple-element.155), channel_id=1, source_target_pairs={{0,6},{2,4},{4,2},{6,0},{1,7},{3,5},{5,3},{7,1},{8,14},{10,12},{12... | collective-permute-start | bytes 1179656 | tf_op jit(solution)/shard_map/ppermute | solution.py:49
  134.0 227.9 %all-gather.8.cloned.1.call-start = ((), (), s32[]{:S(2)}) async-start(), calls=%async_computation.7 | async-start | bytes 5242880 | tf_op jit(solution)/shard_map/all_gather | solution.py:450
  170.8 13.4 %collective-permute-start.10 = (bf16[256,512]{1,0:T(8,128)(2,1)S(1)}, bf16[256,512]{1,0:T(8,128)(2,1)S(1)}, u32[]{:S(2)}, u32[]{:S(2)}) collective-permute-start(bf16[256,512]{1,0:T(8,128)(2,1)S(1)} %fusion.38), channel_id=1, source_target_pairs={{0,8},{8,16},{16,24},{1,9},{9,17},{17,25},{2,10},{10,18},{18,26},{... | collective-permute-start | bytes 786440 | tf_op jit(solution)/shard_map/ppermute | solution.py:55
  205.3 7.2 collective-permute-start.15
  220.9 26.4 %collective-permute-start.16 = (bf16[256,2048]{1,0:T(8,128)(2,1)}, bf16[256,2048]{1,0:T(8,128)(2,1)}, u32[]{:S(2)}, u32[]{:S(2)}) collective-permute-start(bf16[256,2048]{1,0:T(8,128)(2,1)} %get-tuple-element.53), channel_id=1, source_target_pairs={{0,2},{2,0},{4,6},{6,4},{1,3},{3,1},{5,7},{7,5},{8,10},{10,8},{12,... | collective-permute-start | bytes 3145736 | tf_op jit(solution)/shard_map/ppermute | solution.py:49
  222.2 71.3 %collective-permute-start.17 = (bf16[256,2048]{1,0:T(8,128)(2,1)}, bf16[256,2048]{1,0:T(8,128)(2,1)}, u32[]{:S(2)}, u32[]{:S(2)}) collective-permute-start(bf16[256,2048]{1,0:T(8,128)(2,1)} %get-tuple-element.54), channel_id=1, source_target_pairs={{0,4},{2,6},{4,0},{6,2},{1,5},{3,7},{5,1},{7,3},{8,12},{10,14},{12... | collective-permute-start | bytes 3145736 | tf_op jit(solution)/shard_map/ppermute | solution.py:49
  224.0 69.6 %collective-permute-start.18 = (bf16[256,2048]{1,0:T(8,128)(2,1)}, bf16[256,2048]{1,0:T(8,128)(2,1)}, u32[]{:S(2)}, u32[]{:S(2)}) collective-permute-start(bf16[256,2048]{1,0:T(8,128)(2,1)} %get-tuple-element.55), channel_id=1, source_target_pairs={{0,6},{2,4},{4,2},{6,0},{1,7},{3,5},{5,3},{7,1},{8,14},{10,12},{12... | collective-permute-start | bytes 3145736 | tf_op jit(solution)/shard_map/ppermute | solution.py:49
  225.7 369.7 %reduce-scatter.12.cloned.1.call-start = ((), (), s32[]{:S(2)}) async-start(), calls=%async_computation.11 | async-start | bytes 2621440 | tf_op jit(solution)/shard_map/reduce_scatter | solution.py:151
  236.6 80.8 %collective-permute-start.24 = (bf16[256,2048]{1,0:T(8,128)(2,1)S(1)}, bf16[256,2048]{1,0:T(8,128)(2,1)S(1)}, u32[]{:S(2)}, u32[]{:S(2)}) collective-permute-start(bf16[256,2048]{1,0:T(8,128)(2,1)S(1)} %constant_dynamic-slice_fusion.9), channel_id=1, source_target_pairs={{0,6},{2,4},{4,2},{6,0},{1,7},{3,5},{5,3},{7,1},{8,14},{10,12},{12... | collective-permute-start | bytes 3145736 | tf_op jit(solution)/shard_map/ppermute | solution.py:49
  239.1 78.1 %collective-permute-start.23 = (bf16[256,2048]{1,0:T(8,128)(2,1)S(1)}, bf16[256,2048]{1,0:T(8,128)(2,1)S(1)}, u32[]{:S(2)}, u32[]{:S(2)}) collective-permute-start(bf16[256,2048]{1,0:T(8,128)(2,1)S(1)} %constant_dynamic-slice_fusion.9), channel_id=1, source_target_pairs={{0,4},{2,6},{4,0},{6,2},{1,5},{3,7},{5,1},{7,3},{8,12},{10,14},{12... | collective-permute-start | bytes 3145736 | tf_op jit(solution)/shard_map/ppermute | solution.py:49
  247.2 67.4 %collective-permute-start.22 = (bf16[256,2048]{1,0:T(8,128)(2,1)S(1)}, bf16[256,2048]{1,0:T(8,128)(2,1)S(1)}, u32[]{:S(2)}, u32[]{:S(2)}) collective-permute-start(bf16[256,2048]{1,0:T(8,128)(2,1)S(1)} %constant_dynamic-slice_fusion.9), channel_id=1, source_target_pairs={{0,2},{2,0},{4,6},{6,4},{1,3},{3,1},{5,7},{7,5},{8,10},{10,8},{12,... | collective-permute-start | bytes 3145736 | tf_op jit(solution)/shard_map/ppermute | solution.py:49
  297.8 39.3 %collective-permute-start.19 = (bf16[256,2048]{1,0:T(8,128)(2,1)S(1)}, bf16[256,2048]{1,0:T(8,128)(2,1)S(1)}, u32[]{:S(2)}, u32[]{:S(2)}) collective-permute-start(bf16[256,2048]{1,0:T(8,128)(2,1)S(1)} %multiply_convert_fusion), channel_id=1, source_target_pairs={{0,2},{2,0},{4,6},{6,4},{1,3},{3,1},{5,7},{7,5},{8,10},{10,8},{12,... | collective-permute-start | bytes 3145736 | tf_op jit(solution)/shard_map/ppermute | solution.py:49
  298.0 61.7 %collective-permute-start.20 = (bf16[256,2048]{1,0:T(8,128)(2,1)S(1)}, bf16[256,2048]{1,0:T(8,128)(2,1)S(1)}, u32[]{:S(2)}, u32[]{:S(2)}) collective-permute-start(bf16[256,2048]{1,0:T(8,128)(2,1)S(1)} %multiply_convert_fusion), channel_id=1, source_target_pairs={{0,4},{2,6},{4,0},{6,2},{1,5},{3,7},{5,1},{7,3},{8,12},{10,14},{12... | collective-permute-start | bytes 3145736 | tf_op jit(solution)/shard_map/ppermute | solution.py:49
  314.6 46.2 %collective-permute-start.21 = (bf16[256,2048]{1,0:T(8,128)(2,1)S(1)}, bf16[256,2048]{1,0:T(8,128)(2,1)S(1)}, u32[]{:S(2)}, u32[]{:S(2)}) collective-permute-start(bf16[256,2048]{1,0:T(8,128)(2,1)S(1)} %multiply_convert_fusion), channel_id=1, source_target_pairs={{0,6},{2,4},{4,2},{6,0},{1,7},{3,5},{5,3},{7,1},{8,14},{10,12},{12... | collective-permute-start | bytes 3145736 | tf_op jit(solution)/shard_map/ppermute | solution.py:49
  317.4 44.5 %collective-permute-start.26 = (bf16[1024,2048]{1,0:T(8,128)(2,1)S(1)}, bf16[1024,2048]{1,0:T(8,128)(2,1)}, u32[]{:S(2)}, u32[]{:S(2)}) collective-permute-start(bf16[1024,2048]{1,0:T(8,128)(2,1)S(1)} %constant_dynamic-update-slice_fusion.7), channel_id=1, source_target_pairs={{0,1},{1,0},{2,3},{3,2},{4,5},{5,4},{6,7},{7,6},{8,9},{9,8},{10,11... | collective-permute-start | bytes 12582920 | tf_op jit(solution)/shard_map/ppermute | solution.py:49
  361.9 7.5 collective-permute-start.25
  383.2 11.1 %collective-permute-start.27 = (bf16[1024,2048]{1,0:T(8,128)(2,1)}, bf16[1024,2048]{1,0:T(8,128)(2,1)}, u32[]{:S(2)}, u32[]{:S(2)}) collective-permute-start(bf16[1024,2048]{1,0:T(8,128)(2,1)} %convolution_convert_fusion.2), channel_id=1, source_target_pairs={{0,1},{1,0},{2,3},{3,2},{4,5},{5,4},{6,7},{7,6},{8,9},{9,8},{10,11... | collective-permute-start | bytes 12582920 | tf_op jit(solution)/shard_map/ppermute | solution.py:49
  400.8 26.2 %collective-permute-start.28 = (bf16[256,2048]{1,0:T(8,128)(2,1)}, bf16[256,2048]{1,0:T(8,128)(2,1)S(1)}, u32[]{:S(2)}, u32[]{:S(2)}) collective-permute-start(bf16[256,2048]{1,0:T(8,128)(2,1)} %get-tuple-element.62), channel_id=1, source_target_pairs={{0,2},{2,0},{4,6},{6,4},{1,3},{3,1},{5,7},{7,5},{8,10},{10,8},{12,... | collective-permute-start | bytes 3145736 | tf_op jit(solution)/shard_map/ppermute | solution.py:49
  401.1 47.2 %collective-permute-start.29 = (bf16[256,2048]{1,0:T(8,128)(2,1)}, bf16[256,2048]{1,0:T(8,128)(2,1)}, u32[]{:S(2)}, u32[]{:S(2)}) collective-permute-start(bf16[256,2048]{1,0:T(8,128)(2,1)} %get-tuple-element.63), channel_id=1, source_target_pairs={{0,4},{2,6},{4,0},{6,2},{1,5},{3,7},{5,1},{7,3},{8,12},{10,14},{12... | collective-permute-start | bytes 3145736 | tf_op jit(solution)/shard_map/ppermute | solution.py:49
  402.8 47.3 %collective-permute-start.30 = (bf16[256,2048]{1,0:T(8,128)(2,1)}, bf16[256,2048]{1,0:T(8,128)(2,1)}, u32[]{:S(2)}, u32[]{:S(2)}) collective-permute-start(bf16[256,2048]{1,0:T(8,128)(2,1)} %get-tuple-element.64), channel_id=1, source_target_pairs={{0,6},{2,4},{4,2},{6,0},{1,7},{3,5},{5,3},{7,1},{8,14},{10,12},{12... | collective-permute-start | bytes 3145736 | tf_op jit(solution)/shard_map/ppermute | solution.py:49
  415.2 181.4 %reduce-scatter.14.cloned.1.call-start = ((), (), s32[]{:S(2)}) async-start(), calls=%async_computation.12 | async-start | bytes 2621440 | tf_op jit(solution)/shard_map/reduce_scatter | solution.py:151
  455.7 26.0 %collective-permute-start.31 = (bf16[256,2048]{1,0:T(8,128)(2,1)S(1)}, bf16[256,2048]{1,0:T(8,128)(2,1)S(1)}, u32[]{:S(2)}, u32[]{:S(2)}) collective-permute-start(bf16[256,2048]{1,0:T(8,128)(2,1)S(1)} %get-tuple-element.110), channel_id=1, source_target_pairs={{0,2},{2,0},{4,6},{6,4},{1,3},{3,1},{5,7},{7,5},{8,10},{10,8},{12,... | collective-permute-start | bytes 3145736 | tf_op jit(solution)/shard_map/ppermute | solution.py:49
  456.3 46.6 %collective-permute-start.32 = (bf16[256,2048]{1,0:T(8,128)(2,1)S(1)}, bf16[256,2048]{1,0:T(8,128)(2,1)S(1)}, u32[]{:S(2)}, u32[]{:S(2)}) collective-permute-start(bf16[256,2048]{1,0:T(8,128)(2,1)S(1)} %get-tuple-element.110), channel_id=1, source_target_pairs={{0,4},{2,6},{4,0},{6,2},{1,5},{3,7},{5,1},{7,3},{8,12},{10,14},{12... | collective-permute-start | bytes 3145736 | tf_op jit(solution)/shard_map/ppermute | solution.py:49
  458.0 46.0 %collective-permute-start.33 = (bf16[256,2048]{1,0:T(8,128)(2,1)S(1)}, bf16[256,2048]{1,0:T(8,128)(2,1)S(1)}, u32[]{:S(2)}, u32[]{:S(2)}) collective-permute-start(bf16[256,2048]{1,0:T(8,128)(2,1)S(1)} %get-tuple-element.110), channel_id=1, source_target_pairs={{0,6},{2,4},{4,2},{6,0},{1,7},{3,5},{5,3},{7,1},{8,14},{10,12},{12... | collective-permute-start | bytes 3145736 | tf_op jit(solution)/shard_map/ppermute | solution.py:49
  505.1 8.5 %collective-permute-start.34 = (bf16[1024,2048]{1,0:T(8,128)(2,1)}, bf16[1024,2048]{1,0:T(8,128)(2,1)}, u32[]{:S(2)}, u32[]{:S(2)}) collective-permute-start(bf16[1024,2048]{1,0:T(8,128)(2,1)} %constant_dynamic-update-slice_fusion.4.grad_ref), channel_id=1, source_target_pairs={{0,1},{1,0},{2,3},{3,2},{4,5},{5,4},{6,7},{7,6},{8,9},{9,8},{10,11... | collective-permute-start | bytes 12582920 | tf_op jit(solution)/shard_map/ppermute | solution.py:49
  513.5 105.1 %reduce-scatter.8.cloned.1.call-start = ((), (), s32[]{:S(2)}) async-start(), calls=%async_computation.9 | async-start | bytes 2621440 | tf_op jit(solution)/shard_map/reduce_scatter | solution.py:151
  524.5 134.6 %reduce-scatter.10.cloned.1.call-start = ((), (), s32[]{:S(2)}) async-start(), calls=%async_computation.10 | async-start | bytes 2621440 | tf_op jit(solution)/shard_map/reduce_scatter | solution.py:151
  546.0 22.2 %collective-permute-start.40 = (bf16[256,512]{1,0:T(8,128)(2,1)}, bf16[256,512]{1,0:T(8,128)(2,1)S(1)}, u32[]{:S(2)}, u32[]{:S(2)}) collective-permute-start(bf16[256,512]{1,0:T(8,128)(2,1)} %convolution_add_fusion), channel_id=1, source_target_pairs={{8,0},{16,8},{24,16},{9,1},{17,9},{25,17},{10,2},{18,10},{26,18},{... | collective-permute-start | bytes 786440 | tf_op jit(solution)/shard_map/ppermute | solution.py:55
  551.9 111.0 %collective-permute-start.35 = (bf16[1024,2048]{1,0:T(8,128)(2,1)}, bf16[1024,2048]{1,0:T(8,128)(2,1)}, u32[]{:S(2)}, u32[]{:S(2)}) collective-permute-start(bf16[1024,2048]{1,0:T(8,128)(2,1)} %convolution_convert_fusion.1), channel_id=1, source_target_pairs={{0,1},{1,0},{2,3},{3,2},{4,5},{5,4},{6,7},{7,6},{8,9},{9,8},{10,11... | collective-permute-start | bytes 12582920 | tf_op jit(solution)/shard_map/ppermute | solution.py:49
  563.2 237.0 %reduce-scatter.6.cloned.1.call-start = ((), (), s32[]{:S(2)}) async-start(), calls=%async_computation.8 | async-start | bytes 5242880 | tf_op jit(solution)/shard_map/reduce_scatter | solution.py:151
  594.7 77.8 %collective-permute-start.41 = (bf16[1024,2048]{1,0:T(8,128)(2,1)}, bf16[1024,2048]{1,0:T(8,128)(2,1)}, u32[]{:S(2)}, u32[]{:S(2)}) collective-permute-start(bf16[1024,2048]{1,0:T(8,128)(2,1)} %convolution_convert_fusion), channel_id=1, source_target_pairs={{0,1},{1,0},{2,3},{3,2},{4,5},{5,4},{6,7},{7,6},{8,9},{9,8},{10,11... | collective-permute-start | bytes 12582920 | tf_op jit(solution)/shard_map/ppermute | solution.py:49
  598.6 72.7 %collective-permute-start.61 = (bf16[128,1024]{1,0:T(8,128)(2,1)}, bf16[128,1024]{1,0:T(8,128)(2,1)S(1)}, u32[]{:S(2)}, u32[]{:S(2)}) collective-permute-start(bf16[128,1024]{1,0:T(8,128)(2,1)} %get-tuple-element.160), channel_id=1, source_target_pairs={{0,2},{2,0},{4,6},{6,4},{1,3},{3,1},{5,7},{7,5},{8,10},{10,8},{12,... | collective-permute-start | bytes 786440 | tf_op jit(solution)/shard_map/ppermute | solution.py:49
  599.9 85.1 %collective-permute-start.60 = (bf16[128,1024]{1,0:T(8,128)(2,1)}, bf16[128,1024]{1,0:T(8,128)(2,1)}, u32[]{:S(2)}, u32[]{:S(2)}) collective-permute-start(bf16[128,1024]{1,0:T(8,128)(2,1)} %get-tuple-element.161), channel_id=1, source_target_pairs={{0,4},{2,6},{4,0},{6,2},{1,5},{3,7},{5,1},{7,3},{8,12},{10,14},{12... | collective-permute-start | bytes 786440 | tf_op jit(solution)/shard_map/ppermute | solution.py:49
  601.5 85.5 %collective-permute-start.59 = (bf16[128,1024]{1,0:T(8,128)(2,1)}, bf16[128,1024]{1,0:T(8,128)(2,1)}, u32[]{:S(2)}, u32[]{:S(2)}) collective-permute-start(bf16[128,1024]{1,0:T(8,128)(2,1)} %get-tuple-element.162), channel_id=1, source_target_pairs={{0,6},{2,4},{4,2},{6,0},{1,7},{3,5},{5,3},{7,1},{8,14},{10,12},{12... | collective-permute-start | bytes 786440 | tf_op jit(solution)/shard_map/ppermute | solution.py:49
  662.9 25.2 %collective-permute-start.58 = (bf16[128,1024]{1,0:T(8,128)(2,1)}, bf16[128,1024]{1,0:T(8,128)(2,1)}, u32[]{:S(2)}, u32[]{:S(2)}) collective-permute-start(bf16[128,1024]{1,0:T(8,128)(2,1)} %get-tuple-element.166), channel_id=1, source_target_pairs={{0,2},{2,0},{4,6},{6,4},{1,3},{3,1},{5,7},{7,5},{8,10},{10,8},{12,... | collective-permute-start | bytes 786440 | tf_op jit(solution)/shard_map/ppermute | solution.py:49
  671.3 17.3 %collective-permute-start.57 = (bf16[128,1024]{1,0:T(8,128)(2,1)}, bf16[128,1024]{1,0:T(8,128)(2,1)}, u32[]{:S(2)}, u32[]{:S(2)}) collective-permute-start(bf16[128,1024]{1,0:T(8,128)(2,1)} %get-tuple-element.167), channel_id=1, source_target_pairs={{0,4},{2,6},{4,0},{6,2},{1,5},{3,7},{5,1},{7,3},{8,12},{10,14},{12... | collective-permute-start | bytes 786440 | tf_op jit(solution)/shard_map/ppermute | solution.py:49
  672.5 16.1 %collective-permute-start.56 = (bf16[128,1024]{1,0:T(8,128)(2,1)}, bf16[128,1024]{1,0:T(8,128)(2,1)}, u32[]{:S(2)}, u32[]{:S(2)}) collective-permute-start(bf16[128,1024]{1,0:T(8,128)(2,1)} %get-tuple-element.168), channel_id=1, source_target_pairs={{0,6},{2,4},{4,2},{6,0},{1,7},{3,5},{5,3},{7,1},{8,14},{10,12},{12... | collective-permute-start | bytes 786440 | tf_op jit(solution)/shard_map/ppermute | solution.py:49
  685.0 96.5 %collective-permute-start.36 = (bf16[256,2048]{1,0:T(8,128)(2,1)}, bf16[256,2048]{1,0:T(8,128)(2,1)}, u32[]{:S(2)}, u32[]{:S(2)}) collective-permute-start(bf16[256,2048]{1,0:T(8,128)(2,1)} %get-tuple-element.71), channel_id=1, source_target_pairs={{0,2},{2,0},{4,6},{6,4},{1,3},{3,1},{5,7},{7,5},{8,10},{10,8},{12,... | collective-permute-start | bytes 3145736 | tf_op jit(solution)/shard_map/ppermute | solution.py:49
  687.0 94.5 %collective-permute-start.37 = (bf16[256,2048]{1,0:T(8,128)(2,1)}, bf16[256,2048]{1,0:T(8,128)(2,1)}, u32[]{:S(2)}, u32[]{:S(2)}) collective-permute-start(bf16[256,2048]{1,0:T(8,128)(2,1)} %get-tuple-element.72), channel_id=1, source_target_pairs={{0,4},{2,6},{4,0},{6,2},{1,5},{3,7},{5,1},{7,3},{8,12},{10,14},{12... | collective-permute-start | bytes 3145736 | tf_op jit(solution)/shard_map/ppermute | solution.py:49
  688.1 45.8 %collective-permute-start.42 = (bf16[256,2048]{1,0:T(8,128)(2,1)}, bf16[256,2048]{1,0:T(8,128)(2,1)}, u32[]{:S(2)}, u32[]{:S(2)}) collective-permute-start(bf16[256,2048]{1,0:T(8,128)(2,1)} %get-tuple-element.80), channel_id=1, source_target_pairs={{0,2},{2,0},{4,6},{6,4},{1,3},{3,1},{5,7},{7,5},{8,10},{10,8},{12,... | collective-permute-start | bytes 3145736 | tf_op jit(solution)/shard_map/ppermute | solution.py:49
  692.0 85.6 %collective-permute-start.43 = (bf16[256,2048]{1,0:T(8,128)(2,1)}, bf16[256,2048]{1,0:T(8,128)(2,1)}, u32[]{:S(2)}, u32[]{:S(2)}) collective-permute-start(bf16[256,2048]{1,0:T(8,128)(2,1)} %get-tuple-element.81), channel_id=1, source_target_pairs={{0,4},{2,6},{4,0},{6,2},{1,5},{3,7},{5,1},{7,3},{8,12},{10,14},{12... | collective-permute-start | bytes 3145736 | tf_op jit(solution)/shard_map/ppermute | solution.py:49
  692.5 85.1 %collective-permute-start.44 = (bf16[256,2048]{1,0:T(8,128)(2,1)}, bf16[256,2048]{1,0:T(8,128)(2,1)}, u32[]{:S(2)}, u32[]{:S(2)}) collective-permute-start(bf16[256,2048]{1,0:T(8,128)(2,1)} %get-tuple-element.82), channel_id=1, source_target_pairs={{0,6},{2,4},{4,2},{6,0},{1,7},{3,5},{5,3},{7,1},{8,14},{10,12},{12... | collective-permute-start | bytes 3145736 | tf_op jit(solution)/shard_map/ppermute | solution.py:49
  733.9 47.6 %collective-permute-start.38 = (bf16[256,2048]{1,0:T(8,128)(2,1)}, bf16[256,2048]{1,0:T(8,128)(2,1)}, u32[]{:S(2)}, u32[]{:S(2)}) collective-permute-start(bf16[256,2048]{1,0:T(8,128)(2,1)} %get-tuple-element.73), channel_id=1, source_target_pairs={{0,6},{2,4},{4,2},{6,0},{1,7},{3,5},{5,3},{7,1},{8,14},{10,12},{12... | collective-permute-start | bytes 3145736 | tf_op jit(solution)/shard_map/ppermute | solution.py:49
  784.3 14.0 %collective-permute-start.39 = (bf16[256,2048]{1,0:T(8,128)(2,1)S(1)}, bf16[256,2048]{1,0:T(8,128)(2,1)S(1)}, u32[]{:S(2)}, u32[]{:S(2)}) collective-permute-start(bf16[256,2048]{1,0:T(8,128)(2,1)S(1)} %add_convert_fusion.5), channel_id=1, source_target_pairs={{0,1},{1,0},{2,3},{3,2},{4,5},{5,4},{6,7},{7,6},{8,9},{9,8},{10,11... | collective-permute-start | bytes 3145736 | tf_op jit(solution)/shard_map/ppermute | solution.py:49
  791.2 5.6 collective-permute-start.52
  793.1 4.6 collective-permute-start.51
  801.4 9.2 %collective-permute-start.55 = (bf16[128,1024]{1,0:T(8,128)(2,1)S(1)}, bf16[128,1024]{1,0:T(8,128)(2,1)S(1)}, u32[]{:S(2)}, u32[]{:S(2)}) collective-permute-start(bf16[128,1024]{1,0:T(8,128)(2,1)S(1)} %get-tuple-element.163), channel_id=1, source_target_pairs={{0,2},{2,0},{4,6},{6,4},{1,3},{3,1},{5,7},{7,5},{8,10},{10,8},{12,... | collective-permute-start | bytes 786440 | tf_op jit(solution)/shard_map/ppermute | solution.py:49
  802.6 12.8 %collective-permute-start.54 = (bf16[128,1024]{1,0:T(8,128)(2,1)S(1)}, bf16[128,1024]{1,0:T(8,128)(2,1)S(1)}, u32[]{:S(2)}, u32[]{:S(2)}) collective-permute-start(bf16[128,1024]{1,0:T(8,128)(2,1)S(1)} %get-tuple-element.164), channel_id=1, source_target_pairs={{0,4},{2,6},{4,0},{6,2},{1,5},{3,7},{5,1},{7,3},{8,12},{10,14},{12... | collective-permute-start | bytes 786440 | tf_op jit(solution)/shard_map/ppermute | solution.py:49
  804.1 11.4 %collective-permute-start.53 = (bf16[128,1024]{1,0:T(8,128)(2,1)S(1)}, bf16[128,1024]{1,0:T(8,128)(2,1)S(1)}, u32[]{:S(2)}, u32[]{:S(2)}) collective-permute-start(bf16[128,1024]{1,0:T(8,128)(2,1)S(1)} %get-tuple-element.165), channel_id=1, source_target_pairs={{0,6},{2,4},{4,2},{6,0},{1,7},{3,5},{5,3},{7,1},{8,14},{10,12},{12... | collective-permute-start | bytes 786440 | tf_op jit(solution)/shard_map/ppermute | solution.py:49
  (52 other events, 418.9 us)
Sparse Core Ops, SparseCore 0:
  37.5 115.8 all-gather.3
  155.0 46.2 all-gather.5
  225.8 88.7 all-gather.7
  415.3 50.8 reduce-scatter.11
  513.7 52.8 reduce-scatter.13
  568.7 45.1 reduce-scatter.7
  616.2 42.8 reduce-scatter.9
  661.4 75.9 reduce-scatter.5

commit v2 on v1

--- a/solution.py
+++ b/solution.py
@@ -91,8 +91,11 @@
     return out
 
 
-def share(own):
+def share(own, halves=False):
     parts = [own] + [swap(own, "t", d) for d in range(1, lax.axis_size("t"))]
+    if halves:
+        half = own.shape[0] // 2
+        parts = [p[h * half : (h + 1) * half] for h in range(2) for p in parts]
     rows = join(parts)
     return [rows] + [swap(rows, "h", e) for e in range(1, lax.axis_size("h"))]
 
@@ -101,17 +104,68 @@
     return lax.optimization_barrier((values, first))[0]
 
 
-def reduce_kernel(team, rows_ref, weight_ref, *refs):
+def reduce_kernel(team, halves, rows_ref, weight_ref, *refs):
     others, outs = refs[: len(refs) - team], refs[len(refs) - team :]
-    total = dot(rows_ref[...], weight_ref[...], 1, 1)
+    rows = rows_ref[...]
+    total = dot(rows.reshape(-1, rows.shape[-1]), weight_ref[...], 1, 1)
     for other in others:
         total = total + other[...].astype(f32)
-    piece = total.shape[0] // team
+    piece = total.shape[0] // (team * halves)
     for d, out in enumerate(outs):
-        out[...] = total[d * piece : (d + 1) * piece].astype(out.dtype)
-
-
-def reduce(rows, weight, column, stack=None):
+        for h in range(halves):
+            at = (h * team + d) * piece
+            out[h * piece : (h + 1) * piece] = total[at : at + piece].astype(out.dtype)
+
+
+def other_kernel(rows_ref, weight_ref, out_ref):
+    rows = rows_ref[...]
+    out_ref[...] = dot(rows.reshape(-1, rows.shape[-1]), weight_ref[...], 1, 1).astype(bf16)
+
+
+def reduce_half(rows, half, h, weight, column, first=None):
+    team, cores = lax.axis_size("t"), len(rows)
+    width = weight.shape[0]
+    step = min(1024, width)
+
+    def spec(value):
+        depth = value.shape[-1]
+        full = value.shape[0] != team * half
+        value = value.reshape(team, -1, depth)
+        return value, pl.BlockSpec((team, half, depth), lambda i: (0, h if full else 0, 0))
+
+    def call(kernel, e, others, shapes):
+        value, own = spec(rows[e])
+        depth = value.shape[-1]
+        return pl.pallas_call(
+            kernel,
+            grid=(width // step,),
+            in_specs=[own, pl.BlockSpec((step, depth), lambda i: (i, column))]
+            + [pl.BlockSpec((count, step), lambda i: (0, i)) for _ in others],
+            out_specs=[pl.BlockSpec((s.shape[0], step), lambda i: (0, i)) for s in shapes],
+            out_shape=shapes,
+            cost_estimate=pl.CostEstimate(
+                flops=2 * count * depth * width,
+                bytes_accessed=2 * width * (depth + count),
+                transcendentals=0,
+            ),
+        )(value, weight, *others)
+
+    count = team * half
+    shape = [jax.ShapeDtypeStruct((count, width), bf16)]
+    mine = [call(other_kernel, e, [], shape)[0] for e in range(1, cores)]
+    others = [swap(v, "h", e) for e, v in enumerate(mine, 1)]
+    shapes = [jax.ShapeDtypeStruct((count // team, width), bf16 if d else f32) for d in range(team)]
+    out = call(partial(reduce_kernel, team, 1), 0, others, shapes)
+    got = [swap(out[d], "t", d) for d in range(1, team)]
+    if first is not None:
+        got = after(got, first)
+    value = out[0]
+    for v in got:
+        value = value + v.astype(f32)
+    return value, out
+
+
+def reduce(rows, weight, column, stack=None, halves=1):
     team, cores = lax.axis_size("t"), len(rows)
     count, depth = rows[0].shape
     width = weight.shape[0]
@@ -121,7 +175,7 @@
     others = [swap(v, "h", e) for e, v in enumerate(first, 1)]
     piece = count // team
     out = pl.pallas_call(
-        partial(reduce_kernel, team),
+        partial(reduce_kernel, team, halves),
         grid=(width // step,),
         in_specs=[
             pl.BlockSpec((count, depth), lambda i: (0, 0)),
@@ -143,11 +197,41 @@
     return value, out
 
 
-def grads(left, right):
-    value = dot(left[0], right[0], 0, 0)
-    for a, b in zip(left[1:], right[1:]):
-        value = value + dot(a, b, 0, 0)
-    value = value.astype(bf16)
+def grads_kernel(counts, *refs):
+    out_ref = refs[-1]
+    place = column = 0
+    for count in counts:
+        total = None
+        for k in range(place, place + count):
+            value = dot(refs[2 * k][...], refs[2 * k + 1][...], 0, 0)
+            total = value if total is None else total + value
+        width = total.shape[1]
+        out_ref[:, column : column + width] = total.astype(bf16)
+        place, column = place + count, column + width
+
+
+def grads(groups, rows, columns):
+    width = groups[0][0][0].shape[1]
+    step = min(512, width)
+    specs, arrays = [], []
+    for pieces in groups:
+        for left, left_at, right, right_at in pieces:
+            specs.append(pl.BlockSpec((rows, step), lambda i, at=left_at: (at, i)))
+            specs.append(pl.BlockSpec((rows, columns), lambda i, at=right_at: (at, 0)))
+            arrays += [left, right]
+    wide = columns * len(groups)
+    value = pl.pallas_call(
+        partial(grads_kernel, [len(p) for p in groups]),
+        grid=(width // step,),
+        in_specs=specs,
+        out_specs=pl.BlockSpec((step, wide), lambda i: (i, 0)),
+        out_shape=jax.ShapeDtypeStruct((width, wide), bf16),
+        cost_estimate=pl.CostEstimate(
+            flops=rows * len(arrays) * width * columns,
+            bytes_accessed=rows * len(arrays) * (width + columns),
+            transcendentals=0,
+        ),
+    )(*arrays)
     return lax.psum_scatter(value, "g", scatter_dimension=0, tiled=True)
 
 
@@ -168,7 +252,7 @@
         grad_out[at] = (grad_ref[at] * (cumulative + value * density)).astype(bf16)
 
 
-def unit_step(hidden, weight, grad, units):
+def unit_step(hidden, weight, grad, units, h):
     rows, width = hidden.shape
     size = min(256, rows)
     own = lambda i: (i, 0)
@@ -179,7 +263,7 @@
         in_specs=[
             pl.BlockSpec((size, width), own),
             pl.BlockSpec((width, units), lambda i: (0, 0)),
-            pl.BlockSpec((size, units), own),
+            pl.BlockSpec((size, units), lambda i: (h * (rows // size) + i, 0)),
         ],
         out_specs=[pl.BlockSpec((size, units), own)] * 2,
         out_shape=[shape] * 2,
@@ -322,9 +406,13 @@
     )(*edges, *arrays)
 
 
-def gate_back_kernel(grad_ref, weight_ref, gate_ref, normed_ref, scale_ref, gate_out, mixed_out, rest_out):
-    for at in blocks_of(grad_ref):
-        grad_gated = dot(grad_ref[at], weight_ref[...])
+def gate_back_kernel(*refs):
+    grad_refs = refs[:2]
+    weight_ref, gate_ref, normed_ref, scale_ref, gate_out, mixed_out, rest_out = refs[2:]
+    half = grad_refs[0].shape[0]
+    for h in range(2):
+        at = slice(h * half, (h + 1) * half)
+        grad_gated = dot(grad_refs[h][...], weight_ref[...])
         gate = gate_ref[at]
         normed = normed_ref[at]
         sigmoid = 1.0 / (1.0 + jnp.exp(-gate))
@@ -339,19 +427,19 @@
         rest_out[at] = (grad_mixed - rounded.astype(f32)).astype(bf16)
 
 
-def gate_back(grad, weight, gate, normed, scale, e):
-    rows, width = grad.shape
-    size = min(256, rows)
-    steps = rows // size
-    own = lambda i: (i, 0)
-    far = lambda i: (e * steps + i, 0)
+def gate_back(grads, weight, gate, normed, scale, e, team):
+    rows, width = 2 * grads[0].shape[0], grads[0].shape[1]
+    size = rows // team
+    own = lambda d: (d, 0)
+    far = lambda d: (e * team + d, 0)
     shape = jax.ShapeDtypeStruct((rows, VALUE), bf16)
     return pl.pallas_call(
         gate_back_kernel,
-        grid=(steps,),
+        grid=(team,),
         in_specs=[
-            pl.BlockSpec((size, width), own),
-            pl.BlockSpec(weight.shape, lambda i: (0, 0)),
+            pl.BlockSpec((size // 2, width), own),
+            pl.BlockSpec((size // 2, width), own),
+            pl.BlockSpec(weight.shape, lambda d: (0, 0)),
             pl.BlockSpec((size, VALUE), own),
             pl.BlockSpec((size, VALUE), far),
             pl.BlockSpec((size, 1), far),
@@ -361,7 +449,7 @@
         cost_estimate=pl.CostEstimate(
             flops=2 * rows * width * VALUE, bytes_accessed=2 * rows * width, transcendentals=0
         ),
-    )(grad, weight, gate, normed, scale)
+    )(*grads, weight, gate, normed, scale)
 
 
 def shards(tokens, norm_gains, w_mixer, w_out, w_up, w_down, seg_ids, cotangent):
@@ -448,7 +536,7 @@
     rest_rows = join(deal(lambda m: lax.dynamic_index_in_dim(rest, m, 0, keepdims=False)))
     w_o = whole(rest_rows[:, :VALUE])
     w_ud = whole(rest_rows[:, VALUE:])
-    cot_all = share(after(cot, hidden[0]))
+    cot_all = share(after(cot, hidden[0]), True)
 
     qkv = [dot(h, w_mixer_all[:, : 2 * KEY + VALUE]).astype(bf16) for h in hidden]
     end_state = state_sum(
@@ -483,36 +571,73 @@
         gated.append(
             (gate[e] * jax.nn.sigmoid(gate[e]) * here(normed, e)).astype(bf16)
         )
-    stream = stream + reduce(gated, w_o, 0)[0]
-
-    hidden2_own, normed2, scaled2 = layer_norm(stream, gain_two)
-    hidden2 = share(hidden2_own.astype(bf16))
+    half = size // 2
+    both = range(2)
+
+    def of_half(value, h):
+        return value[h * half : (h + 1) * half]
+
+    gated_half = [
+        [v.reshape(team, 2, half, VALUE)[:, h].reshape(-1, VALUE) for h in both] for v in gated
+    ]
     grad_act = [dot(t, w_ud[:, units:]) for t in cot_all]
-    pairs = []
-    for e in near:
-        pairs.append(unit_step(hidden2[e], w_ud, grad_act[e], units))
-    act, grad_up = [p[0] for p in pairs], [p[1] for p in pairs]
+    own = None
+    streams, normed2, scaled2, hidden2, act, grad_up = [], [], [], [], [], []
+    for h in both:
+        added = reduce_half(gated, half, h, w_o, 0, own)[0]
+        streams.append(of_half(stream, h) + added)
+        own, n, s = layer_norm(streams[h], gain_two)
+        normed2.append(n)
+        scaled2.append(s)
+        own = own.astype(bf16)
+        hidden2.append(share(own))
+        pairs = []
+        for e in near:
+            pairs.append(unit_step(hidden2[h][e], w_ud, grad_act[e], units, h))
+        act.append([p[0] for p in pairs])
+        grad_up.append([p[1] for p in pairs])
 
     def both_cores(rows):
         rows = rows.astype(bf16)
         got = [rows] + [swap(rows, "h", e) for e in range(1, cores)]
         return join(straight(got, "h"))
 
-    grad_hidden2, sent = reduce(grad_up, w_ud, 0)
-    down_done = grads(after(cot_all, sent), act)
-    up_done = grads(after(hidden2, sent), grad_up)
-    norm_part, gain_grad_two = norm_back(grad_hidden2, normed2, scaled2, gain_two)
-    grad = cot.astype(f32) + norm_part
-    grad_all = share(grad.astype(bf16))
-    out_done = grads(grad_all, gated)
+    grad, grad_all, gain_grad_two = [], [], 0.0
+    for h in both:
+        value, sent = reduce_half(grad_up[h], half, h, w_ud, 0, own)
+        norm_part, gain_part = norm_back(value, normed2[h], scaled2[h], gain_two)
+        gain_grad_two = gain_grad_two + gain_part
+        grad.append(of_half(cot, h).astype(f32) + norm_part)
+        own = grad[h].astype(bf16)
+        grad_all.append(share(own))
+    cot_late, hidden_late = after((cot_all, hidden2), sent)
+    halves = [(e, h) for e in near for h in both]
+    part = team * half
+    units_done = grads(
+        [
+            [(hidden_late[h][e], 0, grad_up[h][e], 0) for e, h in halves],
+            [(cot_late[e], h, act[h][e], 0) for e, h in halves],
+        ],
+        part,
+        units,
+    )
     backs = []
     for e in near:
-        backs.append(gate_back(grad_all[e], w_o, gate[e], normed, scale, e))
+        grad_here = [grad_all[h][e] for h in both]
+        backs.append(gate_back(grad_here, w_o, gate[e], normed, scale, e, team))
     grad_gate, grad_mixed, mixed_rest = ([v[i] for v in backs] for i in range(3))
-    gate_done = grads(hidden, grad_gate)
+    heads_done = grads(
+        [
+            [(grad_all[h][e], 0, gated_half[e][h], 0) for e, h in halves],
+            [(hidden[e], h, grad_gate[e], h) for e, h in halves],
+        ],
+        part,
+        VALUE,
+    )
     grad_before = state_sum([v[:, :KEY] for v in qkv], from_start, grad_mixed)
     grad_in = passed(grad_before, -1)
-    added = reduce(after(act, grad_before), w_ud, 1)[0]
+    act_rows = [jnp.concatenate([act[h][e] for h in both], axis=0) for e in near]
+    added = reduce(after(act_rows, grad_before), w_ud, 1, halves=2)[0]
     (proj,) = walk(
         backward_kernel,
         cores,
@@ -537,18 +662,19 @@
         chunks * size * 12000,
     )
     grad_proj = [here(proj, e) for e in near]
-    qkv_done = grads(hidden, [v[:, : 2 * KEY + VALUE] for v in grad_proj])
+    qkv_done = grads([[(hidden[e], 0, proj, e) for e in near]], rows, 2 * KEY + VALUE)
     grad_hidden = reduce(grad_proj, w_mixer_all, 0, proj)[0]
-    output = both_cores(stream + added)
+    output = both_cores(jnp.concatenate(streams, axis=0) + added)
     norm_part, gain_grad_one = norm_back(grad_hidden, normed1, scaled1, gain_one)
-    input_grad = both_cores(grad + norm_part)
+    input_grad = both_cores(jnp.concatenate(grad, axis=0) + norm_part)
     gain_grad = total(jnp.stack([gain_grad_one, gain_grad_two]))
 
     def own_rows(done):
         return deal(lambda m: lax.dynamic_slice_in_dim(done, m * rows_here, rows_here, 0))
 
-    own_units = own_rows(jnp.concatenate([up_done, down_done], axis=1))
-    own_heads = own_rows(jnp.concatenate([out_done, gate_done], axis=1))
+    own_units = own_rows(units_done)
+    own_heads = own_rows(heads_done)
+    own_heads = after(own_heads, gain_grad_one)
     own_qkv = own_rows(qkv_done)
     mixer_grad = jnp.concatenate(
         [

time: 836 us -> 741 us (0.89)
  waiting for transfers between devices: 402 us -> 283 us
  Pallas kernels: 87.7 us -> 156 us
  matrix products: 126 us -> 62.9 us
    ppermute x59 -> x75, waiting for transfers between devices: 337 us -> 274 us  [swap(): return lax.ppermute(value, axis, [(i, i ^ d) for i in range(count)])]
    dot_general x24 -> x12, matrix products: 126 us -> 62.9 us  [dot(): lax.dot_general(a, b, (((left,), (right,)), ((), ())), preferred_element_...]
    pallas_call x6 -> x15, Pallas kernels: 47.9 us -> 111 us  [the longest x3 42.9 us: grads(): pl.pallas_call(partial(grads_kernel, [len(p) for p in groups]), grid=(wid...]
    reduce_scatter x5 -> x3, waiting for transfers between devices: 38.6 us -> 0.06 us  [grads(): return lax.psum_scatter(value, 'g', scatter_dimension=0, tiled=True)]
    ppermute x59 -> x75, starting transfers between devices: 64.4 us -> 82 us  [swap(): return lax.ppermute(value, axis, [(i, i ^ d) for i in range(count)])]
    dynamic_update_slice x18 -> x30, local copies, waits for them, and re-layouts: 22.5 us -> 38.6 us  [join(): out = lax.dynamic_update_slice_in_dim(out, part, i * rows, 0)]
    reduce_scatter x5 -> x3, starting transfers between devices: 11.8 us -> 0.34 us  [grads(): return lax.psum_scatter(value, 'g', scatter_dimension=0, tiled=True)]
    all_gather x1, waiting for transfers between devices: 19.1 us -> 7.78 us  [shards(): w_mixer_all = whole(mixer_rows)]
  transfers between devices with their start and end apart: 70 -> 84, of which waited for: 32 -> 43; matrix products, arithmetic and copies ran while one was open for 24% -> 22% of each run, Pallas kernels for 8% -> 21%
where the time goes in v2:
time: 741 us; the launch traced here: 732 us
  waiting for transfers between devices  283 us (38%)
  Pallas kernels  156 us (21%)
  starting transfers between devices  89.8 us (12%)
  local copies, waits for them, and re-layouts  74.9 us (10%)
  matrix products  62.9 us (8%)
  other arithmetic  43.7 us (6%)
  between operations  21.4 us (3%)
    ppermute x75, waiting for transfers between devices, swap(): return lax.ppermute(value, axis, [(i, i ^ d) for i in range(count)])  274 us
    ppermute x75, starting transfers between devices, swap(): return lax.ppermute(value, axis, [(i, i ^ d) for i in range(count)])  82 us
    dot_general x12, matrix products, dot(): lax.dot_general(a, b, (((left,), (right,)), ((), ())), preferred_element_...  62.9 us
    pallas_call x3, Pallas kernels, grads(): pl.pallas_call(partial(grads_kernel, [len(p) for p in groups]), grid=(wid...  42.9 us
    dynamic_update_slice x30, local copies, waits for them, and re-layouts, join(): out = lax.dynamic_update_slice_in_dim(out, part, i * rows, 0)  38.6 us
    pallas_call x8, Pallas kernels, call(): pl.pallas_call(kernel, grid=(width // step,), in_specs=[own, pl.BlockSpec...  33.2 us
    pallas_call x2, Pallas kernels, walk(): pl.pallas_call(partial(kernel, cores, team), grid_spec=pltpu.PrefetchScal...  26.4 us
    pallas_call x4, Pallas kernels, unit_step(): pl.pallas_call(unit_kernel, grid=(rows // size,), in_specs=[pl.BlockSpec(...  19 us
  transfers between devices with their start and end apart: 84, of which 43 were waited for; matrix products, arithmetic and copies ran while one was open for 22% of the time, Pallas kernels for 21%

profile of v2, /device:TPU:0, one launch (start us, length us, event | category | flops | bytes accessed | tf_op | source)
XLA Modules:
  0.0 732.2 jit_solution(1318245817251293456)
XLA Ops:
  7.2 6.5 constant_dynamic-slice_fusion.10
  13.8 4.0 collective-permute-start
  18.6 9.2 %collective-permute-done = bf16[128,1536]{1,0:T(8,128)(2,1)S(1)} collective-permute-done((bf16[128,1536]{1,0:T(8,128)(2,1)S(1)}, bf16[128,1536]{1,0:T(8,128)(2,1)S(1)}, u32[]{:S(2)}, u32[]{:S(2)}) %collective-permute-start) | collective-permute-done | bytes 393248 | tf_op jit(solution)/shard_map/ppermute | solution.py:49
  27.8 7.5 %collective-permute-done.1 = bf16[128,1536]{1,0:T(8,128)(2,1)S(1)} collective-permute-done((bf16[128,1536]{1,0:T(8,128)(2,1)S(1)}, bf16[128,1536]{1,0:T(8,128)(2,1)S(1)}, u32[]{:S(2)}, u32[]{:S(2)}) %collective-permute-start.1) | collective-permute-done | bytes 393248 | tf_op jit(solution)/shard_map/ppermute | solution.py:49
  49.0 6.8 collective-permute-done.12
  57.4 5.6 collective-permute-done.13
  69.5 17.3 %collective-permute-done.3 = bf16[256,2048]{1,0:T(8,128)(2,1)} collective-permute-done((bf16[256,2048]{1,0:T(8,128)(2,1)S(1)}, bf16[256,2048]{1,0:T(8,128)(2,1)}, u32[]{:S(2)}, u32[]{:S(2)}) %collective-permute-start.3) | collective-permute-done | bytes 1048608 | tf_op jit(solution)/shard_map/ppermute | solution.py:49
  91.5 16.6 %collective-permute-done.5 = bf16[256,2048]{1,0:T(8,128)(2,1)} collective-permute-done((bf16[256,2048]{1,0:T(8,128)(2,1)S(1)}, bf16[256,2048]{1,0:T(8,128)(2,1)}, u32[]{:S(2)}, u32[]{:S(2)}) %collective-permute-start.5) | collective-permute-done | bytes 1048608 | tf_op jit(solution)/shard_map/ppermute | solution.py:49
  128.5 4.8 collective-permute-start.11
  145.8 7.8 %all-gather.4.cloned.1.call-done.weight_ref = bf16[2048,1536]{1,0:T(8,128)(2,1)} async-done(((bf16[512,1536]{1,0:T(8,128)(2,1)}), bf16[2048,1536]{1,0:T(8,128)(2,1)}) %all-gather.4.cloned.1.call-update) | async-done | bytes 6291472 | tf_op jit(solution)/shard_map/all_gather | solution.py:477
  153.6 8.1 %fusion.7.refs_0_ = bf16[1024,1024]{1,0:T(8,128)(2,1)S(1)} fusion(bf16[1024,2048]{1,0:T(8,128)(2,1)} %constant_dynamic-update-slice_fusion.12.refs_0_.refs_8_.refs_10_, bf16[2048,1536]{1,0:T(8,128)(2,1)} %all-gather.4.cloned.1.call-done.weight_ref), kind=kOutput, calls=%fused_computation.21 | convolution fusion | flops 4296015872 | bytes 10485760 | tf_op jit(solution)/shard_map/dot_general | solution.py:30
  162.5 6.9 fusion.10.refs_1_
  171.5 4.6 fusion.13.refs_3_
  176.1 6.6 fusion.15.refs_3_
  184.3 10.9 %shard_map.144 = (f32[2048,512]{1,0:T(8,128)}, f32[2048,1]{1,0:T(8,128)}, bf16[8,256,512]{2,1,0:T(8,128)(2,1)}) custom-call(s32[8]{0:T(128)} %fusion.37.order, s32[8]{0:T(128)} %get-tuple-element.165.firsts, s32[8]{0:T(128)} %get-tuple-element.164.lasts, s32[1]{0:T(128)} %bitcast.24.before_group, f32[2]{0:T(128)} %broadcast_multiply_fusion.9.floats, ...), custom_call_target="tpu_custom_call" | custom-call | flops 1879048192 | bytes 8388608 | tf_op jit(solution)/shard_map/pallas_call | solution.py:395
  195.3 5.6 multiply_convert_fusion
  201.5 3.9 shard_map.145
  207.2 3.9 shard_map.147
  218.5 4.2 shard_map.146
  228.1 4.3 shard_map.148
  233.8 3.9 collective-permute-done.16
  239.0 10.2 %collective-permute-done.17 = bf16[128,2048]{1,0:T(8,128)(2,1)S(1)} collective-permute-done((bf16[128,2048]{1,0:T(8,128)(2,1)}, bf16[128,2048]{1,0:T(8,128)(2,1)S(1)}, u32[]{:S(2)}, u32[]{:S(2)}) %collective-permute-start.17) | collective-permute-done | bytes 524320 | tf_op jit(solution)/shard_map/ppermute | solution.py:49
  253.0 7.2 collective-permute-done.20
  260.2 11.4 %collective-permute-done.21 = bf16[128,2048]{1,0:T(8,128)(2,1)S(1)} collective-permute-done((bf16[128,2048]{1,0:T(8,128)(2,1)}, bf16[128,2048]{1,0:T(8,128)(2,1)S(1)}, u32[]{:S(2)}, u32[]{:S(2)}) %collective-permute-start.21) | collective-permute-done | bytes 524320 | tf_op jit(solution)/shard_map/ppermute | solution.py:49
  280.4 7.0 collective-permute-done.29
  289.8 10.1 %collective-permute-done.30 = bf16[128,2048]{1,0:T(8,128)(2,1)S(1)} collective-permute-done((bf16[128,2048]{1,0:T(8,128)(2,1)S(1)}, bf16[128,2048]{1,0:T(8,128)(2,1)S(1)}, u32[]{:S(2)}, u32[]{:S(2)}) %collective-permute-start.30) | collective-permute-done | bytes 524320 | tf_op jit(solution)/shard_map/ppermute | solution.py:49
  301.5 8.4 %collective-permute-done.23 = bf16[128,2048]{1,0:T(8,128)(2,1)S(1)} collective-permute-done((bf16[128,2048]{1,0:T(8,128)(2,1)S(1)}, bf16[128,2048]{1,0:T(8,128)(2,1)S(1)}, u32[]{:S(2)}, u32[]{:S(2)}) %collective-permute-start.23) | collective-permute-done | bytes 524320 | tf_op jit(solution)/shard_map/ppermute | solution.py:49
  310.7 9.7 %collective-permute-done.24 = bf16[128,2048]{1,0:T(8,128)(2,1)S(1)} collective-permute-done((bf16[128,2048]{1,0:T(8,128)(2,1)S(1)}, bf16[128,2048]{1,0:T(8,128)(2,1)S(1)}, u32[]{:S(2)}, u32[]{:S(2)}) %collective-permute-start.24) | collective-permute-done | bytes 524320 | tf_op jit(solution)/shard_map/ppermute | solution.py:49
  322.1 6.5 fusion.18.grad_ref
  328.6 4.7 shard_map.152
  333.4 3.9 shard_map.155
  337.8 4.8 shard_map.151
  342.5 4.0 shard_map.153
  346.6 6.5 fusion.20.grad_ref
  353.1 4.7 shard_map.150
  357.8 4.7 shard_map.149
  362.5 4.5 shard_map.156
  367.0 4.5 shard_map.154
  375.0 14.6 %shard_map.164 = bf16[2048,1024]{1,0:T(8,128)(2,1)} custom-call(bf16[512,2048]{1,0:T(8,128)(2,1)} %constant_dynamic-update-slice_fusion.9.hidden_ref.refs_0_, bf16[512,512]{1,0:T(8,128)(2,1)} %get-tuple-element.95.refs_1_, bf16[512,2048]{1,0:T(8,128)(2,1)} %constant_dynamic-update-slice_fusion.6.hidden_ref.refs_2_, ...), custom_call_target="tpu_custom_call" | custom-call | flops 8589934592 | bytes 20971520 | tf_op jit(solution)/shard_map/pallas_call | solution.py:223
  393.3 4.5 collective-permute-done.37
  400.7 8.3 %collective-permute-done.43 = bf16[128,2048]{1,0:T(8,128)(2,1)S(1)} collective-permute-done((bf16[128,2048]{1,0:T(8,128)(2,1)}, bf16[128,2048]{1,0:T(8,128)(2,1)S(1)}, u32[]{:S(2)}, u32[]{:S(2)}) %collective-permute-start.43) | collective-permute-done | bytes 524320 | tf_op jit(solution)/shard_map/ppermute | solution.py:49
  409.0 11.0 %collective-permute-done.44 = bf16[128,2048]{1,0:T(8,128)(2,1)S(1)} collective-permute-done((bf16[128,2048]{1,0:T(8,128)(2,1)}, bf16[128,2048]{1,0:T(8,128)(2,1)S(1)}, u32[]{:S(2)}, u32[]{:S(2)}) %collective-permute-start.44) | collective-permute-done | bytes 524320 | tf_op jit(solution)/shard_map/ppermute | solution.py:49
  430.8 6.2 collective-permute-done.46
  439.3 10.4 %collective-permute-done.47 = bf16[128,2048]{1,0:T(8,128)(2,1)S(1)} collective-permute-done((bf16[128,2048]{1,0:T(8,128)(2,1)S(1)}, bf16[128,2048]{1,0:T(8,128)(2,1)S(1)}, u32[]{:S(2)}, u32[]{:S(2)}) %collective-permute-start.47) | collective-permute-done | bytes 524320 | tf_op jit(solution)/shard_map/ppermute | solution.py:49
  451.4 8.1 %collective-permute-done.39 = bf16[128,2048]{1,0:T(8,128)(2,1)S(1)} collective-permute-done((bf16[128,2048]{1,0:T(8,128)(2,1)S(1)}, bf16[128,2048]{1,0:T(8,128)(2,1)S(1)}, u32[]{:S(2)}, u32[]{:S(2)}) %collective-permute-start.39) | collective-permute-done | bytes 524320 | tf_op jit(solution)/shard_map/ppermute | solution.py:49
  460.4 10.0 %collective-permute-done.40 = bf16[128,2048]{1,0:T(8,128)(2,1)S(1)} collective-permute-done((bf16[128,2048]{1,0:T(8,128)(2,1)S(1)}, bf16[128,2048]{1,0:T(8,128)(2,1)S(1)}, u32[]{:S(2)}, u32[]{:S(2)}) %collective-permute-start.40) | collective-permute-done | bytes 524320 | tf_op jit(solution)/shard_map/ppermute | solution.py:49
  476.4 8.4 %shard_map.157 = (bf16[1024,512]{1,0:T(8,128)(2,1)}, bf16[1024,512]{1,0:T(8,128)(2,1)}, bf16[1024,512]{1,0:T(8,128)(2,1)}) custom-call(bf16[512,2048]{1,0:T(8,128)(2,1)} %constant_dynamic-update-slice_fusion.3.refs_0_, bf16[512,2048]{1,0:T(8,128)(2,1)} %constant_dynamic-update-slice_fusion.refs_1_.refs_2_, ...), custom_call_target="tpu_custom_call" | custom-call | flops 2147483648 | bytes 4194304 | tf_op jit(solution)/shard_map/pallas_call | solution.py:436
  484.8 8.1 %shard_map.158 = (bf16[1024,512]{1,0:T(8,128)(2,1)}, bf16[1024,512]{1,0:T(8,128)(2,1)}, bf16[1024,512]{1,0:T(8,128)(2,1)}) custom-call(bf16[512,2048]{1,0:T(8,128)(2,1)} %collective-permute-done.49.refs_0_.refs_4_, bf16[512,2048]{1,0:T(8,128)(2,1)} %collective-permute-done.50.refs_1_.refs_6_, ...), custom_call_target="tpu_custom_call" | custom-call | flops 2147483648 | bytes 4194304 | tf_op jit(solution)/shard_map/pallas_call | solution.py:436
  498.9 14.6 %shard_map.163 = bf16[2048,1024]{1,0:T(8,128)(2,1)} custom-call(bf16[512,2048]{1,0:T(8,128)(2,1)} %constant_dynamic-update-slice_fusion.3.refs_0_, bf16[512,512]{1,0:T(8,128)(2,1)} %bitcast.181, bf16[512,2048]{1,0:T(8,128)(2,1)} %constant_dynamic-update-slice_fusion.refs_1_.refs_2_, bf16[512,512]{1,0:T(8,128)(2,1)} %bitcast.180, ...), custom_call_target="tpu_custom_call" | custom-call | flops 8589934592 | bytes 20971520 | tf_op jit(solution)/shard_map/pallas_call | solution.py:223
  513.6 6.2 convolution_convert_fusion.1
  521.0 15.5 %shard_map.160.rows_ref.refs_1_.refs_3_ = bf16[2048,1536]{1,0:T(8,128)(2,1)} custom-call(s32[8]{0:T(128)} %fusion.37.order, s32[8]{0:T(128)} %get-tuple-element.165.firsts, s32[8]{0:T(128)} %get-tuple-element.164.lasts, s32[1]{0:T(128)} %bitcast.24.before_group, f32[2]{0:T(128)} %broadcast_multiply_fusion.9.floats, bf16[1024,1024]{1,0:T(8,128)(2,1)} %copy-done.39, ...), custom_call_target="tpu_custom_call" | custom-call | flops 5637144576 | bytes 24576000 | tf_op jit(solution)/shard_map/pallas_call | solution.py:395
  536.5 11.2 %convolution_convert_fusion = bf16[1024,2048]{1,0:T(8,128)(2,1)} fusion(bf16[2048,1536]{1,0:T(8,128)(2,1)} %all-gather.4.cloned.1.call-done.weight_ref, bf16[2048,1536]{1,0:T(8,128)(2,1)} %shard_map.160.rows_ref.refs_1_.refs_3_), kind=kOutput, calls=%fused_computation | convolution fusion | flops 6444548096 | bytes 13631488 | tf_op jit(solution)/shard_map/dot_general | solution.py:30
  547.7 6.6 shard_map.159
  557.8 11.7 %shard_map.161 = (f32[256,2048]{1,0:T(8,128)}, bf16[256,2048]{1,0:T(8,128)(2,1)}, bf16[256,2048]{1,0:T(8,128)(2,1)}, bf16[256,2048]{1,0:T(8,128)(2,1)}) custom-call(bf16[2048,1536]{1,0:T(8,128)(2,1)} %shard_map.160.rows_ref.refs_1_.refs_3_, bf16[2048,1536]{1,0:T(8,128)(2,1)} %all-gather.4.cloned.1.call-done.weight_ref, ...), custom_call_target="tpu_custom_call" | custom-call | flops 6442450944 | bytes 14680064 | tf_op jit(solution)/shard_map/pallas_call | solution.py:177
  571.9 8.7 %collective-permute-done.52 = bf16[256,2048]{1,0:T(8,128)(2,1)} collective-permute-done((bf16[256,2048]{1,0:T(8,128)(2,1)}, bf16[256,2048]{1,0:T(8,128)(2,1)}, u32[]{:S(2)}, u32[]{:S(2)}) %collective-permute-start.52) | collective-permute-done | bytes 1048608 | tf_op jit(solution)/shard_map/ppermute | solution.py:49
  582.5 13.7 %shard_map.162 = bf16[2048,1024]{1,0:T(8,128)(2,1)} custom-call(bf16[1024,2048]{1,0:T(8,128)(2,1)} %constant_dynamic-update-slice_fusion.12.refs_0_.refs_8_.refs_10_, bf16[2048,1536]{1,0:T(8,128)(2,1)} %shard_map.160.rows_ref.refs_1_.refs_3_, bf16[1024,2048]{1,0:T(8,128)(2,1)} %collective-permute-done.6.refs_2_.refs_12_.refs_14_, ...), custom_call_target="tpu_custom_call" | custom-call | flops 8589934592 | bytes 12582912 | tf_op jit(solution)/shard_map/pallas_call | solution.py:223
  597.4 6.3 collective-permute-done.53
  606.6 4.4 fusion.5
  611.0 14.6 %collective-permute-done.58 = bf16[256,2048]{1,0:T(8,128)(2,1)} collective-permute-done((bf16[256,2048]{1,0:T(8,128)(2,1)}, bf16[256,2048]{1,0:T(8,128)(2,1)}, u32[]{:S(2)}, u32[]{:S(2)}) %collective-permute-start.58) | collective-permute-done | bytes 1048608 | tf_op jit(solution)/shard_map/ppermute | solution.py:49
  626.2 28.0 %collective-permute-done.59 = bf16[256,2048]{1,0:T(8,128)(2,1)} collective-permute-done((bf16[256,2048]{1,0:T(8,128)(2,1)}, bf16[256,2048]{1,0:T(8,128)(2,1)}, u32[]{:S(2)}, u32[]{:S(2)}) %collective-permute-start.59) | collective-permute-done | bytes 1048608 | tf_op jit(solution)/shard_map/ppermute | solution.py:49
  668.1 7.6 %collective-permute-start.66 = (f32[2,2048]{1,0:T(2,128)S(1)}, f32[2,2048]{1,0:T(2,128)S(1)}, u32[]{:S(2)}, u32[]{:S(2)}) collective-permute-start(f32[2,2048]{1,0:T(2,128)S(1)} %add_add_fusion), channel_id=1, source_target_pairs={{0,8},{8,0},{16,24},{24,16},{1,9},{9,1},{17,25},{25,17},{2,10},{10... | collective-permute-start | bytes 49160 | tf_op jit(solution)/shard_map/ppermute | solution.py:49
  694.9 4.5 collective-permute-done.72
  710.4 5.3 collective-permute-done.69
  721.2 3.7 copy.41
  (361 shorter events, 197.0 us)
Async XLA Ops:
  7.2 146.4 %all-gather.4.cloned.1.call-start = ((), (), s32[]{:S(2)}) async-start(), calls=%async_computation.3 | async-start | bytes 7864320 | tf_op jit(solution)/shard_map/all_gather | solution.py:477
  13.8 14.0 %collective-permute-start = (bf16[128,1536]{1,0:T(8,128)(2,1)S(1)}, bf16[128,1536]{1,0:T(8,128)(2,1)S(1)}, u32[]{:S(2)}, u32[]{:S(2)}) collective-permute-start(bf16[128,1536]{1,0:T(8,128)(2,1)S(1)} %bitcast.199), channel_id=1, source_target_pairs={{0,6},{2,4},{4,2},{6,0},{1,7},{3,5},{5,3},{7,1},{8,14},{10,12},{12... | collective-permute-start | bytes 1179656 | tf_op jit(solution)/shard_map/ppermute | solution.py:49
  17.8 17.5 %collective-permute-start.1 = (bf16[128,1536]{1,0:T(8,128)(2,1)S(1)}, bf16[128,1536]{1,0:T(8,128)(2,1)S(1)}, u32[]{:S(2)}, u32[]{:S(2)}) collective-permute-start(bf16[128,1536]{1,0:T(8,128)(2,1)S(1)} %bitcast.200), channel_id=1, source_target_pairs={{0,4},{2,6},{4,0},{6,2},{1,5},{3,7},{5,1},{7,3},{8,12},{10,14},{12... | collective-permute-start | bytes 1179656 | tf_op jit(solution)/shard_map/ppermute | solution.py:49
  18.4 17.1 %collective-permute-start.2 = (bf16[128,1536]{1,0:T(8,128)(2,1)S(1)}, bf16[128,1536]{1,0:T(8,128)(2,1)S(1)}, u32[]{:S(2)}, u32[]{:S(2)}) collective-permute-start(bf16[128,1536]{1,0:T(8,128)(2,1)S(1)} %bitcast.201), channel_id=1, source_target_pairs={{0,2},{2,0},{4,6},{6,4},{1,3},{3,1},{5,7},{7,5},{8,10},{10,8},{12,... | collective-permute-start | bytes 1179656 | tf_op jit(solution)/shard_map/ppermute | solution.py:49
  37.5 163.9 %all-gather.6.cloned.1.call-start = ((), (), s32[]{:S(2)}) async-start(), calls=%async_computation.4 | async-start | bytes 2621440 | tf_op jit(solution)/shard_map/all_gather | solution.py:537
  42.8 13.0 %collective-permute-start.12 = (bf16[128,1536]{1,0:T(8,128)(2,1)S(1)}, bf16[128,1536]{1,0:T(8,128)(2,1)S(1)}, u32[]{:S(2)}, u32[]{:S(2)}) collective-permute-start(bf16[128,1536]{1,0:T(8,128)(2,1)S(1)} %get-tuple-element.217), channel_id=1, source_target_pairs={{0,6},{2,4},{4,2},{6,0},{1,7},{3,5},{5,3},{7,1},{8,14},{10,12},{12... | collective-permute-start | bytes 1179656 | tf_op jit(solution)/shard_map/ppermute | solution.py:49
  44.5 18.6 %collective-permute-start.13 = (bf16[128,1536]{1,0:T(8,128)(2,1)S(1)}, bf16[128,1536]{1,0:T(8,128)(2,1)S(1)}, u32[]{:S(2)}, u32[]{:S(2)}) collective-permute-start(bf16[128,1536]{1,0:T(8,128)(2,1)S(1)} %get-tuple-element.216), channel_id=1, source_target_pairs={{0,4},{2,6},{4,0},{6,2},{1,5},{3,7},{5,1},{7,3},{8,12},{10,14},{12... | collective-permute-start | bytes 1179656 | tf_op jit(solution)/shard_map/ppermute | solution.py:49
  45.8 18.4 %collective-permute-start.14 = (bf16[128,1536]{1,0:T(8,128)(2,1)S(1)}, bf16[128,1536]{1,0:T(8,128)(2,1)S(1)}, u32[]{:S(2)}, u32[]{:S(2)}) collective-permute-start(bf16[128,1536]{1,0:T(8,128)(2,1)S(1)} %get-tuple-element.215), channel_id=1, source_target_pairs={{0,2},{2,0},{4,6},{6,4},{1,3},{3,1},{5,7},{7,5},{8,10},{10,8},{12,... | collective-permute-start | bytes 1179656 | tf_op jit(solution)/shard_map/ppermute | solution.py:49
  46.8 40.0 %collective-permute-start.3 = (bf16[256,2048]{1,0:T(8,128)(2,1)S(1)}, bf16[256,2048]{1,0:T(8,128)(2,1)}, u32[]{:S(2)}, u32[]{:S(2)}) collective-permute-start(bf16[256,2048]{1,0:T(8,128)(2,1)S(1)} %multiply_convert_fusion.2), channel_id=1, source_target_pairs={{0,2},{2,0},{4,6},{6,4},{1,3},{3,1},{5,7},{7,5},{8,10},{10,8},{12,... | collective-permute-start | bytes 3145736 | tf_op jit(solution)/shard_map/ppermute | solution.py:49
  48.3 40.8 %collective-permute-start.4 = (bf16[256,2048]{1,0:T(8,128)(2,1)S(1)}, bf16[256,2048]{1,0:T(8,128)(2,1)}, u32[]{:S(2)}, u32[]{:S(2)}) collective-permute-start(bf16[256,2048]{1,0:T(8,128)(2,1)S(1)} %multiply_convert_fusion.2), channel_id=1, source_target_pairs={{0,4},{2,6},{4,0},{6,2},{1,5},{3,7},{5,1},{7,3},{8,12},{10,14},{12... | collective-permute-start | bytes 3145736 | tf_op jit(solution)/shard_map/ppermute | solution.py:49
  55.8 52.2 %collective-permute-start.5 = (bf16[256,2048]{1,0:T(8,128)(2,1)S(1)}, bf16[256,2048]{1,0:T(8,128)(2,1)}, u32[]{:S(2)}, u32[]{:S(2)}) collective-permute-start(bf16[256,2048]{1,0:T(8,128)(2,1)S(1)} %multiply_convert_fusion.2), channel_id=1, source_target_pairs={{0,6},{2,4},{4,2},{6,0},{1,7},{3,5},{5,3},{7,1},{8,14},{10,12},{12... | collective-permute-start | bytes 3145736 | tf_op jit(solution)/shard_map/ppermute | solution.py:49
  67.0 255.1 %all-gather.8.cloned.1.call-start = ((), (), s32[]{:S(2)}) async-start(), calls=%async_computation.5 | async-start | bytes 5242880 | tf_op jit(solution)/shard_map/all_gather | solution.py:538
  110.4 52.1 %collective-permute-start.6 = (bf16[1024,2048]{1,0:T(8,128)(2,1)}, bf16[1024,2048]{1,0:T(8,128)(2,1)}, u32[]{:S(2)}, u32[]{:S(2)}) collective-permute-start(bf16[1024,2048]{1,0:T(8,128)(2,1)} %constant_dynamic-update-slice_fusion.12.refs_0_.refs_8_.refs_10_), channel_id=1, source_target_pairs={{0,1},{1,0},{2,3},{3,2},{4,5},{5,4},{6,7},{7,6},{8,9},{9,8},{10,11... | collective-permute-start | bytes 12582920 | tf_op jit(solution)/shard_map/ppermute | solution.py:49
  118.8 26.1 %collective-permute-start.26 = (bf16[256,2048]{1,0:T(8,128)(2,1)S(1)}, bf16[256,2048]{1,0:T(8,128)(2,1)S(1)}, u32[]{:S(2)}, u32[]{:S(2)}) collective-permute-start(bf16[256,2048]{1,0:T(8,128)(2,1)S(1)} %constant_dynamic-slice_fusion.9), channel_id=1, source_target_pairs={{0,2},{2,0},{4,6},{6,4},{1,3},{3,1},{5,7},{7,5},{8,10},{10,8},{12,... | collective-permute-start | bytes 3145736 | tf_op jit(solution)/shard_map/ppermute | solution.py:49
  138.4 457.8 %reduce-scatter.8.cloned.1.call-start = ((), (), s32[]{:S(2)}) async-start(), calls=%async_computation.8 | async-start | bytes 5242880 | tf_op jit(solution)/shard_map/reduce_scatter | solution.py:235
  138.7 66.6 %collective-permute-start.27 = (bf16[256,2048]{1,0:T(8,128)(2,1)S(1)}, bf16[256,2048]{1,0:T(8,128)(2,1)}, u32[]{:S(2)}, u32[]{:S(2)}) collective-permute-start(bf16[256,2048]{1,0:T(8,128)(2,1)S(1)} %constant_dynamic-slice_fusion.9), channel_id=1, source_target_pairs={{0,4},{2,6},{4,0},{6,2},{1,5},{3,7},{5,1},{7,3},{8,12},{10,14},{12... | collective-permute-start | bytes 3145736 | tf_op jit(solution)/shard_map/ppermute | solution.py:49
  139.1 72.5 %collective-permute-start.28 = (bf16[256,2048]{1,0:T(8,128)(2,1)S(1)}, bf16[256,2048]{1,0:T(8,128)(2,1)}, u32[]{:S(2)}, u32[]{:S(2)}) collective-permute-start(bf16[256,2048]{1,0:T(8,128)(2,1)S(1)} %constant_dynamic-slice_fusion.9), channel_id=1, source_target_pairs={{0,6},{2,4},{4,2},{6,0},{1,7},{3,5},{5,3},{7,1},{8,14},{10,12},{12... | collective-permute-start | bytes 3145736 | tf_op jit(solution)/shard_map/ppermute | solution.py:49
  170.2 13.4 %collective-permute-start.10 = (bf16[256,512]{1,0:T(8,128)(2,1)S(1)}, bf16[256,512]{1,0:T(8,128)(2,1)S(1)}, u32[]{:S(2)}, u32[]{:S(2)}) collective-permute-start(bf16[256,512]{1,0:T(8,128)(2,1)S(1)} %fusion.22), channel_id=1, source_target_pairs={{0,8},{8,16},{16,24},{1,9},{9,17},{17,25},{2,10},{10,18},{18,26},{... | collective-permute-start | bytes 786440 | tf_op jit(solution)/shard_map/ppermute | solution.py:55
  211.1 17.0 %collective-permute-start.19 = (bf16[512,2048]{1,0:T(8,128)(2,1)}, bf16[512,2048]{1,0:T(8,128)(2,1)}, u32[]{:S(2)}, u32[]{:S(2)}) collective-permute-start(bf16[512,2048]{1,0:T(8,128)(2,1)} %shard_map.147), channel_id=1, source_target_pairs={{0,1},{1,0},{2,3},{3,2},{4,5},{5,4},{6,7},{7,6},{8,9},{9,8},{10,11... | collective-permute-start | bytes 6291464 | tf_op jit(solution)/shard_map/ppermute | solution.py:49
  222.7 15.0 %collective-permute-start.16 = (bf16[128,2048]{1,0:T(8,128)(2,1)}, bf16[128,2048]{1,0:T(8,128)(2,1)S(1)}, u32[]{:S(2)}, u32[]{:S(2)}) collective-permute-start(bf16[128,2048]{1,0:T(8,128)(2,1)} %get-tuple-element.80), channel_id=1, source_target_pairs={{0,2},{2,0},{4,6},{6,4},{1,3},{3,1},{5,7},{7,5},{8,10},{10,8},{12,... | collective-permute-start | bytes 1572872 | tf_op jit(solution)/shard_map/ppermute | solution.py:49
  224.0 25.2 %collective-permute-start.17 = (bf16[128,2048]{1,0:T(8,128)(2,1)}, bf16[128,2048]{1,0:T(8,128)(2,1)S(1)}, u32[]{:S(2)}, u32[]{:S(2)}) collective-permute-start(bf16[128,2048]{1,0:T(8,128)(2,1)} %get-tuple-element.81), channel_id=1, source_target_pairs={{0,4},{2,6},{4,0},{6,2},{1,5},{3,7},{5,1},{7,3},{8,12},{10,14},{12... | collective-permute-start | bytes 1572872 | tf_op jit(solution)/shard_map/ppermute | solution.py:49
  225.5 24.8 %collective-permute-start.18 = (bf16[128,2048]{1,0:T(8,128)(2,1)}, bf16[128,2048]{1,0:T(8,128)(2,1)}, u32[]{:S(2)}, u32[]{:S(2)}) collective-permute-start(bf16[128,2048]{1,0:T(8,128)(2,1)} %get-tuple-element.82), channel_id=1, source_target_pairs={{0,6},{2,4},{4,2},{6,0},{1,7},{3,5},{5,3},{7,1},{8,14},{10,12},{12... | collective-permute-start | bytes 1572872 | tf_op jit(solution)/shard_map/ppermute | solution.py:49
  228.1 94.0 %collective-permute-start.33 = (bf16[1024,2048]{1,0:T(8,128)(2,1)}, bf16[1024,2048]{1,0:T(8,128)(2,1)}, u32[]{:S(2)}, u32[]{:S(2)}) collective-permute-start(bf16[1024,2048]{1,0:T(8,128)(2,1)} %slice_dynamic-update-slice_fusion.refs_8_.refs_10_), channel_id=1, source_target_pairs={{0,1},{1,0},{2,3},{3,2},{4,5},{5,4},{6,7},{7,6},{8,9},{9,8},{10,11... | collective-permute-start | bytes 12582920 | tf_op jit(solution)/shard_map/ppermute | solution.py:49
  232.4 27.8 %collective-permute-start.20 = (bf16[128,2048]{1,0:T(8,128)(2,1)}, bf16[128,2048]{1,0:T(8,128)(2,1)S(1)}, u32[]{:S(2)}, u32[]{:S(2)}) collective-permute-start(bf16[128,2048]{1,0:T(8,128)(2,1)} %get-tuple-element.84), channel_id=1, source_target_pairs={{0,2},{2,0},{4,6},{6,4},{1,3},{3,1},{5,7},{7,5},{8,10},{10,8},{12,... | collective-permute-start | bytes 1572872 | tf_op jit(solution)/shard_map/ppermute | solution.py:49
  237.7 33.9 %collective-permute-start.21 = (bf16[128,2048]{1,0:T(8,128)(2,1)}, bf16[128,2048]{1,0:T(8,128)(2,1)S(1)}, u32[]{:S(2)}, u32[]{:S(2)}) collective-permute-start(bf16[128,2048]{1,0:T(8,128)(2,1)} %get-tuple-element.85), channel_id=1, source_target_pairs={{0,4},{2,6},{4,0},{6,2},{1,5},{3,7},{5,1},{7,3},{8,12},{10,14},{12... | collective-permute-start | bytes 1572872 | tf_op jit(solution)/shard_map/ppermute | solution.py:49
  249.2 22.4 %collective-permute-start.22 = (bf16[128,2048]{1,0:T(8,128)(2,1)}, bf16[128,2048]{1,0:T(8,128)(2,1)S(1)}, u32[]{:S(2)}, u32[]{:S(2)}) collective-permute-start(bf16[128,2048]{1,0:T(8,128)(2,1)} %get-tuple-element.86), channel_id=1, source_target_pairs={{0,6},{2,4},{4,2},{6,0},{1,7},{3,5},{5,3},{7,1},{8,14},{10,12},{12... | collective-permute-start | bytes 1572872 | tf_op jit(solution)/shard_map/ppermute | solution.py:49
  272.5 14.9 %collective-permute-start.29 = (bf16[128,2048]{1,0:T(8,128)(2,1)S(1)}, bf16[128,2048]{1,0:T(8,128)(2,1)S(1)}, u32[]{:S(2)}, u32[]{:S(2)}) collective-permute-start(bf16[128,2048]{1,0:T(8,128)(2,1)S(1)} %multiply_convert_fusion.5), channel_id=1, source_target_pairs={{0,2},{2,0},{4,6},{6,4},{1,3},{3,1},{5,7},{7,5},{8,10},{10,8},{12,... | collective-permute-start | bytes 1572872 | tf_op jit(solution)/shard_map/ppermute | solution.py:49
  273.8 26.0 %collective-permute-start.30 = (bf16[128,2048]{1,0:T(8,128)(2,1)S(1)}, bf16[128,2048]{1,0:T(8,128)(2,1)S(1)}, u32[]{:S(2)}, u32[]{:S(2)}) collective-permute-start(bf16[128,2048]{1,0:T(8,128)(2,1)S(1)} %multiply_convert_fusion.5), channel_id=1, source_target_pairs={{0,4},{2,6},{4,0},{6,2},{1,5},{3,7},{5,1},{7,3},{8,12},{10,14},{12... | collective-permute-start | bytes 1572872 | tf_op jit(solution)/shard_map/ppermute | solution.py:49
  274.6 26.0 %collective-permute-start.31 = (bf16[128,2048]{1,0:T(8,128)(2,1)S(1)}, bf16[128,2048]{1,0:T(8,128)(2,1)S(1)}, u32[]{:S(2)}, u32[]{:S(2)}) collective-permute-start(bf16[128,2048]{1,0:T(8,128)(2,1)S(1)} %multiply_convert_fusion.5), channel_id=1, source_target_pairs={{0,6},{2,4},{4,2},{6,0},{1,7},{3,5},{5,3},{7,1},{8,14},{10,12},{12... | collective-permute-start | bytes 1572872 | tf_op jit(solution)/shard_map/ppermute | solution.py:49
  279.2 30.7 %collective-permute-start.23 = (bf16[128,2048]{1,0:T(8,128)(2,1)S(1)}, bf16[128,2048]{1,0:T(8,128)(2,1)S(1)}, u32[]{:S(2)}, u32[]{:S(2)}) collective-permute-start(bf16[128,2048]{1,0:T(8,128)(2,1)S(1)} %multiply_convert_fusion.6), channel_id=1, source_target_pairs={{0,2},{2,0},{4,6},{6,4},{1,3},{3,1},{5,7},{7,5},{8,10},{10,8},{12,... | collective-permute-start | bytes 1572872 | tf_op jit(solution)/shard_map/ppermute | solution.py:49
  287.4 33.1 %collective-permute-start.24 = (bf16[128,2048]{1,0:T(8,128)(2,1)S(1)}, bf16[128,2048]{1,0:T(8,128)(2,1)S(1)}, u32[]{:S(2)}, u32[]{:S(2)}) collective-permute-start(bf16[128,2048]{1,0:T(8,128)(2,1)S(1)} %multiply_convert_fusion.6), channel_id=1, source_target_pairs={{0,4},{2,6},{4,0},{6,2},{1,5},{3,7},{5,1},{7,3},{8,12},{10,14},{12... | collective-permute-start | bytes 1572872 | tf_op jit(solution)/shard_map/ppermute | solution.py:49
  299.8 21.4 %collective-permute-start.25 = (bf16[128,2048]{1,0:T(8,128)(2,1)S(1)}, bf16[128,2048]{1,0:T(8,128)(2,1)S(1)}, u32[]{:S(2)}, u32[]{:S(2)}) collective-permute-start(bf16[128,2048]{1,0:T(8,128)(2,1)S(1)} %multiply_convert_fusion.6), channel_id=1, source_target_pairs={{0,6},{2,4},{4,2},{6,0},{1,7},{3,5},{5,3},{7,1},{8,14},{10,12},{12... | collective-permute-start | bytes 1572872 | tf_op jit(solution)/shard_map/ppermute | solution.py:49
  301.5 27.1 %collective-permute-start.34 = (bf16[512,2048]{1,0:T(8,128)(2,1)}, bf16[512,2048]{1,0:T(8,128)(2,1)}, u32[]{:S(2)}, u32[]{:S(2)}) collective-permute-start(bf16[512,2048]{1,0:T(8,128)(2,1)} %constant_dynamic-update-slice_fusion.6.hidden_ref.refs_2_), channel_id=1, source_target_pairs={{0,1},{1,0},{2,3},{3,2},{4,5},{5,4},{6,7},{7,6},{8,9},{9,8},{10,11... | collective-permute-start | bytes 6291464 | tf_op jit(solution)/shard_map/ppermute | solution.py:49
  322.1 15.7 %collective-permute-start.32 = (bf16[512,2048]{1,0:T(8,128)(2,1)}, bf16[512,2048]{1,0:T(8,128)(2,1)}, u32[]{:S(2)}, u32[]{:S(2)}) collective-permute-start(bf16[512,2048]{1,0:T(8,128)(2,1)} %constant_dynamic-update-slice_fusion.9.hidden_ref.refs_0_), channel_id=1, source_target_pairs={{0,1},{1,0},{2,3},{3,2},{4,5},{5,4},{6,7},{7,6},{8,9},{9,8},{10,11... | collective-permute-start | bytes 6291464 | tf_op jit(solution)/shard_map/ppermute | solution.py:49
  337.2 25.3 %collective-permute-start.42 = (bf16[512,2048]{1,0:T(8,128)(2,1)}, bf16[512,2048]{1,0:T(8,128)(2,1)}, u32[]{:S(2)}, u32[]{:S(2)}) collective-permute-start(bf16[512,2048]{1,0:T(8,128)(2,1)} %shard_map.155), channel_id=1, source_target_pairs={{0,1},{1,0},{2,3},{3,2},{4,5},{5,4},{6,7},{7,6},{8,9},{9,8},{10,11... | collective-permute-start | bytes 6291464 | tf_op jit(solution)/shard_map/ppermute | solution.py:49
  346.6 20.5 %collective-permute-start.35 = (bf16[512,2048]{1,0:T(8,128)(2,1)}, bf16[512,2048]{1,0:T(8,128)(2,1)}, u32[]{:S(2)}, u32[]{:S(2)}) collective-permute-start(bf16[512,2048]{1,0:T(8,128)(2,1)} %shard_map.153), channel_id=1, source_target_pairs={{0,1},{1,0},{2,3},{3,2},{4,5},{5,4},{6,7},{7,6},{8,9},{9,8},{10,11... | collective-permute-start | bytes 6291464 | tf_op jit(solution)/shard_map/ppermute | solution.py:49
  371.5 19.3 %collective-permute-start.36 = (bf16[128,2048]{1,0:T(8,128)(2,1)}, bf16[128,2048]{1,0:T(8,128)(2,1)}, u32[]{:S(2)}, u32[]{:S(2)}) collective-permute-start(bf16[128,2048]{1,0:T(8,128)(2,1)} %get-tuple-element.98), channel_id=1, source_target_pairs={{0,2},{2,0},{4,6},{6,4},{1,3},{3,1},{5,7},{7,5},{8,10},{10,8},{12,... | collective-permute-start | bytes 1572872 | tf_op jit(solution)/shard_map/ppermute | solution.py:49
  372.1 25.7 %collective-permute-start.37 = (bf16[128,2048]{1,0:T(8,128)(2,1)}, bf16[128,2048]{1,0:T(8,128)(2,1)}, u32[]{:S(2)}, u32[]{:S(2)}) collective-permute-start(bf16[128,2048]{1,0:T(8,128)(2,1)} %get-tuple-element.99), channel_id=1, source_target_pairs={{0,4},{2,6},{4,0},{6,2},{1,5},{3,7},{5,1},{7,3},{8,12},{10,14},{12... | collective-permute-start | bytes 1572872 | tf_op jit(solution)/shard_map/ppermute | solution.py:49
  372.5 25.4 %collective-permute-start.38 = (bf16[128,2048]{1,0:T(8,128)(2,1)}, bf16[128,2048]{1,0:T(8,128)(2,1)}, u32[]{:S(2)}, u32[]{:S(2)}) collective-permute-start(bf16[128,2048]{1,0:T(8,128)(2,1)} %get-tuple-element.100), channel_id=1, source_target_pairs={{0,6},{2,4},{4,2},{6,0},{1,7},{3,5},{5,3},{7,1},{8,14},{10,12},{12... | collective-permute-start | bytes 1572872 | tf_op jit(solution)/shard_map/ppermute | solution.py:49
  389.7 299.0 %reduce-scatter.6.cloned.1.call-start = ((), (), s32[]{:S(2)}) async-start(), calls=%async_computation.7 | async-start | bytes 5242880 | tf_op jit(solution)/shard_map/reduce_scatter | solution.py:235
  389.7 19.3 %collective-permute-start.43 = (bf16[128,2048]{1,0:T(8,128)(2,1)}, bf16[128,2048]{1,0:T(8,128)(2,1)S(1)}, u32[]{:S(2)}, u32[]{:S(2)}) collective-permute-start(bf16[128,2048]{1,0:T(8,128)(2,1)} %get-tuple-element.107), channel_id=1, source_target_pairs={{0,2},{2,0},{4,6},{6,4},{1,3},{3,1},{5,7},{7,5},{8,10},{10,8},{12,... | collective-permute-start | bytes 1572872 | tf_op jit(solution)/shard_map/ppermute | solution.py:49
  390.3 29.7 %collective-permute-start.44 = (bf16[128,2048]{1,0:T(8,128)(2,1)}, bf16[128,2048]{1,0:T(8,128)(2,1)S(1)}, u32[]{:S(2)}, u32[]{:S(2)}) collective-permute-start(bf16[128,2048]{1,0:T(8,128)(2,1)} %get-tuple-element.108), channel_id=1, source_target_pairs={{0,4},{2,6},{4,0},{6,2},{1,5},{3,7},{5,1},{7,3},{8,12},{10,14},{12... | collective-permute-start | bytes 1572872 | tf_op jit(solution)/shard_map/ppermute | solution.py:49
  390.8 29.3 %collective-permute-start.45 = (bf16[128,2048]{1,0:T(8,128)(2,1)}, bf16[128,2048]{1,0:T(8,128)(2,1)S(1)}, u32[]{:S(2)}, u32[]{:S(2)}) collective-permute-start(bf16[128,2048]{1,0:T(8,128)(2,1)} %get-tuple-element.109), channel_id=1, source_target_pairs={{0,6},{2,4},{4,2},{6,0},{1,7},{3,5},{5,3},{7,1},{8,14},{10,12},{12... | collective-permute-start | bytes 1572872 | tf_op jit(solution)/shard_map/ppermute | solution.py:49
  422.2 14.8 %collective-permute-start.46 = (bf16[128,2048]{1,0:T(8,128)(2,1)S(1)}, bf16[128,2048]{1,0:T(8,128)(2,1)S(1)}, u32[]{:S(2)}, u32[]{:S(2)}) collective-permute-start(bf16[128,2048]{1,0:T(8,128)(2,1)S(1)} %get-tuple-element.167), channel_id=1, source_target_pairs={{0,2},{2,0},{4,6},{6,4},{1,3},{3,1},{5,7},{7,5},{8,10},{10,8},{12,... | collective-permute-start | bytes 1572872 | tf_op jit(solution)/shard_map/ppermute | solution.py:49
  423.6 26.0 %collective-permute-start.47 = (bf16[128,2048]{1,0:T(8,128)(2,1)S(1)}, bf16[128,2048]{1,0:T(8,128)(2,1)S(1)}, u32[]{:S(2)}, u32[]{:S(2)}) collective-permute-start(bf16[128,2048]{1,0:T(8,128)(2,1)S(1)} %get-tuple-element.167), channel_id=1, source_target_pairs={{0,4},{2,6},{4,0},{6,2},{1,5},{3,7},{5,1},{7,3},{8,12},{10,14},{12... | collective-permute-start | bytes 1572872 | tf_op jit(solution)/shard_map/ppermute | solution.py:49
  424.2 26.3 %collective-permute-start.48 = (bf16[128,2048]{1,0:T(8,128)(2,1)S(1)}, bf16[128,2048]{1,0:T(8,128)(2,1)S(1)}, u32[]{:S(2)}, u32[]{:S(2)}) collective-permute-start(bf16[128,2048]{1,0:T(8,128)(2,1)S(1)} %get-tuple-element.167), channel_id=1, source_target_pairs={{0,6},{2,4},{4,2},{6,0},{1,7},{3,5},{5,3},{7,1},{8,14},{10,12},{12... | collective-permute-start | bytes 1572872 | tf_op jit(solution)/shard_map/ppermute | solution.py:49
  428.7 30.7 %collective-permute-start.39 = (bf16[128,2048]{1,0:T(8,128)(2,1)S(1)}, bf16[128,2048]{1,0:T(8,128)(2,1)S(1)}, u32[]{:S(2)}, u32[]{:S(2)}) collective-permute-start(bf16[128,2048]{1,0:T(8,128)(2,1)S(1)} %get-tuple-element.170), channel_id=1, source_target_pairs={{0,2},{2,0},{4,6},{6,4},{1,3},{3,1},{5,7},{7,5},{8,10},{10,8},{12,... | collective-permute-start | bytes 1572872 | tf_op jit(solution)/shard_map/ppermute | solution.py:49
  430.2 40.2 %collective-permute-start.40 = (bf16[128,2048]{1,0:T(8,128)(2,1)S(1)}, bf16[128,2048]{1,0:T(8,128)(2,1)S(1)}, u32[]{:S(2)}, u32[]{:S(2)}) collective-permute-start(bf16[128,2048]{1,0:T(8,128)(2,1)S(1)} %get-tuple-element.170), channel_id=1, source_target_pairs={{0,4},{2,6},{4,0},{6,2},{1,5},{3,7},{5,1},{7,3},{8,12},{10,14},{12... | collective-permute-start | bytes 1572872 | tf_op jit(solution)/shard_map/ppermute | solution.py:49
  437.0 34.2 %collective-permute-start.41 = (bf16[128,2048]{1,0:T(8,128)(2,1)S(1)}, bf16[128,2048]{1,0:T(8,128)(2,1)S(1)}, u32[]{:S(2)}, u32[]{:S(2)}) collective-permute-start(bf16[128,2048]{1,0:T(8,128)(2,1)S(1)} %get-tuple-element.170), channel_id=1, source_target_pairs={{0,6},{2,4},{4,2},{6,0},{1,7},{3,5},{5,3},{7,1},{8,14},{10,12},{12... | collective-permute-start | bytes 1572872 | tf_op jit(solution)/shard_map/ppermute | solution.py:49
  451.4 33.4 %collective-permute-start.50 = (bf16[512,2048]{1,0:T(8,128)(2,1)}, bf16[512,2048]{1,0:T(8,128)(2,1)}, u32[]{:S(2)}, u32[]{:S(2)}) collective-permute-start(bf16[512,2048]{1,0:T(8,128)(2,1)} %constant_dynamic-update-slice_fusion.refs_1_.refs_2_), channel_id=1, source_target_pairs={{0,1},{1,0},{2,3},{3,2},{4,5},{5,4},{6,7},{7,6},{8,9},{9,8},{10,11... | collective-permute-start | bytes 6291464 | tf_op jit(solution)/shard_map/ppermute | solution.py:49
  497.6 22.7 %collective-permute-start.56 = (bf16[256,512]{1,0:T(8,128)(2,1)}, bf16[256,512]{1,0:T(8,128)(2,1)S(1)}, u32[]{:S(2)}, u32[]{:S(2)}) collective-permute-start(bf16[256,512]{1,0:T(8,128)(2,1)} %convolution_add_fusion), channel_id=1, source_target_pairs={{8,0},{16,8},{24,16},{9,1},{17,9},{25,17},{10,2},{18,10},{26,18},{... | collective-permute-start | bytes 786440 | tf_op jit(solution)/shard_map/ppermute | solution.py:55
  513.5 190.0 %reduce-scatter.4.cloned.1.call-start = ((), (), s32[]{:S(2)}) async-start(), calls=%async_computation.6 | async-start | bytes 5242880 | tf_op jit(solution)/shard_map/reduce_scatter | solution.py:235
  519.8 27.9 %collective-permute-start.51 = (bf16[1024,2048]{1,0:T(8,128)(2,1)}, bf16[1024,2048]{1,0:T(8,128)(2,1)}, u32[]{:S(2)}, u32[]{:S(2)}) collective-permute-start(bf16[1024,2048]{1,0:T(8,128)(2,1)} %convolution_convert_fusion.1), channel_id=1, source_target_pairs={{0,1},{1,0},{2,3},{3,2},{4,5},{5,4},{6,7},{7,6},{8,9},{9,8},{10,11... | collective-permute-start | bytes 12582920 | tf_op jit(solution)/shard_map/ppermute | solution.py:49
  554.3 26.3 %collective-permute-start.52 = (bf16[256,2048]{1,0:T(8,128)(2,1)}, bf16[256,2048]{1,0:T(8,128)(2,1)}, u32[]{:S(2)}, u32[]{:S(2)}) collective-permute-start(bf16[256,2048]{1,0:T(8,128)(2,1)} %get-tuple-element.119), channel_id=1, source_target_pairs={{0,2},{2,0},{4,6},{6,4},{1,3},{3,1},{5,7},{7,5},{8,10},{10,8},{12,... | collective-permute-start | bytes 3145736 | tf_op jit(solution)/shard_map/ppermute | solution.py:49
  554.9 48.8 %collective-permute-start.53 = (bf16[256,2048]{1,0:T(8,128)(2,1)}, bf16[256,2048]{1,0:T(8,128)(2,1)}, u32[]{:S(2)}, u32[]{:S(2)}) collective-permute-start(bf16[256,2048]{1,0:T(8,128)(2,1)} %get-tuple-element.120), channel_id=1, source_target_pairs={{0,4},{2,6},{4,0},{6,2},{1,5},{3,7},{5,1},{7,3},{8,12},{10,14},{12... | collective-permute-start | bytes 3145736 | tf_op jit(solution)/shard_map/ppermute | solution.py:49
  556.7 48.5 %collective-permute-start.54 = (bf16[256,2048]{1,0:T(8,128)(2,1)}, bf16[256,2048]{1,0:T(8,128)(2,1)}, u32[]{:S(2)}, u32[]{:S(2)}) collective-permute-start(bf16[256,2048]{1,0:T(8,128)(2,1)} %get-tuple-element.121), channel_id=1, source_target_pairs={{0,6},{2,4},{4,2},{6,0},{1,7},{3,5},{5,3},{7,1},{8,14},{10,12},{12... | collective-permute-start | bytes 3145736 | tf_op jit(solution)/shard_map/ppermute | solution.py:49
  569.4 56.1 %collective-permute-start.58 = (bf16[256,2048]{1,0:T(8,128)(2,1)}, bf16[256,2048]{1,0:T(8,128)(2,1)}, u32[]{:S(2)}, u32[]{:S(2)}) collective-permute-start(bf16[256,2048]{1,0:T(8,128)(2,1)} %get-tuple-element.128), channel_id=1, source_target_pairs={{0,2},{2,0},{4,6},{6,4},{1,3},{3,1},{5,7},{7,5},{8,10},{10,8},{12,... | collective-permute-start | bytes 3145736 | tf_op jit(solution)/shard_map/ppermute | solution.py:49
  570.1 84.1 %collective-permute-start.59 = (bf16[256,2048]{1,0:T(8,128)(2,1)}, bf16[256,2048]{1,0:T(8,128)(2,1)}, u32[]{:S(2)}, u32[]{:S(2)}) collective-permute-start(bf16[256,2048]{1,0:T(8,128)(2,1)} %get-tuple-element.129), channel_id=1, source_target_pairs={{0,4},{2,6},{4,0},{6,2},{1,5},{3,7},{5,1},{7,3},{8,12},{10,14},{12... | collective-permute-start | bytes 3145736 | tf_op jit(solution)/shard_map/ppermute | solution.py:49
  580.6 73.6 %collective-permute-start.60 = (bf16[256,2048]{1,0:T(8,128)(2,1)}, bf16[256,2048]{1,0:T(8,128)(2,1)}, u32[]{:S(2)}, u32[]{:S(2)}) collective-permute-start(bf16[256,2048]{1,0:T(8,128)(2,1)} %get-tuple-element.130), channel_id=1, source_target_pairs={{0,6},{2,4},{4,2},{6,0},{1,7},{3,5},{5,3},{7,1},{8,14},{10,12},{12... | collective-permute-start | bytes 3145736 | tf_op jit(solution)/shard_map/ppermute | solution.py:49
  603.7 54.4 %collective-permute-start.75 = (bf16[128,1024]{1,0:T(8,128)(2,1)S(1)}, bf16[128,1024]{1,0:T(8,128)(2,1)S(1)}, u32[]{:S(2)}, u32[]{:S(2)}) collective-permute-start(bf16[128,1024]{1,0:T(8,128)(2,1)S(1)} %get-tuple-element.224), channel_id=1, source_target_pairs={{0,6},{2,4},{4,2},{6,0},{1,7},{3,5},{5,3},{7,1},{8,14},{10,12},{12... | collective-permute-start | bytes 786440 | tf_op jit(solution)/shard_map/ppermute | solution.py:49
  605.2 53.8 %collective-permute-start.76 = (bf16[128,1024]{1,0:T(8,128)(2,1)S(1)}, bf16[128,1024]{1,0:T(8,128)(2,1)S(1)}, u32[]{:S(2)}, u32[]{:S(2)}) collective-permute-start(bf16[128,1024]{1,0:T(8,128)(2,1)S(1)} %get-tuple-element.223), channel_id=1, source_target_pairs={{0,4},{2,6},{4,0},{6,2},{1,5},{3,7},{5,1},{7,3},{8,12},{10,14},{12... | collective-permute-start | bytes 786440 | tf_op jit(solution)/shard_map/ppermute | solution.py:49
  625.6 33.4 %collective-permute-start.77 = (bf16[128,1024]{1,0:T(8,128)(2,1)S(1)}, bf16[128,1024]{1,0:T(8,128)(2,1)S(1)}, u32[]{:S(2)}, u32[]{:S(2)}) collective-permute-start(bf16[128,1024]{1,0:T(8,128)(2,1)S(1)} %get-tuple-element.222), channel_id=1, source_target_pairs={{0,2},{2,0},{4,6},{6,4},{1,3},{3,1},{5,7},{7,5},{8,10},{10,8},{12,... | collective-permute-start | bytes 786440 | tf_op jit(solution)/shard_map/ppermute | solution.py:49
  654.3 31.0 %collective-permute-start.55 = (bf16[256,2048]{1,0:T(8,128)(2,1)}, bf16[256,2048]{1,0:T(8,128)(2,1)}, u32[]{:S(2)}, u32[]{:S(2)}) collective-permute-start(bf16[256,2048]{1,0:T(8,128)(2,1)} %fusion.5), channel_id=1, source_target_pairs={{0,1},{1,0},{2,3},{3,2},{4,5},{5,4},{6,7},{7,6},{8,9},{9,8},{10,11... | collective-permute-start | bytes 3145736 | tf_op jit(solution)/shard_map/ppermute | solution.py:49
  668.1 13.4 %collective-permute-start.66 = (f32[2,2048]{1,0:T(2,128)S(1)}, f32[2,2048]{1,0:T(2,128)S(1)}, u32[]{:S(2)}, u32[]{:S(2)}) collective-permute-start(f32[2,2048]{1,0:T(2,128)S(1)} %add_add_fusion), channel_id=1, source_target_pairs={{0,8},{8,0},{16,24},{24,16},{1,9},{9,1},{17,25},{25,17},{2,10},{10... | collective-permute-start | bytes 49160 | tf_op jit(solution)/shard_map/ppermute | solution.py:49
  (61 other events, 695.1 us)
Sparse Core Ops, SparseCore 0:
  37.6 115.8 all-gather.3
  155.1 46.2 all-gather.5
  203.0 82.6 all-gather.7
  389.8 83.4 reduce-scatter.7
  513.6 84.8 reduce-scatter.5
  600.7 80.2 reduce-scatter.3

commit v3 on v2

--- a/solution.py
+++ b/solution.py
@@ -91,8 +91,21 @@
     return out
 
 
-def share(own, halves=False):
-    parts = [own] + [swap(own, "t", d) for d in range(1, lax.axis_size("t"))]
+def share(own, halves=False, relay=False):
+    team = lax.axis_size("t")
+    relay = relay and team == 4
+    parts = [own] + [swap(own, "t", d) for d in range(1, 3 if relay else team)]
+    if relay:
+        half = own.shape[1] // 2
+        left = swap(parts[1][:, :half], "t", 2)
+        right = swap(parts[2][:, half:], "t", 1)
+        count = own.shape[0]
+        rows = jnp.zeros((team * count, own.shape[1]), own.dtype)
+        for d, part in enumerate(parts):
+            rows = lax.dynamic_update_slice(rows, part, (d * count, 0))
+        rows = lax.dynamic_update_slice(rows, left, (3 * count, 0))
+        rows = lax.dynamic_update_slice(rows, right, (3 * count, half))
+        return [rows] + [swap(rows, "h", e) for e in range(1, lax.axis_size("h"))]
     if halves:
         half = own.shape[0] // 2
         parts = [p[h * half : (h + 1) * half] for h in range(2) for p in parts]
@@ -535,7 +548,8 @@
     rest = after(rest, mixer_rows)
     rest_rows = join(deal(lambda m: lax.dynamic_index_in_dim(rest, m, 0, keepdims=False)))
     w_o = whole(rest_rows[:, :VALUE])
-    w_ud = whole(rest_rows[:, VALUE:])
+    w_d = whole(rest_rows[:, VALUE + units :])
+    w_u = whole(rest_rows[:, VALUE : VALUE + units])
     cot_all = share(after(cot, hidden[0]), True)
 
     qkv = [dot(h, w_mixer_all[:, : 2 * KEY + VALUE]).astype(bf16) for h in hidden]
@@ -580,7 +594,7 @@
     gated_half = [
         [v.reshape(team, 2, half, VALUE)[:, h].reshape(-1, VALUE) for h in both] for v in gated
     ]
-    grad_act = [dot(t, w_ud[:, units:]) for t in cot_all]
+    grad_act = [dot(t, w_d) for t in cot_all]
     own = None
     streams, normed2, scaled2, hidden2, act, grad_up = [], [], [], [], [], []
     for h in both:
@@ -593,7 +607,7 @@
         hidden2.append(share(own))
         pairs = []
         for e in near:
-            pairs.append(unit_step(hidden2[h][e], w_ud, grad_act[e], units, h))
+            pairs.append(unit_step(hidden2[h][e], w_u, grad_act[e], units, h))
         act.append([p[0] for p in pairs])
         grad_up.append([p[1] for p in pairs])
 
@@ -604,12 +618,12 @@
 
     grad, grad_all, gain_grad_two = [], [], 0.0
     for h in both:
-        value, sent = reduce_half(grad_up[h], half, h, w_ud, 0, own)
+        value, sent = reduce_half(grad_up[h], half, h, w_u, 0, own)
         norm_part, gain_part = norm_back(value, normed2[h], scaled2[h], gain_two)
         gain_grad_two = gain_grad_two + gain_part
         grad.append(of_half(cot, h).astype(f32) + norm_part)
         own = grad[h].astype(bf16)
-        grad_all.append(share(own))
+        grad_all.append(share(own, relay=True))
     cot_late, hidden_late = after((cot_all, hidden2), sent)
     halves = [(e, h) for e in near for h in both]
     part = team * half
@@ -637,7 +651,7 @@
     grad_before = state_sum([v[:, :KEY] for v in qkv], from_start, grad_mixed)
     grad_in = passed(grad_before, -1)
     act_rows = [jnp.concatenate([act[h][e] for h in both], axis=0) for e in near]
-    added = reduce(after(act_rows, grad_before), w_ud, 1, halves=2)[0]
+    added = reduce(after(act_rows, grad_before), w_d, 0, halves=2)[0]
     (proj,) = walk(
         backward_kernel,
         cores,

time: 741 us -> 774 us (1.045)
  waiting for transfers between devices: 283 us -> 322 us
    ppermute x3, waiting for transfers between devices: 0.93 us -> 21.6 us  [shift(): return lax.ppermute(value, 'g', pairs)]
    ppermute x75 -> x77, waiting for transfers between devices: 274 us -> 292 us  [swap(): return lax.ppermute(value, axis, [(i, i ^ d) for i in range(count)])]
    dynamic_update_slice x0 -> x10, local copies, waits for them, and re-layouts: none -> 9.43 us  [the longest x6 6.46 us: share(): rows = lax.dynamic_update_slice(rows, part, (d * count, 0))]
    dynamic_update_slice x30 -> x22, local copies, waits for them, and re-layouts: 38.6 us -> 31.4 us  [join(): out = lax.dynamic_update_slice_in_dim(out, part, i * rows, 0)]
    ppermute x75 -> x77, starting transfers between devices: 82 us -> 80.1 us  [swap(): return lax.ppermute(value, axis, [(i, i ^ d) for i in range(count)])]
  transfers between devices with their start and end apart: 84 -> 87, of which waited for: 43 -> 45; matrix products, arithmetic and copies ran while one was open for 22% -> 21% of each run, Pallas kernels for 21% -> 20%
where the time goes in v3:
time: 774 us; the launch traced here: 765 us
  waiting for transfers between devices  322 us (42%)
  Pallas kernels  154 us (20%)
  starting transfers between devices  89.1 us (12%)
  local copies, waits for them, and re-layouts  75.5 us (10%)
  matrix products  60 us (8%)
  other arithmetic  42.7 us (6%)
  between operations  21.6 us (3%)
    ppermute x77, waiting for transfers between devices, swap(): return lax.ppermute(value, axis, [(i, i ^ d) for i in range(count)])  292 us
    ppermute x77, starting transfers between devices, swap(): return lax.ppermute(value, axis, [(i, i ^ d) for i in range(count)])  80.1 us
    dot_general x12, matrix products, dot(): lax.dot_general(a, b, (((left,), (right,)), ((), ())), preferred_element_...  60 us
    pallas_call x3, Pallas kernels, grads(): pl.pallas_call(partial(grads_kernel, [len(p) for p in groups]), grid=(wid...  42.7 us
    pallas_call x8, Pallas kernels, call(): pl.pallas_call(kernel, grid=(width // step,), in_specs=[own, pl.BlockSpec...  33.3 us
    dynamic_update_slice x22, local copies, waits for them, and re-layouts, join(): out = lax.dynamic_update_slice_in_dim(out, part, i * rows, 0)  31.4 us
    pallas_call x2, Pallas kernels, walk(): pl.pallas_call(partial(kernel, cores, team), grid_spec=pltpu.PrefetchScal...  25.1 us
    ppermute x3, waiting for transfers between devices, shift(): return lax.ppermute(value, 'g', pairs)  21.6 us
  transfers between devices with their start and end apart: 87, of which 45 were waited for; matrix products, arithmetic and copies ran while one was open for 21% of the time, Pallas kernels for 20%

profile of v3, /device:TPU:0, one launch (start us, length us, event | category | flops | bytes accessed | tf_op | source)
XLA Modules:
  0.0 765.4 jit_solution(11565287452655090342)
XLA Ops:
  7.2 6.3 constant_dynamic-slice_fusion.10
  13.6 4.0 collective-permute-start
  18.4 9.2 %collective-permute-done = bf16[128,1536]{1,0:T(8,128)(2,1)S(1)} collective-permute-done((bf16[128,1536]{1,0:T(8,128)(2,1)S(1)}, bf16[128,1536]{1,0:T(8,128)(2,1)S(1)}, u32[]{:S(2)}, u32[]{:S(2)}) %collective-permute-start) | collective-permute-done | bytes 393248 | tf_op jit(solution)/shard_map/ppermute | solution.py:49
  27.6 7.5 collective-permute-done.1
  48.8 6.8 collective-permute-done.12
  57.2 5.6 collective-permute-done.13
  68.6 18.0 %collective-permute-done.3 = bf16[256,2048]{1,0:T(8,128)(2,1)} collective-permute-done((bf16[256,2048]{1,0:T(8,128)(2,1)S(1)}, bf16[256,2048]{1,0:T(8,128)(2,1)}, u32[]{:S(2)}, u32[]{:S(2)}) %collective-permute-start.3) | collective-permute-done | bytes 1048608 | tf_op jit(solution)/shard_map/ppermute | solution.py:49
  91.2 16.6 %collective-permute-done.5 = bf16[256,2048]{1,0:T(8,128)(2,1)} collective-permute-done((bf16[256,2048]{1,0:T(8,128)(2,1)S(1)}, bf16[256,2048]{1,0:T(8,128)(2,1)}, u32[]{:S(2)}, u32[]{:S(2)}) %collective-permute-start.5) | collective-permute-done | bytes 1048608 | tf_op jit(solution)/shard_map/ppermute | solution.py:49
  128.4 4.8 collective-permute-start.11
  140.8 3.8 collective-permute-done.26
  145.5 7.8 %all-gather.5.cloned.1.call-done.weight_ref = bf16[2048,1536]{1,0:T(8,128)(2,1)} async-done(((bf16[512,1536]{1,0:T(8,128)(2,1)}), bf16[2048,1536]{1,0:T(8,128)(2,1)}) %all-gather.5.cloned.1.call-update) | async-done | bytes 6291472 | tf_op jit(solution)/shard_map/all_gather | solution.py:490
  153.4 8.1 %fusion.7.refs_0_ = bf16[1024,1024]{1,0:T(8,128)(2,1)S(1)} fusion(bf16[1024,2048]{1,0:T(8,128)(2,1)} %constant_dynamic-update-slice_fusion.12.refs_0_.refs_8_.refs_10_, bf16[2048,1536]{1,0:T(8,128)(2,1)} %all-gather.5.cloned.1.call-done.weight_ref), kind=kOutput, calls=%fused_computation.21 | convolution fusion | flops 4296015872 | bytes 10485760 | tf_op jit(solution)/shard_map/dot_general | solution.py:30
  162.3 6.9 fusion.10.refs_1_
  171.6 4.6 fusion.13.refs_3_
  176.2 6.6 fusion.15.refs_3_
  184.1 10.6 %shard_map.144 = (f32[2048,512]{1,0:T(8,128)}, f32[2048,1]{1,0:T(8,128)}, bf16[8,256,512]{2,1,0:T(8,128)(2,1)}) custom-call(s32[8]{0:T(128)} %fusion.32.order, s32[8]{0:T(128)} %get-tuple-element.165.firsts, s32[8]{0:T(128)} %get-tuple-element.164.lasts, s32[1]{0:T(128)} %bitcast.24.before_group, f32[2]{0:T(128)} %broadcast_multiply_fusion.9.floats, ...), custom_call_target="tpu_custom_call" | custom-call | flops 1879048192 | bytes 8388608 | tf_op jit(solution)/shard_map/pallas_call | solution.py:408
  194.7 5.6 multiply_convert_fusion
  201.3 3.9 shard_map.145
  207.1 3.9 shard_map.147
  218.3 4.2 shard_map.146
  227.9 4.4 shard_map.148
  233.6 3.9 collective-permute-done.16
  238.8 10.1 %collective-permute-done.17 = bf16[128,2048]{1,0:T(8,128)(2,1)S(1)} collective-permute-done((bf16[128,2048]{1,0:T(8,128)(2,1)}, bf16[128,2048]{1,0:T(8,128)(2,1)S(1)}, u32[]{:S(2)}, u32[]{:S(2)}) %collective-permute-start.17) | collective-permute-done | bytes 524320 | tf_op jit(solution)/shard_map/ppermute | solution.py:49
  252.8 7.2 collective-permute-done.20
  260.0 11.3 %collective-permute-done.21 = bf16[128,2048]{1,0:T(8,128)(2,1)S(1)} collective-permute-done((bf16[128,2048]{1,0:T(8,128)(2,1)}, bf16[128,2048]{1,0:T(8,128)(2,1)S(1)}, u32[]{:S(2)}, u32[]{:S(2)}) %collective-permute-start.21) | collective-permute-done | bytes 524320 | tf_op jit(solution)/shard_map/ppermute | solution.py:49
  279.2 8.0 %collective-permute-done.29 = bf16[128,2048]{1,0:T(8,128)(2,1)} collective-permute-done((bf16[128,2048]{1,0:T(8,128)(2,1)S(1)}, bf16[128,2048]{1,0:T(8,128)(2,1)}, u32[]{:S(2)}, u32[]{:S(2)}) %collective-permute-start.29) | collective-permute-done | bytes 524320 | tf_op jit(solution)/shard_map/ppermute | solution.py:49
  290.7 9.6 %collective-permute-done.30 = bf16[128,2048]{1,0:T(8,128)(2,1)S(1)} collective-permute-done((bf16[128,2048]{1,0:T(8,128)(2,1)S(1)}, bf16[128,2048]{1,0:T(8,128)(2,1)S(1)}, u32[]{:S(2)}, u32[]{:S(2)}) %collective-permute-start.30) | collective-permute-done | bytes 524320 | tf_op jit(solution)/shard_map/ppermute | solution.py:49
  303.5 6.2 collective-permute-done.23
  310.5 10.2 %collective-permute-done.24 = bf16[128,2048]{1,0:T(8,128)(2,1)S(1)} collective-permute-done((bf16[128,2048]{1,0:T(8,128)(2,1)S(1)}, bf16[128,2048]{1,0:T(8,128)(2,1)S(1)}, u32[]{:S(2)}, u32[]{:S(2)}) %collective-permute-start.24) | collective-permute-done | bytes 524320 | tf_op jit(solution)/shard_map/ppermute | solution.py:49
  322.4 6.5 fusion.54.grad_ref
  328.8 4.8 shard_map.152
  333.6 3.9 shard_map.155
  338.0 4.7 shard_map.151
  342.7 3.9 shard_map.153
  346.6 6.5 fusion.53.grad_ref
  353.1 4.7 shard_map.150
  357.8 4.7 shard_map.149
  362.6 4.5 shard_map.156
  367.1 14.6 %shard_map.164 = bf16[2048,1024]{1,0:T(8,128)(2,1)} custom-call(bf16[512,2048]{1,0:T(8,128)(2,1)} %constant_dynamic-update-slice_fusion.9.hidden_ref.refs_0_, bf16[512,512]{1,0:T(8,128)(2,1)} %get-tuple-element.95.refs_1_, bf16[512,2048]{1,0:T(8,128)(2,1)} %constant_dynamic-update-slice_fusion.6.hidden_ref.refs_2_, ...), custom_call_target="tpu_custom_call" | custom-call | flops 8589934592 | bytes 20971520 | tf_op jit(solution)/shard_map/pallas_call | solution.py:236
  382.0 4.5 shard_map.154
  391.4 10.2 %collective-permute-done.36 = bf16[128,2048]{1,0:T(8,128)(2,1)S(1)} collective-permute-done((bf16[128,2048]{1,0:T(8,128)(2,1)}, bf16[128,2048]{1,0:T(8,128)(2,1)S(1)}, u32[]{:S(2)}, u32[]{:S(2)}) %collective-permute-start.36) | collective-permute-done | bytes 524320 | tf_op jit(solution)/shard_map/ppermute | solution.py:49
  402.3 11.1 %collective-permute-done.37 = bf16[128,2048]{1,0:T(8,128)(2,1)S(1)} collective-permute-done((bf16[128,2048]{1,0:T(8,128)(2,1)}, bf16[128,2048]{1,0:T(8,128)(2,1)S(1)}, u32[]{:S(2)}, u32[]{:S(2)}) %collective-permute-start.37) | collective-permute-done | bytes 524320 | tf_op jit(solution)/shard_map/ppermute | solution.py:49
  417.1 7.0 collective-permute-done.44
  424.0 11.0 %collective-permute-done.45 = bf16[128,2048]{1,0:T(8,128)(2,1)S(1)} collective-permute-done((bf16[128,2048]{1,0:T(8,128)(2,1)}, bf16[128,2048]{1,0:T(8,128)(2,1)S(1)}, u32[]{:S(2)}, u32[]{:S(2)}) %collective-permute-start.45) | collective-permute-done | bytes 524320 | tf_op jit(solution)/shard_map/ppermute | solution.py:49
  444.4 7.6 collective-permute-done.47
  454.2 9.0 %collective-permute-done.39 = bf16[128,2048]{1,0:T(8,128)(2,1)S(1)} collective-permute-done((bf16[128,2048]{1,0:T(8,128)(2,1)S(1)}, bf16[128,2048]{1,0:T(8,128)(2,1)S(1)}, u32[]{:S(2)}, u32[]{:S(2)}) %collective-permute-start.39) | collective-permute-done | bytes 524320 | tf_op jit(solution)/shard_map/ppermute | solution.py:49
  477.8 8.2 %shard_map.157 = (bf16[1024,512]{1,0:T(8,128)(2,1)}, bf16[1024,512]{1,0:T(8,128)(2,1)}, bf16[1024,512]{1,0:T(8,128)(2,1)}) custom-call(bf16[512,2048]{1,0:T(8,128)(2,1)} %constant_dynamic-update-slice_fusion.16.refs_0_, bf16[512,2048]{1,0:T(8,128)(2,1)} %constant_dynamic-update-slice_fusion.15.refs_1_.refs_2_, ...), custom_call_target="tpu_custom_call" | custom-call | flops 2147483648 | bytes 4194304 | tf_op jit(solution)/shard_map/pallas_call | solution.py:449
  486.0 8.0 %shard_map.158 = (bf16[1024,512]{1,0:T(8,128)(2,1)}, bf16[1024,512]{1,0:T(8,128)(2,1)}, bf16[1024,512]{1,0:T(8,128)(2,1)}) custom-call(bf16[512,2048]{1,0:T(8,128)(2,1)} %collective-permute-done.51.refs_0_.refs_4_, bf16[512,2048]{1,0:T(8,128)(2,1)} %collective-permute-done.52.refs_1_.refs_6_, ...), custom_call_target="tpu_custom_call" | custom-call | flops 2147483648 | bytes 4194304 | tf_op jit(solution)/shard_map/pallas_call | solution.py:449
  494.0 14.6 %shard_map.163 = bf16[2048,1024]{1,0:T(8,128)(2,1)} custom-call(bf16[512,2048]{1,0:T(8,128)(2,1)} %constant_dynamic-update-slice_fusion.16.refs_0_, bf16[512,512]{1,0:T(8,128)(2,1)} %bitcast.188, bf16[512,2048]{1,0:T(8,128)(2,1)} %constant_dynamic-update-slice_fusion.15.refs_1_.refs_2_, bf16[512,512]{1,0:T(8,128)(2,1)} %bitcast.187, ...), custom_call_target="tpu_custom_call" | custom-call | flops 8589934592 | bytes 20971520 | tf_op jit(solution)/shard_map/pallas_call | solution.py:236
  516.5 4.3 convolution_convert_fusion.1
  521.4 20.9 %collective-permute-done.58.refs_11_ = bf16[256,512]{1,0:T(8,128)(2,1)S(1)} collective-permute-done((bf16[256,512]{1,0:T(8,128)(2,1)S(1)}, bf16[256,512]{1,0:T(8,128)(2,1)S(1)}, u32[]{:S(2)}, u32[]{:S(2)}) %collective-permute-start.58) | collective-permute-done | bytes 262176 | tf_op jit(solution)/shard_map/ppermute | solution.py:55
  543.0 14.5 %shard_map.160.rows_ref.refs_1_.refs_3_ = bf16[2048,1536]{1,0:T(8,128)(2,1)} custom-call(s32[8]{0:T(128)} %fusion.32.order, s32[8]{0:T(128)} %get-tuple-element.165.firsts, s32[8]{0:T(128)} %get-tuple-element.164.lasts, s32[1]{0:T(128)} %bitcast.24.before_group, f32[2]{0:T(128)} %broadcast_multiply_fusion.9.floats, bf16[1024,1024]{1,0:T(8,128)(2,1)} %copy-done.40, ...), custom_call_target="tpu_custom_call" | custom-call | flops 5637144576 | bytes 24576000 | tf_op jit(solution)/shard_map/pallas_call | solution.py:408
  557.5 11.2 %convolution_convert_fusion = bf16[1024,2048]{1,0:T(8,128)(2,1)} fusion(bf16[2048,1536]{1,0:T(8,128)(2,1)} %all-gather.5.cloned.1.call-done.weight_ref, bf16[2048,1536]{1,0:T(8,128)(2,1)} %shard_map.160.rows_ref.refs_1_.refs_3_), kind=kOutput, calls=%fused_computation | convolution fusion | flops 6444548096 | bytes 13631488 | tf_op jit(solution)/shard_map/dot_general | solution.py:30
  568.9 13.5 %shard_map.162 = bf16[2048,1024]{1,0:T(8,128)(2,1)} custom-call(bf16[1024,2048]{1,0:T(8,128)(2,1)} %constant_dynamic-update-slice_fusion.12.refs_0_.refs_8_.refs_10_, bf16[2048,1536]{1,0:T(8,128)(2,1)} %shard_map.160.rows_ref.refs_1_.refs_3_, bf16[1024,2048]{1,0:T(8,128)(2,1)} %collective-permute-done.6.refs_2_.refs_12_.refs_14_, ...), custom_call_target="tpu_custom_call" | custom-call | flops 8589934592 | bytes 12582912 | tf_op jit(solution)/shard_map/pallas_call | solution.py:236
  582.4 6.2 shard_map.159
  595.7 12.0 %shard_map.161 = (f32[256,2048]{1,0:T(8,128)}, bf16[256,2048]{1,0:T(8,128)(2,1)}, bf16[256,2048]{1,0:T(8,128)(2,1)}, bf16[256,2048]{1,0:T(8,128)(2,1)}) custom-call(bf16[2048,1536]{1,0:T(8,128)(2,1)} %shard_map.160.rows_ref.refs_1_.refs_3_, bf16[2048,1536]{1,0:T(8,128)(2,1)} %all-gather.5.cloned.1.call-done.weight_ref, ...), custom_call_target="tpu_custom_call" | custom-call | flops 6442450944 | bytes 14680064 | tf_op jit(solution)/shard_map/pallas_call | solution.py:190
  607.8 12.1 %collective-permute-done.77 = bf16[128,1024]{1,0:T(8,128)(2,1)S(1)} collective-permute-done((bf16[128,1024]{1,0:T(8,128)(2,1)}, bf16[128,1024]{1,0:T(8,128)(2,1)S(1)}, u32[]{:S(2)}, u32[]{:S(2)}) %collective-permute-start.77) | collective-permute-done | bytes 262176 | tf_op jit(solution)/shard_map/ppermute | solution.py:49
  621.4 26.9 %collective-permute-done.78 = bf16[128,1024]{1,0:T(8,128)(2,1)} collective-permute-done((bf16[128,1024]{1,0:T(8,128)(2,1)}, bf16[128,1024]{1,0:T(8,128)(2,1)}, u32[]{:S(2)}, u32[]{:S(2)}) %collective-permute-start.78) | collective-permute-done | bytes 262176 | tf_op jit(solution)/shard_map/ppermute | solution.py:49
  660.0 14.7 %collective-permute-done.60 = bf16[256,2048]{1,0:T(8,128)(2,1)} collective-permute-done((bf16[256,2048]{1,0:T(8,128)(2,1)}, bf16[256,2048]{1,0:T(8,128)(2,1)}, u32[]{:S(2)}, u32[]{:S(2)}) %collective-permute-start.60) | collective-permute-done | bytes 1048608 | tf_op jit(solution)/shard_map/ppermute | solution.py:49
  674.7 18.3 %collective-permute-done.61 = bf16[256,2048]{1,0:T(8,128)(2,1)} collective-permute-done((bf16[256,2048]{1,0:T(8,128)(2,1)}, bf16[256,2048]{1,0:T(8,128)(2,1)}, u32[]{:S(2)}, u32[]{:S(2)}) %collective-permute-start.61) | collective-permute-done | bytes 1048608 | tf_op jit(solution)/shard_map/ppermute | solution.py:49
  704.3 8.3 %collective-permute-start.68 = (f32[2,2048]{1,0:T(2,128)S(1)}, f32[2,2048]{1,0:T(2,128)S(1)}, u32[]{:S(2)}, u32[]{:S(2)}) collective-permute-start(f32[2,2048]{1,0:T(2,128)S(1)} %add_add_fusion), channel_id=1, source_target_pairs={{0,8},{8,0},{16,24},{24,16},{1,9},{9,1},{17,25},{25,17},{2,10},{10... | collective-permute-start | bytes 49160 | tf_op jit(solution)/shard_map/ppermute | solution.py:49
  726.7 5.1 collective-permute-done.74
  743.1 5.4 collective-permute-done.71
  748.4 4.3 collective-permute-done.72
  (375 shorter events, 200.5 us)
Async XLA Ops:
  7.2 146.2 %all-gather.5.cloned.1.call-start = ((), (), s32[]{:S(2)}) async-start(), calls=%async_computation.3 | async-start | bytes 7864320 | tf_op jit(solution)/shard_map/all_gather | solution.py:490
  13.6 14.0 %collective-permute-start = (bf16[128,1536]{1,0:T(8,128)(2,1)S(1)}, bf16[128,1536]{1,0:T(8,128)(2,1)S(1)}, u32[]{:S(2)}, u32[]{:S(2)}) collective-permute-start(bf16[128,1536]{1,0:T(8,128)(2,1)S(1)} %bitcast.202), channel_id=1, source_target_pairs={{0,6},{2,4},{4,2},{6,0},{1,7},{3,5},{5,3},{7,1},{8,14},{10,12},{12... | collective-permute-start | bytes 1179656 | tf_op jit(solution)/shard_map/ppermute | solution.py:49
  17.6 17.5 %collective-permute-start.1 = (bf16[128,1536]{1,0:T(8,128)(2,1)S(1)}, bf16[128,1536]{1,0:T(8,128)(2,1)S(1)}, u32[]{:S(2)}, u32[]{:S(2)}) collective-permute-start(bf16[128,1536]{1,0:T(8,128)(2,1)S(1)} %bitcast.203), channel_id=1, source_target_pairs={{0,4},{2,6},{4,0},{6,2},{1,5},{3,7},{5,1},{7,3},{8,12},{10,14},{12... | collective-permute-start | bytes 1179656 | tf_op jit(solution)/shard_map/ppermute | solution.py:49
  18.3 17.1 %collective-permute-start.2 = (bf16[128,1536]{1,0:T(8,128)(2,1)S(1)}, bf16[128,1536]{1,0:T(8,128)(2,1)S(1)}, u32[]{:S(2)}, u32[]{:S(2)}) collective-permute-start(bf16[128,1536]{1,0:T(8,128)(2,1)S(1)} %bitcast.204), channel_id=1, source_target_pairs={{0,2},{2,0},{4,6},{6,4},{1,3},{3,1},{5,7},{7,5},{8,10},{10,8},{12,... | collective-permute-start | bytes 1179656 | tf_op jit(solution)/shard_map/ppermute | solution.py:49
  37.3 163.9 %all-gather.7.cloned.1.call-start = ((), (), s32[]{:S(2)}) async-start(), calls=%async_computation.4 | async-start | bytes 2621440 | tf_op jit(solution)/shard_map/all_gather | solution.py:550
  44.3 18.6 %collective-permute-start.13 = (bf16[128,1536]{1,0:T(8,128)(2,1)S(1)}, bf16[128,1536]{1,0:T(8,128)(2,1)S(1)}, u32[]{:S(2)}, u32[]{:S(2)}) collective-permute-start(bf16[128,1536]{1,0:T(8,128)(2,1)S(1)} %get-tuple-element.219), channel_id=1, source_target_pairs={{0,4},{2,6},{4,0},{6,2},{1,5},{3,7},{5,1},{7,3},{8,12},{10,14},{12... | collective-permute-start | bytes 1179656 | tf_op jit(solution)/shard_map/ppermute | solution.py:49
  45.6 18.4 %collective-permute-start.14 = (bf16[128,1536]{1,0:T(8,128)(2,1)S(1)}, bf16[128,1536]{1,0:T(8,128)(2,1)S(1)}, u32[]{:S(2)}, u32[]{:S(2)}) collective-permute-start(bf16[128,1536]{1,0:T(8,128)(2,1)S(1)} %get-tuple-element.218), channel_id=1, source_target_pairs={{0,2},{2,0},{4,6},{6,4},{1,3},{3,1},{5,7},{7,5},{8,10},{10,8},{12,... | collective-permute-start | bytes 1179656 | tf_op jit(solution)/shard_map/ppermute | solution.py:49
  46.6 40.0 %collective-permute-start.3 = (bf16[256,2048]{1,0:T(8,128)(2,1)S(1)}, bf16[256,2048]{1,0:T(8,128)(2,1)}, u32[]{:S(2)}, u32[]{:S(2)}) collective-permute-start(bf16[256,2048]{1,0:T(8,128)(2,1)S(1)} %multiply_convert_fusion.2), channel_id=1, source_target_pairs={{0,2},{2,0},{4,6},{6,4},{1,3},{3,1},{5,7},{7,5},{8,10},{10,8},{12,... | collective-permute-start | bytes 3145736 | tf_op jit(solution)/shard_map/ppermute | solution.py:49
  48.1 40.8 %collective-permute-start.4 = (bf16[256,2048]{1,0:T(8,128)(2,1)S(1)}, bf16[256,2048]{1,0:T(8,128)(2,1)}, u32[]{:S(2)}, u32[]{:S(2)}) collective-permute-start(bf16[256,2048]{1,0:T(8,128)(2,1)S(1)} %multiply_convert_fusion.2), channel_id=1, source_target_pairs={{0,4},{2,6},{4,0},{6,2},{1,5},{3,7},{5,1},{7,3},{8,12},{10,14},{12... | collective-permute-start | bytes 3145736 | tf_op jit(solution)/shard_map/ppermute | solution.py:49
  55.6 52.2 %collective-permute-start.5 = (bf16[256,2048]{1,0:T(8,128)(2,1)S(1)}, bf16[256,2048]{1,0:T(8,128)(2,1)}, u32[]{:S(2)}, u32[]{:S(2)}) collective-permute-start(bf16[256,2048]{1,0:T(8,128)(2,1)S(1)} %multiply_convert_fusion.2), channel_id=1, source_target_pairs={{0,6},{2,4},{4,2},{6,0},{1,7},{3,5},{5,3},{7,1},{8,14},{10,12},{12... | collective-permute-start | bytes 3145736 | tf_op jit(solution)/shard_map/ppermute | solution.py:49
  66.1 256.3 %all-gather.11.cloned.1.call-start = ((), (), s32[]{:S(2)}) async-start(), calls=%async_computation.6 | async-start | bytes 2621440 | tf_op jit(solution)/shard_map/all_gather | solution.py:551
  110.1 52.1 %collective-permute-start.6 = (bf16[1024,2048]{1,0:T(8,128)(2,1)}, bf16[1024,2048]{1,0:T(8,128)(2,1)}, u32[]{:S(2)}, u32[]{:S(2)}) collective-permute-start(bf16[1024,2048]{1,0:T(8,128)(2,1)} %constant_dynamic-update-slice_fusion.12.refs_0_.refs_8_.refs_10_), channel_id=1, source_target_pairs={{0,1},{1,0},{2,3},{3,2},{4,5},{5,4},{6,7},{7,6},{8,9},{9,8},{10,11... | collective-permute-start | bytes 12582920 | tf_op jit(solution)/shard_map/ppermute | solution.py:49
  118.6 26.1 %collective-permute-start.26 = (bf16[256,2048]{1,0:T(8,128)(2,1)S(1)}, bf16[256,2048]{1,0:T(8,128)(2,1)S(1)}, u32[]{:S(2)}, u32[]{:S(2)}) collective-permute-start(bf16[256,2048]{1,0:T(8,128)(2,1)S(1)} %constant_dynamic-slice_fusion.9), channel_id=1, source_target_pairs={{0,2},{2,0},{4,6},{6,4},{1,3},{3,1},{5,7},{7,5},{8,10},{10,8},{12,... | collective-permute-start | bytes 3145736 | tf_op jit(solution)/shard_map/ppermute | solution.py:49
  136.0 192.8 %all-gather.9.cloned.1.call-start = ((), (), s32[]{:S(2)}) async-start(), calls=%async_computation.5 | async-start | bytes 2621440 | tf_op jit(solution)/shard_map/all_gather | solution.py:552
  136.3 68.8 %collective-permute-start.27 = (bf16[256,2048]{1,0:T(8,128)(2,1)S(1)}, bf16[256,2048]{1,0:T(8,128)(2,1)}, u32[]{:S(2)}, u32[]{:S(2)}) collective-permute-start(bf16[256,2048]{1,0:T(8,128)(2,1)S(1)} %constant_dynamic-slice_fusion.9), channel_id=1, source_target_pairs={{0,4},{2,6},{4,0},{6,2},{1,5},{3,7},{5,1},{7,3},{8,12},{10,14},{12... | collective-permute-start | bytes 3145736 | tf_op jit(solution)/shard_map/ppermute | solution.py:49
  136.7 74.7 %collective-permute-start.28 = (bf16[256,2048]{1,0:T(8,128)(2,1)S(1)}, bf16[256,2048]{1,0:T(8,128)(2,1)}, u32[]{:S(2)}, u32[]{:S(2)}) collective-permute-start(bf16[256,2048]{1,0:T(8,128)(2,1)S(1)} %constant_dynamic-slice_fusion.9), channel_id=1, source_target_pairs={{0,6},{2,4},{4,2},{6,0},{1,7},{3,5},{5,3},{7,1},{8,14},{10,12},{12... | collective-permute-start | bytes 3145736 | tf_op jit(solution)/shard_map/ppermute | solution.py:49
  211.0 16.9 %collective-permute-start.19 = (bf16[512,2048]{1,0:T(8,128)(2,1)}, bf16[512,2048]{1,0:T(8,128)(2,1)}, u32[]{:S(2)}, u32[]{:S(2)}) collective-permute-start(bf16[512,2048]{1,0:T(8,128)(2,1)} %shard_map.147), channel_id=1, source_target_pairs={{0,1},{1,0},{2,3},{3,2},{4,5},{5,4},{6,7},{7,6},{8,9},{9,8},{10,11... | collective-permute-start | bytes 6291464 | tf_op jit(solution)/shard_map/ppermute | solution.py:49
  222.5 15.0 %collective-permute-start.16 = (bf16[128,2048]{1,0:T(8,128)(2,1)}, bf16[128,2048]{1,0:T(8,128)(2,1)S(1)}, u32[]{:S(2)}, u32[]{:S(2)}) collective-permute-start(bf16[128,2048]{1,0:T(8,128)(2,1)} %get-tuple-element.80), channel_id=1, source_target_pairs={{0,2},{2,0},{4,6},{6,4},{1,3},{3,1},{5,7},{7,5},{8,10},{10,8},{12,... | collective-permute-start | bytes 1572872 | tf_op jit(solution)/shard_map/ppermute | solution.py:49
  223.8 25.1 %collective-permute-start.17 = (bf16[128,2048]{1,0:T(8,128)(2,1)}, bf16[128,2048]{1,0:T(8,128)(2,1)S(1)}, u32[]{:S(2)}, u32[]{:S(2)}) collective-permute-start(bf16[128,2048]{1,0:T(8,128)(2,1)} %get-tuple-element.81), channel_id=1, source_target_pairs={{0,4},{2,6},{4,0},{6,2},{1,5},{3,7},{5,1},{7,3},{8,12},{10,14},{12... | collective-permute-start | bytes 1572872 | tf_op jit(solution)/shard_map/ppermute | solution.py:49
  225.3 24.8 %collective-permute-start.18 = (bf16[128,2048]{1,0:T(8,128)(2,1)}, bf16[128,2048]{1,0:T(8,128)(2,1)}, u32[]{:S(2)}, u32[]{:S(2)}) collective-permute-start(bf16[128,2048]{1,0:T(8,128)(2,1)} %get-tuple-element.82), channel_id=1, source_target_pairs={{0,6},{2,4},{4,2},{6,0},{1,7},{3,5},{5,3},{7,1},{8,14},{10,12},{12... | collective-permute-start | bytes 1572872 | tf_op jit(solution)/shard_map/ppermute | solution.py:49
  227.9 94.5 %collective-permute-start.33 = (bf16[1024,2048]{1,0:T(8,128)(2,1)}, bf16[1024,2048]{1,0:T(8,128)(2,1)}, u32[]{:S(2)}, u32[]{:S(2)}) collective-permute-start(bf16[1024,2048]{1,0:T(8,128)(2,1)} %slice_dynamic-update-slice_fusion.refs_8_.refs_10_), channel_id=1, source_target_pairs={{0,1},{1,0},{2,3},{3,2},{4,5},{5,4},{6,7},{7,6},{8,9},{9,8},{10,11... | collective-permute-start | bytes 12582920 | tf_op jit(solution)/shard_map/ppermute | solution.py:49
  232.3 27.7 %collective-permute-start.20 = (bf16[128,2048]{1,0:T(8,128)(2,1)}, bf16[128,2048]{1,0:T(8,128)(2,1)S(1)}, u32[]{:S(2)}, u32[]{:S(2)}) collective-permute-start(bf16[128,2048]{1,0:T(8,128)(2,1)} %get-tuple-element.84), channel_id=1, source_target_pairs={{0,2},{2,0},{4,6},{6,4},{1,3},{3,1},{5,7},{7,5},{8,10},{10,8},{12,... | collective-permute-start | bytes 1572872 | tf_op jit(solution)/shard_map/ppermute | solution.py:49
  237.5 33.8 %collective-permute-start.21 = (bf16[128,2048]{1,0:T(8,128)(2,1)}, bf16[128,2048]{1,0:T(8,128)(2,1)S(1)}, u32[]{:S(2)}, u32[]{:S(2)}) collective-permute-start(bf16[128,2048]{1,0:T(8,128)(2,1)} %get-tuple-element.85), channel_id=1, source_target_pairs={{0,4},{2,6},{4,0},{6,2},{1,5},{3,7},{5,1},{7,3},{8,12},{10,14},{12... | collective-permute-start | bytes 1572872 | tf_op jit(solution)/shard_map/ppermute | solution.py:49
  248.9 22.5 %collective-permute-start.22 = (bf16[128,2048]{1,0:T(8,128)(2,1)}, bf16[128,2048]{1,0:T(8,128)(2,1)S(1)}, u32[]{:S(2)}, u32[]{:S(2)}) collective-permute-start(bf16[128,2048]{1,0:T(8,128)(2,1)} %get-tuple-element.86), channel_id=1, source_target_pairs={{0,6},{2,4},{4,2},{6,0},{1,7},{3,5},{5,3},{7,1},{8,14},{10,12},{12... | collective-permute-start | bytes 1572872 | tf_op jit(solution)/shard_map/ppermute | solution.py:49
  272.3 15.0 %collective-permute-start.29 = (bf16[128,2048]{1,0:T(8,128)(2,1)S(1)}, bf16[128,2048]{1,0:T(8,128)(2,1)}, u32[]{:S(2)}, u32[]{:S(2)}) collective-permute-start(bf16[128,2048]{1,0:T(8,128)(2,1)S(1)} %multiply_convert_fusion.5), channel_id=1, source_target_pairs={{0,2},{2,0},{4,6},{6,4},{1,3},{3,1},{5,7},{7,5},{8,10},{10,8},{12,... | collective-permute-start | bytes 1572872 | tf_op jit(solution)/shard_map/ppermute | solution.py:49
  273.6 316.6 %reduce-scatter.8.cloned.1.call-start = ((), (), s32[]{:S(2)}) async-start(), calls=%async_computation.9 | async-start | bytes 5242880 | tf_op jit(solution)/shard_map/reduce_scatter | solution.py:248
  274.1 26.1 %collective-permute-start.30 = (bf16[128,2048]{1,0:T(8,128)(2,1)S(1)}, bf16[128,2048]{1,0:T(8,128)(2,1)S(1)}, u32[]{:S(2)}, u32[]{:S(2)}) collective-permute-start(bf16[128,2048]{1,0:T(8,128)(2,1)S(1)} %multiply_convert_fusion.5), channel_id=1, source_target_pairs={{0,4},{2,6},{4,0},{6,2},{1,5},{3,7},{5,1},{7,3},{8,12},{10,14},{12... | collective-permute-start | bytes 1572872 | tf_op jit(solution)/shard_map/ppermute | solution.py:49
  275.0 26.1 %collective-permute-start.31 = (bf16[128,2048]{1,0:T(8,128)(2,1)S(1)}, bf16[128,2048]{1,0:T(8,128)(2,1)S(1)}, u32[]{:S(2)}, u32[]{:S(2)}) collective-permute-start(bf16[128,2048]{1,0:T(8,128)(2,1)S(1)} %multiply_convert_fusion.5), channel_id=1, source_target_pairs={{0,6},{2,4},{4,2},{6,0},{1,7},{3,5},{5,3},{7,1},{8,14},{10,12},{12... | collective-permute-start | bytes 1572872 | tf_op jit(solution)/shard_map/ppermute | solution.py:49
  278.0 31.7 %collective-permute-start.23 = (bf16[128,2048]{1,0:T(8,128)(2,1)S(1)}, bf16[128,2048]{1,0:T(8,128)(2,1)S(1)}, u32[]{:S(2)}, u32[]{:S(2)}) collective-permute-start(bf16[128,2048]{1,0:T(8,128)(2,1)S(1)} %multiply_convert_fusion.6), channel_id=1, source_target_pairs={{0,2},{2,0},{4,6},{6,4},{1,3},{3,1},{5,7},{7,5},{8,10},{10,8},{12,... | collective-permute-start | bytes 1572872 | tf_op jit(solution)/shard_map/ppermute | solution.py:49
  287.3 33.4 %collective-permute-start.24 = (bf16[128,2048]{1,0:T(8,128)(2,1)S(1)}, bf16[128,2048]{1,0:T(8,128)(2,1)S(1)}, u32[]{:S(2)}, u32[]{:S(2)}) collective-permute-start(bf16[128,2048]{1,0:T(8,128)(2,1)S(1)} %multiply_convert_fusion.6), channel_id=1, source_target_pairs={{0,4},{2,6},{4,0},{6,2},{1,5},{3,7},{5,1},{7,3},{8,12},{10,14},{12... | collective-permute-start | bytes 1572872 | tf_op jit(solution)/shard_map/ppermute | solution.py:49
  301.9 26.9 %collective-permute-start.34 = (bf16[512,2048]{1,0:T(8,128)(2,1)}, bf16[512,2048]{1,0:T(8,128)(2,1)}, u32[]{:S(2)}, u32[]{:S(2)}) collective-permute-start(bf16[512,2048]{1,0:T(8,128)(2,1)} %constant_dynamic-update-slice_fusion.6.hidden_ref.refs_2_), channel_id=1, source_target_pairs={{0,1},{1,0},{2,3},{3,2},{4,5},{5,4},{6,7},{7,6},{8,9},{9,8},{10,11... | collective-permute-start | bytes 6291464 | tf_op jit(solution)/shard_map/ppermute | solution.py:49
  301.9 19.6 %collective-permute-start.25 = (bf16[128,2048]{1,0:T(8,128)(2,1)S(1)}, bf16[128,2048]{1,0:T(8,128)(2,1)S(1)}, u32[]{:S(2)}, u32[]{:S(2)}) collective-permute-start(bf16[128,2048]{1,0:T(8,128)(2,1)S(1)} %multiply_convert_fusion.6), channel_id=1, source_target_pairs={{0,6},{2,4},{4,2},{6,0},{1,7},{3,5},{5,3},{7,1},{8,14},{10,12},{12... | collective-permute-start | bytes 1572872 | tf_op jit(solution)/shard_map/ppermute | solution.py:49
  322.3 15.7 %collective-permute-start.32 = (bf16[512,2048]{1,0:T(8,128)(2,1)}, bf16[512,2048]{1,0:T(8,128)(2,1)}, u32[]{:S(2)}, u32[]{:S(2)}) collective-permute-start(bf16[512,2048]{1,0:T(8,128)(2,1)} %constant_dynamic-update-slice_fusion.9.hidden_ref.refs_0_), channel_id=1, source_target_pairs={{0,1},{1,0},{2,3},{3,2},{4,5},{5,4},{6,7},{7,6},{8,9},{9,8},{10,11... | collective-permute-start | bytes 6291464 | tf_op jit(solution)/shard_map/ppermute | solution.py:49
  337.5 25.1 %collective-permute-start.43 = (bf16[512,2048]{1,0:T(8,128)(2,1)}, bf16[512,2048]{1,0:T(8,128)(2,1)}, u32[]{:S(2)}, u32[]{:S(2)}) collective-permute-start(bf16[512,2048]{1,0:T(8,128)(2,1)} %shard_map.155), channel_id=1, source_target_pairs={{0,1},{1,0},{2,3},{3,2},{4,5},{5,4},{6,7},{7,6},{8,9},{9,8},{10,11... | collective-permute-start | bytes 6291464 | tf_op jit(solution)/shard_map/ppermute | solution.py:49
  346.6 35.4 %collective-permute-start.35 = (bf16[512,2048]{1,0:T(8,128)(2,1)}, bf16[512,2048]{1,0:T(8,128)(2,1)}, u32[]{:S(2)}, u32[]{:S(2)}) collective-permute-start(bf16[512,2048]{1,0:T(8,128)(2,1)} %shard_map.153), channel_id=1, source_target_pairs={{0,1},{1,0},{2,3},{3,2},{4,5},{5,4},{6,7},{7,6},{8,9},{9,8},{10,11... | collective-permute-start | bytes 6291464 | tf_op jit(solution)/shard_map/ppermute | solution.py:49
  381.7 338.8 %reduce-scatter.6.cloned.1.call-start = ((), (), s32[]{:S(2)}) async-start(), calls=%async_computation.8 | async-start | bytes 5242880 | tf_op jit(solution)/shard_map/reduce_scatter | solution.py:248
  386.5 15.0 %collective-permute-start.36 = (bf16[128,2048]{1,0:T(8,128)(2,1)}, bf16[128,2048]{1,0:T(8,128)(2,1)S(1)}, u32[]{:S(2)}, u32[]{:S(2)}) collective-permute-start(bf16[128,2048]{1,0:T(8,128)(2,1)} %get-tuple-element.98), channel_id=1, source_target_pairs={{0,2},{2,0},{4,6},{6,4},{1,3},{3,1},{5,7},{7,5},{8,10},{10,8},{12,... | collective-permute-start | bytes 1572872 | tf_op jit(solution)/shard_map/ppermute | solution.py:49
  387.2 26.2 %collective-permute-start.37 = (bf16[128,2048]{1,0:T(8,128)(2,1)}, bf16[128,2048]{1,0:T(8,128)(2,1)S(1)}, u32[]{:S(2)}, u32[]{:S(2)}) collective-permute-start(bf16[128,2048]{1,0:T(8,128)(2,1)} %get-tuple-element.99), channel_id=1, source_target_pairs={{0,4},{2,6},{4,0},{6,2},{1,5},{3,7},{5,1},{7,3},{8,12},{10,14},{12... | collective-permute-start | bytes 1572872 | tf_op jit(solution)/shard_map/ppermute | solution.py:49
  387.9 25.5 %collective-permute-start.38 = (bf16[128,2048]{1,0:T(8,128)(2,1)}, bf16[128,2048]{1,0:T(8,128)(2,1)}, u32[]{:S(2)}, u32[]{:S(2)}) collective-permute-start(bf16[128,2048]{1,0:T(8,128)(2,1)} %get-tuple-element.100), channel_id=1, source_target_pairs={{0,6},{2,4},{4,2},{6,0},{1,7},{3,5},{5,3},{7,1},{8,14},{10,12},{12... | collective-permute-start | bytes 1572872 | tf_op jit(solution)/shard_map/ppermute | solution.py:49
  390.0 34.0 %collective-permute-start.44 = (bf16[128,2048]{1,0:T(8,128)(2,1)}, bf16[128,2048]{1,0:T(8,128)(2,1)S(1)}, u32[]{:S(2)}, u32[]{:S(2)}) collective-permute-start(bf16[128,2048]{1,0:T(8,128)(2,1)} %get-tuple-element.107), channel_id=1, source_target_pairs={{0,2},{2,0},{4,6},{6,4},{1,3},{3,1},{5,7},{7,5},{8,10},{10,8},{12,... | collective-permute-start | bytes 1572872 | tf_op jit(solution)/shard_map/ppermute | solution.py:49
  390.6 44.5 %collective-permute-start.45 = (bf16[128,2048]{1,0:T(8,128)(2,1)}, bf16[128,2048]{1,0:T(8,128)(2,1)S(1)}, u32[]{:S(2)}, u32[]{:S(2)}) collective-permute-start(bf16[128,2048]{1,0:T(8,128)(2,1)} %get-tuple-element.108), channel_id=1, source_target_pairs={{0,4},{2,6},{4,0},{6,2},{1,5},{3,7},{5,1},{7,3},{8,12},{10,14},{12... | collective-permute-start | bytes 1572872 | tf_op jit(solution)/shard_map/ppermute | solution.py:49
  401.5 33.6 %collective-permute-start.46 = (bf16[128,2048]{1,0:T(8,128)(2,1)}, bf16[128,2048]{1,0:T(8,128)(2,1)S(1)}, u32[]{:S(2)}, u32[]{:S(2)}) collective-permute-start(bf16[128,2048]{1,0:T(8,128)(2,1)} %get-tuple-element.109), channel_id=1, source_target_pairs={{0,6},{2,4},{4,2},{6,0},{1,7},{3,5},{5,3},{7,1},{8,14},{10,12},{12... | collective-permute-start | bytes 1572872 | tf_op jit(solution)/shard_map/ppermute | solution.py:49
  437.3 14.8 %collective-permute-start.47 = (bf16[128,2048]{1,0:T(8,128)(2,1)S(1)}, bf16[128,2048]{1,0:T(8,128)(2,1)S(1)}, u32[]{:S(2)}, u32[]{:S(2)}) collective-permute-start(bf16[128,2048]{1,0:T(8,128)(2,1)S(1)} %get-tuple-element.167), channel_id=1, source_target_pairs={{0,2},{2,0},{4,6},{6,4},{1,3},{3,1},{5,7},{7,5},{8,10},{10,8},{12,... | collective-permute-start | bytes 1572872 | tf_op jit(solution)/shard_map/ppermute | solution.py:49
  438.7 14.8 %collective-permute-start.48 = (bf16[128,2048]{1,0:T(8,128)(2,1)S(1)}, bf16[128,2048]{1,0:T(8,128)(2,1)S(1)}, u32[]{:S(2)}, u32[]{:S(2)}) collective-permute-start(bf16[128,2048]{1,0:T(8,128)(2,1)S(1)} %get-tuple-element.167), channel_id=1, source_target_pairs={{0,4},{2,6},{4,0},{6,2},{1,5},{3,7},{5,1},{7,3},{8,12},{10,14},{12... | collective-permute-start | bytes 1572872 | tf_op jit(solution)/shard_map/ppermute | solution.py:49
  439.3 24.0 %collective-permute-start.39 = (bf16[128,2048]{1,0:T(8,128)(2,1)S(1)}, bf16[128,2048]{1,0:T(8,128)(2,1)S(1)}, u32[]{:S(2)}, u32[]{:S(2)}) collective-permute-start(bf16[128,2048]{1,0:T(8,128)(2,1)S(1)} %get-tuple-element.170), channel_id=1, source_target_pairs={{0,2},{2,0},{4,6},{6,4},{1,3},{3,1},{5,7},{7,5},{8,10},{10,8},{12,... | collective-permute-start | bytes 1572872 | tf_op jit(solution)/shard_map/ppermute | solution.py:49
  440.4 24.2 %collective-permute-start.40 = (bf16[128,2048]{1,0:T(8,128)(2,1)S(1)}, bf16[128,2048]{1,0:T(8,128)(2,1)S(1)}, u32[]{:S(2)}, u32[]{:S(2)}) collective-permute-start(bf16[128,2048]{1,0:T(8,128)(2,1)S(1)} %get-tuple-element.170), channel_id=1, source_target_pairs={{0,4},{2,6},{4,0},{6,2},{1,5},{3,7},{5,1},{7,3},{8,12},{10,14},{12... | collective-permute-start | bytes 1572872 | tf_op jit(solution)/shard_map/ppermute | solution.py:49
  452.1 18.2 %collective-permute-start.49 = (bf16[128,1024]{1,0:T(8,128)(2,1)S(1)}, bf16[128,1024]{1,0:T(8,128)(2,1)S(1)}, u32[]{:S(2)}, u32[]{:S(2)}) collective-permute-start(bf16[128,1024]{1,0:T(8,128)(2,1)S(1)} %slice.259), channel_id=1, source_target_pairs={{0,4},{2,6},{4,0},{6,2},{1,5},{3,7},{5,1},{7,3},{8,12},{10,14},{12... | collective-permute-start | bytes 786440 | tf_op jit(solution)/shard_map/ppermute | solution.py:49
  453.5 17.6 %collective-permute-start.50 = (bf16[128,1024]{1,0:T(8,128)(2,1)S(1)}, bf16[128,1024]{1,0:T(8,128)(2,1)S(1)}, u32[]{:S(2)}, u32[]{:S(2)}) collective-permute-start(bf16[128,1024]{1,0:T(8,128)(2,1)S(1)} %slice.260), channel_id=1, source_target_pairs={{0,2},{2,0},{4,6},{6,4},{1,3},{3,1},{5,7},{7,5},{8,10},{10,8},{12,... | collective-permute-start | bytes 786440 | tf_op jit(solution)/shard_map/ppermute | solution.py:49
  471.8 14.2 %collective-permute-start.52 = (bf16[512,2048]{1,0:T(8,128)(2,1)}, bf16[512,2048]{1,0:T(8,128)(2,1)}, u32[]{:S(2)}, u32[]{:S(2)}) collective-permute-start(bf16[512,2048]{1,0:T(8,128)(2,1)} %constant_dynamic-update-slice_fusion.15.refs_1_.refs_2_), channel_id=1, source_target_pairs={{0,1},{1,0},{2,3},{3,2},{4,5},{5,4},{6,7},{7,6},{8,9},{9,8},{10,11... | collective-permute-start | bytes 6291464 | tf_op jit(solution)/shard_map/ppermute | solution.py:49
  508.7 227.5 %reduce-scatter.4.cloned.1.call-start = ((), (), s32[]{:S(2)}) async-start(), calls=%async_computation.7 | async-start | bytes 5242880 | tf_op jit(solution)/shard_map/reduce_scatter | solution.py:248
  515.0 27.2 %collective-permute-start.58 = (bf16[256,512]{1,0:T(8,128)(2,1)S(1)}, bf16[256,512]{1,0:T(8,128)(2,1)S(1)}, u32[]{:S(2)}, u32[]{:S(2)}) collective-permute-start(bf16[256,512]{1,0:T(8,128)(2,1)S(1)} %convolution_add_fusion), channel_id=1, source_target_pairs={{8,0},{16,8},{24,16},{9,1},{17,9},{25,17},{10,2},{18,10},{26,18},{... | collective-permute-start | bytes 786440 | tf_op jit(solution)/shard_map/ppermute | solution.py:55
  520.9 61.5 %collective-permute-start.53 = (bf16[1024,2048]{1,0:T(8,128)(2,1)}, bf16[1024,2048]{1,0:T(8,128)(2,1)}, u32[]{:S(2)}, u32[]{:S(2)}) collective-permute-start(bf16[1024,2048]{1,0:T(8,128)(2,1)} %convolution_convert_fusion.1), channel_id=1, source_target_pairs={{0,1},{1,0},{2,3},{3,2},{4,5},{5,4},{6,7},{7,6},{8,9},{9,8},{10,11... | collective-permute-start | bytes 12582920 | tf_op jit(solution)/shard_map/ppermute | solution.py:49
  568.7 25.4 %collective-permute-start.59 = (bf16[1024,2048]{1,0:T(8,128)(2,1)}, bf16[1024,2048]{1,0:T(8,128)(2,1)}, u32[]{:S(2)}, u32[]{:S(2)}) collective-permute-start(bf16[1024,2048]{1,0:T(8,128)(2,1)} %convolution_convert_fusion), channel_id=1, source_target_pairs={{0,1},{1,0},{2,3},{3,2},{4,5},{5,4},{6,7},{7,6},{8,9},{9,8},{10,11... | collective-permute-start | bytes 12582920 | tf_op jit(solution)/shard_map/ppermute | solution.py:49
  588.6 63.6 %collective-permute-start.54 = (bf16[256,2048]{1,0:T(8,128)(2,1)}, bf16[256,2048]{1,0:T(8,128)(2,1)S(1)}, u32[]{:S(2)}, u32[]{:S(2)}) collective-permute-start(bf16[256,2048]{1,0:T(8,128)(2,1)} %get-tuple-element.119), channel_id=1, source_target_pairs={{0,2},{2,0},{4,6},{6,4},{1,3},{3,1},{5,7},{7,5},{8,10},{10,8},{12,... | collective-permute-start | bytes 3145736 | tf_op jit(solution)/shard_map/ppermute | solution.py:49
  588.6 66.8 %collective-permute-start.55 = (bf16[256,2048]{1,0:T(8,128)(2,1)}, bf16[256,2048]{1,0:T(8,128)(2,1)}, u32[]{:S(2)}, u32[]{:S(2)}) collective-permute-start(bf16[256,2048]{1,0:T(8,128)(2,1)} %get-tuple-element.120), channel_id=1, source_target_pairs={{0,4},{2,6},{4,0},{6,2},{1,5},{3,7},{5,1},{7,3},{8,12},{10,14},{12... | collective-permute-start | bytes 3145736 | tf_op jit(solution)/shard_map/ppermute | solution.py:49
  592.2 27.6 %collective-permute-start.77 = (bf16[128,1024]{1,0:T(8,128)(2,1)}, bf16[128,1024]{1,0:T(8,128)(2,1)S(1)}, u32[]{:S(2)}, u32[]{:S(2)}) collective-permute-start(bf16[128,1024]{1,0:T(8,128)(2,1)} %get-tuple-element.227), channel_id=1, source_target_pairs={{0,6},{2,4},{4,2},{6,0},{1,7},{3,5},{5,3},{7,1},{8,14},{10,12},{12... | collective-permute-start | bytes 786440 | tf_op jit(solution)/shard_map/ppermute | solution.py:49
  594.1 54.2 %collective-permute-start.78 = (bf16[128,1024]{1,0:T(8,128)(2,1)}, bf16[128,1024]{1,0:T(8,128)(2,1)}, u32[]{:S(2)}, u32[]{:S(2)}) collective-permute-start(bf16[128,1024]{1,0:T(8,128)(2,1)} %get-tuple-element.226), channel_id=1, source_target_pairs={{0,4},{2,6},{4,0},{6,2},{1,5},{3,7},{5,1},{7,3},{8,12},{10,14},{12... | collective-permute-start | bytes 786440 | tf_op jit(solution)/shard_map/ppermute | solution.py:49
  594.1 55.8 %collective-permute-start.79 = (bf16[128,1024]{1,0:T(8,128)(2,1)}, bf16[128,1024]{1,0:T(8,128)(2,1)}, u32[]{:S(2)}, u32[]{:S(2)}) collective-permute-start(bf16[128,1024]{1,0:T(8,128)(2,1)} %get-tuple-element.225), channel_id=1, source_target_pairs={{0,2},{2,0},{4,6},{6,4},{1,3},{3,1},{5,7},{7,5},{8,10},{10,8},{12,... | collective-permute-start | bytes 786440 | tf_op jit(solution)/shard_map/ppermute | solution.py:49
  619.8 35.6 %collective-permute-start.56 = (bf16[256,2048]{1,0:T(8,128)(2,1)}, bf16[256,2048]{1,0:T(8,128)(2,1)}, u32[]{:S(2)}, u32[]{:S(2)}) collective-permute-start(bf16[256,2048]{1,0:T(8,128)(2,1)} %get-tuple-element.121), channel_id=1, source_target_pairs={{0,6},{2,4},{4,2},{6,0},{1,7},{3,5},{5,3},{7,1},{8,14},{10,12},{12... | collective-permute-start | bytes 3145736 | tf_op jit(solution)/shard_map/ppermute | solution.py:49
  648.3 26.3 %collective-permute-start.60 = (bf16[256,2048]{1,0:T(8,128)(2,1)}, bf16[256,2048]{1,0:T(8,128)(2,1)}, u32[]{:S(2)}, u32[]{:S(2)}) collective-permute-start(bf16[256,2048]{1,0:T(8,128)(2,1)} %get-tuple-element.128), channel_id=1, source_target_pairs={{0,2},{2,0},{4,6},{6,4},{1,3},{3,1},{5,7},{7,5},{8,10},{10,8},{12,... | collective-permute-start | bytes 3145736 | tf_op jit(solution)/shard_map/ppermute | solution.py:49
  650.0 43.0 %collective-permute-start.61 = (bf16[256,2048]{1,0:T(8,128)(2,1)}, bf16[256,2048]{1,0:T(8,128)(2,1)}, u32[]{:S(2)}, u32[]{:S(2)}) collective-permute-start(bf16[256,2048]{1,0:T(8,128)(2,1)} %get-tuple-element.129), channel_id=1, source_target_pairs={{0,4},{2,6},{4,0},{6,2},{1,5},{3,7},{5,1},{7,3},{8,12},{10,14},{12... | collective-permute-start | bytes 3145736 | tf_op jit(solution)/shard_map/ppermute | solution.py:49
  652.2 40.8 %collective-permute-start.62 = (bf16[256,2048]{1,0:T(8,128)(2,1)}, bf16[256,2048]{1,0:T(8,128)(2,1)}, u32[]{:S(2)}, u32[]{:S(2)}) collective-permute-start(bf16[256,2048]{1,0:T(8,128)(2,1)} %get-tuple-element.130), channel_id=1, source_target_pairs={{0,6},{2,4},{4,2},{6,0},{1,7},{3,5},{5,3},{7,1},{8,14},{10,12},{12... | collective-permute-start | bytes 3145736 | tf_op jit(solution)/shard_map/ppermute | solution.py:49
  658.9 59.9 %collective-permute-start.57 = (bf16[256,2048]{1,0:T(8,128)(2,1)S(1)}, bf16[256,2048]{1,0:T(8,128)(2,1)S(1)}, u32[]{:S(2)}, u32[]{:S(2)}) collective-permute-start(bf16[256,2048]{1,0:T(8,128)(2,1)S(1)} %fusion.5), channel_id=1, source_target_pairs={{0,1},{1,0},{2,3},{3,2},{4,5},{5,4},{6,7},{7,6},{8,9},{9,8},{10,11... | collective-permute-start | bytes 3145736 | tf_op jit(solution)/shard_map/ppermute | solution.py:49
  739.3 13.4 %collective-permute-start.72 = (bf16[128,1024]{1,0:T(8,128)(2,1)S(1)}, bf16[128,1024]{1,0:T(8,128)(2,1)S(1)}, u32[]{:S(2)}, u32[]{:S(2)}) collective-permute-start(bf16[128,1024]{1,0:T(8,128)(2,1)S(1)} %get-tuple-element.229), channel_id=1, source_target_pairs={{0,4},{2,6},{4,0},{6,2},{1,5},{3,7},{5,1},{7,3},{8,12},{10,14},{12... | collective-permute-start | bytes 786440 | tf_op jit(solution)/shard_map/ppermute | solution.py:49
  (65 other events, 700.0 us)
Sparse Core Ops, SparseCore 0:
  37.5 115.8 all-gather.4
  155.0 46.2 all-gather.6
  202.8 47.5 all-gather.10
  273.7 52.3 all-gather.8
  381.9 83.4 reduce-scatter.7
  508.8 89.1 reduce-scatter.5
  600.3 77.2 reduce-scatter.3
